TPU v7x, 32 devices: a whole 2x2x4 slice. The times are simulated.
32 devices in a mesh: ctx: 4 (over x, core), fsdp: 8 (over z, y).
Axes of the slice: x: 2, y: 2, z: 4, core: 2. Of those that a mesh axis runs over, the one named last changes fastest.
Arguments:
- hidden_in: bfloat16 [4096, 8, 768], P(('ctx', 'fsdp')), may hold values from -6 to 6
- lengths: int32 [8], replicated, may hold values from 1 to 4096, 24576 in all
- seq_order: int32 [8], replicated, may hold values from 0 to 7, each once
- query_weight: bfloat16 [768, 768], P('fsdp'), may hold values from -0.21875 to 0.21875
- query_bias: bfloat16 [768], P('fsdp'), may hold values from -3 to 3
- key_weight: bfloat16 [768, 768], P('fsdp'), may hold values from -0.3125 to 0.3125
- value_weight: bfloat16 [768, 768], P('fsdp'), may hold values from -0.21875 to 0.21875
- value_bias: bfloat16 [768], P('fsdp'), may hold values from -0.29882812 to 0.29882812
- output_weight: bfloat16 [768, 768], P('fsdp'), may hold values from -4 to 4
- output_bias: bfloat16 [768], P('fsdp'), may hold values from -3 to 3
- norm1_gain: bfloat16 [768], P('fsdp'), may hold values from 0.5 to 1.5
- norm1_shift: bfloat16 [768], P('fsdp'), may hold values from -3 to 3
- inner_weight: bfloat16 [768, 3072], P('fsdp'), may hold values from -0.21875 to 0.21875
- inner_bias: bfloat16 [3072], P('fsdp'), may hold values from -3 to 3
- outer_weight: bfloat16 [3072, 768], P('fsdp'), may hold values from -0.109375 to 0.109375
- outer_bias: bfloat16 [768], P('fsdp'), may hold values from -3 to 3
- norm2_gain: bfloat16 [768], P('fsdp'), may hold values from 0.5 to 1.5
- norm2_shift: bfloat16 [768], P('fsdp'), may hold values from -3 to 3
- cotangent: bfloat16 [4096, 8, 768], P('ctx', 'fsdp'), may hold values from -6 to 6
Outputs:
- layer_out: bfloat16 [4096, 8, 768], P('ctx', 'fsdp')
- grad_in: bfloat16 [4096, 8, 768], P(('ctx', 'fsdp'))
- grad_query_weight: float32 [768, 768], P('fsdp')
- grad_query_bias: float32 [768], P('fsdp')
- grad_key_weight: float32 [768, 768], P('fsdp')
- grad_value_weight: float32 [768, 768], P('fsdp')
- grad_value_bias: float32 [768], P('fsdp')
- grad_output_weight: float32 [768, 768], P('fsdp')
- grad_output_bias: float32 [768], P('fsdp')
- grad_norm1_gain: float32 [768], P('fsdp')
- grad_norm1_shift: float32 [768], P('fsdp')
- grad_inner_weight: float32 [768, 3072], P('fsdp')
- grad_inner_bias: float32 [3072], P('fsdp')
- grad_outer_weight: float32 [3072, 768], P('fsdp')
- grad_outer_bias: float32 [768], P('fsdp')
- grad_norm2_gain: float32 [768], P('fsdp')
- grad_norm2_shift: float32 [768], P('fsdp')
Inputs may be any that keep to these rules, and one draw needn't show every extreme that they name: The 8 lengths sum to 24576 and the largest is exactly 4096. `seq_order`: a permutation; index f of fsdp holds slot f.
All inputs are finite; a program needn't handle non-finite values.
Results may differ from a plain program's by a relative error of at most 0.02.
Values may be sent and summed in bfloat16 or wider, within the bound.
A program may use at most 192 MiB of HBM per device.

v0:
```python
import jax
import jax.numpy as jnp
from jax import lax
from jax.sharding import PartitionSpec as P

H = 12
HD = 64
QB = 512
KB = 512


NORM_EPSILON = 1e-12
NEG_BIG = -1e30
ROOT_HALF = 0.7071067811865476
ROOT_TWO_PI = 2.5066282746310002


def norm_forward(source, gain_vec, shift_vec):
    centre = source - jnp.mean(source, axis=-1, keepdims=True)
    inv_scale = lax.rsqrt(jnp.mean(centre * centre, axis=-1, keepdims=True) + NORM_EPSILON)
    unit_rows = centre * inv_scale
    return (unit_rows * gain_vec + shift_vec, unit_rows, inv_scale)


def norm_backward(upstream, unit_rows, inv_scale, gain_vec):
    scaled = upstream * gain_vec
    plain_mean = jnp.mean(scaled, axis=-1, keepdims=True)
    cross_mean = jnp.mean(scaled * unit_rows, axis=-1, keepdims=True)
    d_source = inv_scale * (scaled - plain_mean - unit_rows * cross_mean)
    return (d_source, jnp.sum(upstream * unit_rows, axis=0), jnp.sum(upstream, axis=0))


def gelu_exact(source):
    return 0.5 * source * (1.0 + jax.scipy.special.erf(source * ROOT_HALF))


def gelu_slope(source):
    return (
        0.5 * (1.0 + jax.scipy.special.erf(source * ROOT_HALF))
        + source * jnp.exp(-0.5 * source * source) / ROOT_TWO_PI
    )


def score_tile(query_tile, key_tile, tile_start, limits):
    scores = jnp.einsum(
        "qshd,kshd->shqk", query_tile, key_tile, preferred_element_type=jnp.float32
    ) * HD ** (-0.5)
    places = tile_start + jnp.arange(key_tile.shape[0], dtype=jnp.int32)
    usable = places[None, :] < limits[:, None]
    return (scores, usable[:, None, None, :])


def attend_forward(query_heads, key_heads, value_heads, limits):
    tile_count = key_heads.shape[0] // KB
    attended_list = []
    total_list = []
    for first_row in range(0, query_heads.shape[0], QB):
        query_tile = query_heads[first_row : first_row + QB]
        stat_shape = (query_tile.shape[1], H, QB)

        def measure(state_pair, tile_index):
            top_now, mass_now = state_pair
            tile_start = tile_index * KB
            scores, usable = score_tile(
                query_tile,
                lax.dynamic_slice_in_dim(key_heads, tile_start, KB, 0),
                tile_start,
                limits,
            )
            top_next = jnp.maximum(top_now, jnp.max(jnp.where(usable, scores, NEG_BIG), axis=-1))
            tile_mass = jnp.where(usable, jnp.exp(scores - top_next[..., None]), 0.0)
            return (
                (top_next, mass_now * jnp.exp(top_now - top_next) + jnp.sum(tile_mass, axis=-1)),
                None,
            )

        start_pair = (
            jnp.full(stat_shape, NEG_BIG, jnp.float32),
            jnp.zeros(stat_shape, jnp.float32),
        )
        (top_all, mass_all), _ = lax.scan(
            measure, start_pair, jnp.arange(tile_count, dtype=jnp.int32)
        )
        log_total = top_all + jnp.log(mass_all)

        def collect(running, tile_index):
            tile_start = tile_index * KB
            scores, usable = score_tile(
                query_tile,
                lax.dynamic_slice_in_dim(key_heads, tile_start, KB, 0),
                tile_start,
                limits,
            )
            weights = jnp.where(usable, jnp.exp(scores - log_total[..., None]), 0.0).astype(
                jnp.bfloat16
            )
            value_tile = lax.dynamic_slice_in_dim(value_heads, tile_start, KB, 0)
            return (
                running
                + jnp.einsum(
                    "shqk,kshd->qshd", weights, value_tile, preferred_element_type=jnp.float32
                ),
                None,
            )

        start_sum = jnp.zeros(query_tile.shape, jnp.float32)
        attended_tile, _ = lax.scan(collect, start_sum, jnp.arange(tile_count, dtype=jnp.int32))
        attended_list.append(attended_tile)
        total_list.append(log_total)
    return (jnp.concatenate(attended_list, axis=0), total_list)


def attend_backward(query_heads, key_heads, value_heads, limits, grad_heads, row_delta, total_list):
    tile_count = key_heads.shape[0] // KB
    scale_now = HD ** (-0.5)
    key_terms = jnp.zeros(key_heads.shape, jnp.float32)
    value_terms = jnp.zeros(value_heads.shape, jnp.float32)
    query_list = []
    for tile_number, first_row in enumerate(range(0, query_heads.shape[0], QB)):
        query_tile = query_heads[first_row : first_row + QB]
        grad_tile = grad_heads[first_row : first_row + QB]
        delta_tile = jnp.transpose(row_delta[first_row : first_row + QB], (1, 2, 0))
        log_total = total_list[tile_number]

        def sweep(state_trio, tile_index):
            query_grad, key_accum, value_accum = state_trio
            tile_start = tile_index * KB
            key_tile = lax.dynamic_slice_in_dim(key_heads, tile_start, KB, 0)
            value_tile = lax.dynamic_slice_in_dim(value_heads, tile_start, KB, 0)
            scores, usable = score_tile(query_tile, key_tile, tile_start, limits)
            probs = jnp.where(usable, jnp.exp(scores - log_total[..., None]), 0.0)
            slopes = jnp.einsum(
                "qshd,kshd->shqk", grad_tile, value_tile, preferred_element_type=jnp.float32
            )
            score_grads = (probs * (slopes - delta_tile[..., None])).astype(jnp.bfloat16)
            query_grad = (
                query_grad
                + jnp.einsum(
                    "shqk,kshd->qshd", score_grads, key_tile, preferred_element_type=jnp.float32
                )
                * scale_now
            )
            key_piece = (
                jnp.einsum(
                    "shqk,qshd->kshd", score_grads, query_tile, preferred_element_type=jnp.float32
                )
                * scale_now
            )
            value_piece = jnp.einsum(
                "shqk,qshd->kshd",
                probs.astype(jnp.bfloat16),
                grad_tile,
                preferred_element_type=jnp.float32,
            )
            key_accum = lax.dynamic_update_slice_in_dim(
                key_accum,
                lax.dynamic_slice_in_dim(key_accum, tile_start, KB, 0) + key_piece,
                tile_start,
                0,
            )
            value_accum = lax.dynamic_update_slice_in_dim(
                value_accum,
                lax.dynamic_slice_in_dim(value_accum, tile_start, KB, 0) + value_piece,
                tile_start,
                0,
            )
            return ((query_grad, key_accum, value_accum), None)

        start_trio = (jnp.zeros(query_tile.shape, jnp.float32), key_terms, value_terms)
        (query_grad, key_terms, value_terms), _ = lax.scan(
            sweep, start_trio, jnp.arange(tile_count, dtype=jnp.int32)
        )
        query_list.append(query_grad)
    return (jnp.concatenate(query_list, axis=0), key_terms, value_terms)


def on_device(
    hidden_in,
    lengths,
    seq_order,
    query_weight,
    query_bias,
    key_weight,
    value_weight,
    value_bias,
    output_weight,
    output_bias,
    norm1_gain,
    norm1_shift,
    inner_weight,
    inner_bias,
    outer_weight,
    outer_bias,
    norm2_gain,
    norm2_shift,
    cotangent,
):
    feat_width = hidden_in.shape[2]
    per_group = hidden_in.shape[1] // lax.axis_size("fsdp")
    placed = jnp.take(hidden_in, seq_order, axis=1)
    tokens = lax.all_to_all(placed, "fsdp", split_axis=1, concat_axis=0, tiled=True)
    local_len = tokens.shape[0]
    row_count = local_len * per_group
    slot_ids = lax.axis_index("fsdp") * per_group + jnp.arange(per_group, dtype=jnp.int32)
    limits = jnp.take(lengths, jnp.take(seq_order, slot_ids))
    w_query, w_key, w_value, w_output, b_query, b_value, b_output, gain_one, shift_one = (
        lax.all_gather(query_weight, "fsdp", axis=0, tiled=True),
        lax.all_gather(key_weight, "fsdp", axis=0, tiled=True),
        lax.all_gather(value_weight, "fsdp", axis=0, tiled=True),
        lax.all_gather(output_weight, "fsdp", axis=0, tiled=True),
        lax.all_gather(query_bias, "fsdp", axis=0, tiled=True),
        lax.all_gather(value_bias, "fsdp", axis=0, tiled=True),
        lax.all_gather(output_bias, "fsdp", axis=0, tiled=True),
        lax.all_gather(norm1_gain, "fsdp", axis=0, tiled=True),
        lax.all_gather(norm1_shift, "fsdp", axis=0, tiled=True),
    )
    token_rows = tokens.reshape(row_count, feat_width)
    queries = (
        jnp.dot(token_rows, w_query, preferred_element_type=jnp.float32)
        + b_query.astype(jnp.float32)
    ).astype(jnp.bfloat16)
    key_part = jnp.dot(token_rows, w_key, preferred_element_type=jnp.float32)
    value_part = jnp.dot(token_rows, w_value, preferred_element_type=jnp.float32) + b_value.astype(
        jnp.float32
    )
    joined = (
        jnp.concatenate((key_part, value_part), axis=1)
        .astype(jnp.bfloat16)
        .reshape(local_len, per_group, 2 * feat_width)
    )
    joined_all = lax.all_gather(joined, "ctx", axis=0, tiled=True)
    full_len = joined_all.shape[0]
    key_heads = joined_all[:, :, :feat_width].reshape(full_len, per_group, H, HD)
    value_heads = joined_all[:, :, feat_width:].reshape(full_len, per_group, H, HD)
    query_heads = queries.reshape(local_len, per_group, H, HD)
    attended, total_list = attend_forward(query_heads, key_heads, value_heads, limits)
    mixed_low = attended.reshape(row_count, feat_width).astype(jnp.bfloat16)
    branch = jnp.dot(mixed_low, w_output, preferred_element_type=jnp.float32) + b_output.astype(
        jnp.float32
    )
    normed, unit_one, scale_one = norm_forward(
        token_rows.astype(jnp.float32) + branch,
        gain_one.astype(jnp.float32),
        shift_one.astype(jnp.float32),
    )
    normed_low = normed.astype(jnp.bfloat16)
    w_inner, w_outer, b_inner, b_outer, gain_two, shift_two = (
        lax.all_gather(inner_weight, "fsdp", axis=0, tiled=True),
        lax.all_gather(outer_weight, "fsdp", axis=0, tiled=True),
        lax.all_gather(inner_bias, "fsdp", axis=0, tiled=True),
        lax.all_gather(outer_bias, "fsdp", axis=0, tiled=True),
        lax.all_gather(norm2_gain, "fsdp", axis=0, tiled=True),
        lax.all_gather(norm2_shift, "fsdp", axis=0, tiled=True),
    )
    inner_pre = jnp.dot(normed_low, w_inner, preferred_element_type=jnp.float32) + b_inner.astype(
        jnp.float32
    )
    activated = gelu_exact(inner_pre).astype(jnp.bfloat16)
    outer_out = jnp.dot(activated, w_outer, preferred_element_type=jnp.float32) + b_outer.astype(
        jnp.float32
    )
    second, unit_two, scale_two = norm_forward(
        normed + outer_out, gain_two.astype(jnp.float32), shift_two.astype(jnp.float32)
    )
    layer_out = second.astype(jnp.bfloat16).reshape(local_len, per_group, feat_width)
    back_inner, back_outer, back_gain_two = (
        lax.all_gather(inner_weight, "fsdp", axis=0, tiled=True),
        lax.all_gather(outer_weight, "fsdp", axis=0, tiled=True),
        lax.all_gather(norm2_gain, "fsdp", axis=0, tiled=True),
    )
    upstream = cotangent.reshape(row_count, feat_width).astype(jnp.float32)
    d_second, grad_gain_two, grad_shift_two = norm_backward(
        upstream, unit_two, scale_two, back_gain_two.astype(jnp.float32)
    )
    d_outer = d_second.astype(jnp.bfloat16)
    grad_outer_w = jnp.einsum("tf,td->fd", activated, d_outer, preferred_element_type=jnp.float32)
    grad_outer_b = jnp.sum(d_outer.astype(jnp.float32), axis=0)
    inner_grad = jnp.einsum("td,fd->tf", d_outer, back_outer, preferred_element_type=jnp.float32)
    d_inner = (inner_grad * gelu_slope(inner_pre)).astype(jnp.bfloat16)
    grad_inner_w = jnp.einsum("td,tf->df", normed_low, d_inner, preferred_element_type=jnp.float32)
    grad_inner_b = jnp.sum(d_inner.astype(jnp.float32), axis=0)
    d_normed = d_second + jnp.einsum(
        "tf,df->td", d_inner, back_inner, preferred_element_type=jnp.float32
    )
    part_inner_w, part_outer_w, part_inner_b, part_outer_b, part_gain_two, part_shift_two = (
        lax.psum_scatter(grad_inner_w, "fsdp", scatter_dimension=0, tiled=True),
        lax.psum_scatter(grad_outer_w, "fsdp", scatter_dimension=0, tiled=True),
        lax.psum_scatter(grad_inner_b, "fsdp", scatter_dimension=0, tiled=True),
        lax.psum_scatter(grad_outer_b, "fsdp", scatter_dimension=0, tiled=True),
        lax.psum_scatter(grad_gain_two, "fsdp", scatter_dimension=0, tiled=True),
        lax.psum_scatter(grad_shift_two, "fsdp", scatter_dimension=0, tiled=True),
    )
    back_query, back_key, back_value, back_output, back_gain_one = (
        lax.all_gather(query_weight, "fsdp", axis=0, tiled=True),
        lax.all_gather(key_weight, "fsdp", axis=0, tiled=True),
        lax.all_gather(value_weight, "fsdp", axis=0, tiled=True),
        lax.all_gather(output_weight, "fsdp", axis=0, tiled=True),
        lax.all_gather(norm1_gain, "fsdp", axis=0, tiled=True),
    )
    d_res, grad_gain_one, grad_shift_one = norm_backward(
        d_normed, unit_one, scale_one, back_gain_one.astype(jnp.float32)
    )
    d_branch = d_res.astype(jnp.bfloat16)
    grad_output_w = jnp.einsum("td,te->de", mixed_low, d_branch, preferred_element_type=jnp.float32)
    grad_output_b = jnp.sum(d_branch.astype(jnp.float32), axis=0)
    d_mixed = jnp.einsum(
        "te,de->td", d_branch, back_output, preferred_element_type=jnp.float32
    ).astype(jnp.bfloat16)
    grad_heads = d_mixed.reshape(local_len, per_group, H, HD)
    row_delta = jnp.sum(grad_heads.astype(jnp.float32) * attended, axis=-1)
    query_grads, key_terms, value_terms = attend_backward(
        query_heads, key_heads, value_heads, limits, grad_heads, row_delta, total_list
    )
    key_sum, value_sum = (
        lax.psum_scatter(
            key_terms.reshape(full_len, per_group, feat_width).astype(jnp.bfloat16),
            "ctx",
            scatter_dimension=0,
            tiled=True,
        ).astype(jnp.float32),
        lax.psum_scatter(
            value_terms.reshape(full_len, per_group, feat_width).astype(jnp.bfloat16),
            "ctx",
            scatter_dimension=0,
            tiled=True,
        ).astype(jnp.float32),
    )
    d_query = query_grads.reshape(row_count, feat_width).astype(jnp.bfloat16)
    d_keys = key_sum.reshape(row_count, feat_width).astype(jnp.bfloat16)
    d_values = value_sum.reshape(row_count, feat_width).astype(jnp.bfloat16)
    grad_query_w = jnp.einsum("td,te->de", token_rows, d_query, preferred_element_type=jnp.float32)
    grad_query_b = jnp.sum(d_query.astype(jnp.float32), axis=0)
    grad_key_w = jnp.einsum("td,te->de", token_rows, d_keys, preferred_element_type=jnp.float32)
    grad_value_w = jnp.einsum("td,te->de", token_rows, d_values, preferred_element_type=jnp.float32)
    grad_value_b = jnp.sum(d_values.astype(jnp.float32), axis=0)
    d_placed = d_res + jnp.einsum(
        "te,de->td", d_query, back_query, preferred_element_type=jnp.float32
    )
    d_placed = d_placed + jnp.einsum(
        "te,de->td", d_keys, back_key, preferred_element_type=jnp.float32
    )
    d_placed = d_placed + jnp.einsum(
        "te,de->td", d_values, back_value, preferred_element_type=jnp.float32
    )
    back_rows = d_placed.astype(jnp.bfloat16).reshape(local_len, per_group, feat_width)
    returned = lax.all_to_all(back_rows, "fsdp", split_axis=0, concat_axis=1, tiled=True)
    inverse = (
        jnp.zeros(seq_order.shape, jnp.int32)
        .at[seq_order]
        .set(jnp.arange(seq_order.shape[0], dtype=jnp.int32))
    )
    grad_in = jnp.take(returned, inverse, axis=1)
    (
        part_query_w,
        part_query_b,
        part_key_w,
        part_value_w,
        part_value_b,
        part_output_w,
        part_output_b,
        part_gain_one,
        part_shift_one,
    ) = (
        lax.psum_scatter(grad_query_w, "fsdp", scatter_dimension=0, tiled=True),
        lax.psum_scatter(grad_query_b, "fsdp", scatter_dimension=0, tiled=True),
        lax.psum_scatter(grad_key_w, "fsdp", scatter_dimension=0, tiled=True),
        lax.psum_scatter(grad_value_w, "fsdp", scatter_dimension=0, tiled=True),
        lax.psum_scatter(grad_value_b, "fsdp", scatter_dimension=0, tiled=True),
        lax.psum_scatter(grad_output_w, "fsdp", scatter_dimension=0, tiled=True),
        lax.psum_scatter(grad_output_b, "fsdp", scatter_dimension=0, tiled=True),
        lax.psum_scatter(grad_gain_one, "fsdp", scatter_dimension=0, tiled=True),
        lax.psum_scatter(grad_shift_one, "fsdp", scatter_dimension=0, tiled=True),
    )
    summed = (
        lax.psum(part_query_w.astype(jnp.bfloat16), "ctx").astype(jnp.float32),
        lax.psum(part_query_b.astype(jnp.bfloat16), "ctx").astype(jnp.float32),
        lax.psum(part_key_w.astype(jnp.bfloat16), "ctx").astype(jnp.float32),
        lax.psum(part_value_w.astype(jnp.bfloat16), "ctx").astype(jnp.float32),
        lax.psum(part_value_b.astype(jnp.bfloat16), "ctx").astype(jnp.float32),
        lax.psum(part_output_w.astype(jnp.bfloat16), "ctx").astype(jnp.float32),
        lax.psum(part_output_b.astype(jnp.bfloat16), "ctx").astype(jnp.float32),
        lax.psum(part_gain_one.astype(jnp.bfloat16), "ctx").astype(jnp.float32),
        lax.psum(part_shift_one.astype(jnp.bfloat16), "ctx").astype(jnp.float32),
        lax.psum(part_inner_w.astype(jnp.bfloat16), "ctx").astype(jnp.float32),
        lax.psum(part_inner_b.astype(jnp.bfloat16), "ctx").astype(jnp.float32),
        lax.psum(part_outer_w.astype(jnp.bfloat16), "ctx").astype(jnp.float32),
        lax.psum(part_outer_b.astype(jnp.bfloat16), "ctx").astype(jnp.float32),
        lax.psum(part_gain_two.astype(jnp.bfloat16), "ctx").astype(jnp.float32),
        lax.psum(part_shift_two.astype(jnp.bfloat16), "ctx").astype(jnp.float32),
    )
    return (
        layer_out,
        grad_in,
        summed[0],
        summed[1],
        summed[2],
        summed[3],
        summed[4],
        summed[5],
        summed[6],
        summed[7],
        summed[8],
        summed[9],
        summed[10],
        summed[11],
        summed[12],
        summed[13],
        summed[14],
    )


def solution(mesh):
    placed = (
        P(("ctx", "fsdp"), None, None),
        P(),
        P(),
        P("fsdp", None),
        P("fsdp"),
        P("fsdp", None),
        P("fsdp", None),
        P("fsdp"),
        P("fsdp", None),
        P("fsdp"),
        P("fsdp"),
        P("fsdp"),
        P("fsdp", None),
        P("fsdp"),
        P("fsdp", None),
        P("fsdp"),
        P("fsdp"),
        P("fsdp"),
        P("ctx", "fsdp", None),
    )
    return jax.shard_map(
        on_device,
        mesh=mesh,
        in_specs=placed,
        out_specs=(
            P("ctx", "fsdp", None),
            P(("ctx", "fsdp"), None, None),
            P("fsdp", None),
            P("fsdp"),
            P("fsdp", None),
            P("fsdp", None),
            P("fsdp"),
            P("fsdp", None),
            P("fsdp"),
            P("fsdp"),
            P("fsdp"),
            P("fsdp", None),
            P("fsdp"),
            P("fsdp", None),
            P("fsdp"),
            P("fsdp"),
            P("fsdp"),
        ),
        check_vma=False,
    )
```

profile of v0, /device:TPU:29, one launch (start us, length us, event | category | flops | bytes accessed | tf_op | source)
XLA Modules:
  0.0 1988.6 jit_solution(5585431369563168292)
XLA Ops:
  27.4 58.9 %all-reduce.18 = (bf16[768]{0:T(1024)(128)(2,1)S(1)}, bf16[768]{0:T(1024)(128)(2,1)S(1)}, bf16[768]{0:T(1024)(128)(2,1)S(1)}, bf16[768]{0:T(1024)(128)(2,1)S(1)}...) all-reduce(bf16[768]{0:T(1024)(128)(2,1)S(1)} %dynamic-update-slice, ...), channel_id=1, replica_groups=mesh['ctx'=4,'fsdp'=8] {'fsdp'}, use_global_device_ids=true, to_apply=%add | all-reduce | flops 6144 | bytes 24576
  89.6 18.4 all-gather.11.cloned.1.call-done
  116.1 20.8 %all-gather = bf16[8,1,384]{2,1,0:T(2,128)(2,1)S(1)} all-gather(bf16[1,1,384]{2,1,0:T(2,128)(2,1)S(1)} %reshape.624), channel_id=1, replica_groups=mesh['ctx'=4,'fsdp'=8] {'fsdp'}, dimensions={0}, use_global_device_ids=true | all-gather | bytes 6912 | tf_op jit(solution)/shard_map/all_gather | solution.py:250
  142.4 7.6 all-gather.15.cloned.1.call-done
  152.8 83.8 %all-gather.13.cloned.1.call-done = bf16[4096,1,1536]{0,2,1:T(8,128)(2,1)} async-done(((bf16[1024,1,1536]{0,2,1:T(8,128)(2,1)}), bf16[4096,1,1536]{0,2,1:T(8,128)(2,1)}) %all-gather.13.cloned.1.call-update) | async-done | bytes 12582928 | tf_op jit(solution)/shard_map/all_gather | solution.py:231
  236.6 10.5 fusion.136
  247.1 136.5 %while.82 = (s32[]{:T(128)}, f32[1,12,512]{2,1,0:T(8,128)S(1)}, f32[1,12,512]{2,1,0:T(8,128)S(1)}, s32[8]{0:T(128)S(1)}, s32[1]{0:T(128)}, /*index=5*/bf16[4096,...) while((s32[]{:T(128)}, f32[1,12,512]{2,1,0:T(8,128)S(1)}, ...), condition=%wide.region_9.11_spmd.clone, body=%wide.region_6.10_spmd.clone.sunk | while | flops 424705024 | bytes 27059900 | solution.py:81
  248.4 8.5 select_reduce_fusion.10
  265.3 8.5 select_reduce_fusion.10
  282.3 8.8 select_reduce_fusion.10
  299.6 8.5 select_reduce_fusion.10
  316.6 8.6 select_reduce_fusion.10
  333.6 8.5 select_reduce_fusion.10
  342.1 7.3 select_reduce_fusion.11
  350.8 8.5 select_reduce_fusion.10
  367.8 8.6 select_reduce_fusion.10
  383.6 136.7 %while.80 = (s32[]{:T(128)}, f32[1,12,512]{2,1,0:T(8,128)S(1)}, f32[1,12,512]{2,1,0:T(8,128)S(1)}, s32[8]{0:T(128)S(1)}, s32[1]{0:T(128)}, /*index=5*/bf16[4096,...) while((s32[]{:T(128)}, f32[1,12,512]{2,1,0:T(8,128)S(1)}, ...), condition=%wide.region_3.5_spmd.clone, body=%wide.region_0.4_spmd.clone.sunk | while | flops 424705024 | bytes 27059900 | solution.py:81
  385.3 8.5 select_reduce_fusion.8
  393.8 7.7 select_reduce_fusion.9
  402.8 8.5 select_reduce_fusion.8
  419.8 8.5 select_reduce_fusion.8
  436.8 8.5 select_reduce_fusion.8
  453.7 8.5 select_reduce_fusion.8
  470.7 8.5 select_reduce_fusion.8
  487.7 8.5 select_reduce_fusion.8
  504.6 8.5 select_reduce_fusion.8
  520.4 60.9 %while.81 = (s32[]{:T(128)}, f32[512,1,12,64]{0,3,2,1:T(8,128)}, s32[8]{0:T(128)S(1)}, bf16[4096,1,12,64]{0,3,2,1:T(8,128)(2,1)}, s32[1]{0:T(128)}, /*index=5*/b...) while((s32[]{:T(128)}, f32[512,1,12,64]{0,3,2,1:T(8,128)}, ...), condition=%wide.region_5.7_spmd.clone, body=%wide.region_4.6_spmd.clone.sunk | while | flops 818676736 | bytes 5532352 | solution.py:107
  584.1 61.2 %while.83 = (s32[]{:T(128)}, f32[512,1,12,64]{0,3,2,1:T(8,128)}, s32[8]{0:T(128)S(1)}, bf16[4096,1,12,64]{0,3,2,1:T(8,128)(2,1)}, s32[1]{0:T(128)}, /*index=5*/b...) while((s32[]{:T(128)}, f32[512,1,12,64]{0,3,2,1:T(8,128)}, ...), condition=%wide.region_11.13_spmd.clone, body=%wide.region_10.12_spmd.clone.sunk | while | flops 818676736 | bytes 5532352 | solution.py:107
  657.1 13.7 multiply_convert_fusion.2
  670.8 9.7 fusion.141
  687.1 14.7 convert_reduce_fusion
  701.8 9.7 multiply_reduce_fusion
  730.2 211.0 %while.84 = (s32[]{:T(128)}, f32[512,1,12,64]{0,3,2,1:T(8,128)}, f32[4096,1,12,64]{0,3,2,1:T(8,128)}, f32[4096,1,12,64]{0,3,2,1:T(8,128)}, s32[8]{0:T(128)S(1)},...) while((s32[]{:T(128)}, f32[512,1,12,64]{0,3,2,1:T(8,128)}, ...), condition=%wide.region_22.24_spmd.clone, body=%wide.region_21.23_spmd.clone.sunk | while | flops 2047083520 | bytes 96806664 | solution.py:170
  941.2 210.1 %while.85 = (s32[]{:T(128)}, f32[512,1,12,64]{0,3,2,1:T(8,128)}, f32[4096,1,12,64]{0,3,2,1:T(8,128)}, f32[4096,1,12,64]{0,3,2,1:T(8,128)}, s32[8]{0:T(128)S(1)},...) while((s32[]{:T(128)}, f32[512,1,12,64]{0,3,2,1:T(8,128)}, ...), condition=%wide.region_24.26_spmd.clone, body=%wide.region_23.25_spmd.clone.sunk | while | flops 2047083520 | bytes 99952424 | solution.py:170
  1151.3 8.3 convert_element_type.307
  1159.6 8.2 convert_element_type.310
  1179.9 37.2 %reduce-scatter.9.cloned.1.call-done = bf16[1024,1,768]{0,2,1:T(8,128)(2,1)} async-done(((bf16[4096,1,768]{0,2,1:T(8,128)(2,1)}), bf16[1024,1,768]{0,2,1:T(8,128)(2,1)}) %reduce-scatter.9.cloned.1.call-update) | async-done | bytes 1572880 | tf_op jit(solution)/shard_map/reduce_scatter | solution.py:315
  1221.9 55.7 %reduce-scatter.11.cloned.1.call-done = bf16[1024,1,768]{0,2,1:T(8,128)(2,1)} async-done(((bf16[4096,1,768]{0,2,1:T(8,128)(2,1)}), bf16[1024,1,768]{0,2,1:T(8,128)(2,1)}) %reduce-scatter.11.cloned.1.call-update) | async-done | bytes 1572880 | tf_op jit(solution)/shard_map/reduce_scatter | solution.py:321
  1282.4 10.6 fusion.131
  1293.3 9.9 fusion.142
  1324.8 40.8 %reduce-scatter.13.cloned.1.call-done = f32[96,768]{1,0:T(8,128)} async-done(((f32[768,768]{1,0:T(8,128)}), f32[96,768]{1,0:T(8,128)}) %reduce-scatter.13.cloned.1.call-update) | async-done | bytes 294928 | tf_op jit(solution)/shard_map/reduce_scatter | solution.py:364
  1367.2 71.2 %reduce-scatter.19.cloned.1.call-done = f32[96,768]{1,0:T(8,128)} async-done(((f32[768,768]{1,0:T(8,128)}), f32[96,768]{1,0:T(8,128)}) %reduce-scatter.19.cloned.1.call-update) | async-done | bytes 294928 | tf_op jit(solution)/shard_map/reduce_scatter | solution.py:369
  1440.0 70.6 %reduce-scatter.15.cloned.1.call-done = f32[96,768]{1,0:T(8,128)} async-done(((f32[768,768]{1,0:T(8,128)}), f32[96,768]{1,0:T(8,128)}) %reduce-scatter.15.cloned.1.call-update) | async-done | bytes 294928 | tf_op jit(solution)/shard_map/reduce_scatter | solution.py:366
  1512.2 70.8 %reduce-scatter.17.cloned.1.call-done = f32[96,768]{1,0:T(8,128)} async-done(((f32[768,768]{1,0:T(8,128)}), f32[96,768]{1,0:T(8,128)}) %reduce-scatter.17.cloned.1.call-update) | async-done | bytes 294928 | tf_op jit(solution)/shard_map/reduce_scatter | solution.py:367
  1584.7 164.6 %reduce-scatter.21.cloned.1.call-done = f32[96,3072]{1,0:T(8,128)} async-done(((f32[768,3072]{1,0:T(8,128)}), f32[96,3072]{1,0:T(8,128)}) %reduce-scatter.21.cloned.1.call-update) | async-done | bytes 1179664 | tf_op jit(solution)/shard_map/reduce_scatter | solution.py:286
  1751.4 162.5 %reduce-scatter.23.cloned.1.call-done = f32[384,768]{1,0:T(8,128)} async-done(((f32[3072,768]{1,0:T(8,128)}), f32[384,768]{1,0:T(8,128)}) %reduce-scatter.23.cloned.1.call-update) | async-done | bytes 1179664 | tf_op jit(solution)/shard_map/reduce_scatter | solution.py:287
  1918.4 26.2 %all-reduce.17 = (bf16[768]{0:T(1024)(128)(2,1)S(1)}, bf16[768]{0:T(1024)(128)(2,1)S(1)}, bf16[768]{0:T(1024)(128)(2,1)S(1)}, bf16[768]{0:T(1024)(128)(2,1)S(1)}...) all-reduce(f32[768]{0:T(1024)S(1)} %reduce_sum.196, ...), channel_id=5, replica_groups=mesh['ctx'=4,'fsdp'=8] {'fsdp'}, use_global_device_ids=true, to_apply=%region_31.33.clone | all-reduce | flops 9216 | bytes 55296
  1945.3 12.8 all-reduce.19
  (612 shorter events, 787.3 us)
Async XLA Ops:
  7.2 79.1 %all-gather.9.cloned.1.call-start = ((), (), s32[]{:S(2)}) async-start(), calls=%async_computation.10 | async-start | bytes 1327104 | tf_op jit(solution)/shard_map/all_gather | solution.py:208
  7.9 100.0 %all-gather.11.cloned.1.call-start = ((), (), s32[]{:S(2)}) async-start(), calls=%async_computation.11 | async-start | bytes 1327104 | tf_op jit(solution)/shard_map/all_gather | solution.py:209
  16.5 9.0 copy-start.54
  16.5 9.2 copy-start.55
  16.5 9.5 copy-start.56
  16.5 9.7 copy-start.57
  16.5 9.9 copy-start.58
  16.6 10.1 copy-start.59
  16.6 10.4 copy-start.60
  16.6 10.6 copy-start.61
  18.0 68.3 %all-to-all-start = ((bf16[128,8,768]{2,0,1:T(8,128)(2,1)}), bf16[128,8,768]{2,0,1:T(8,128)(2,1)S(1)}, u32[]{:S(2)}, u32[]{:S(2)}) async-start(bf16[128,8,768]{2,0,1:T(8,128)(2,1)} %copy.73), calls=%async_computation | async-start | bytes 3145728 | tf_op jit(solution)/shard_map/all_to_all | solution.py:201
  23.5 126.5 %all-gather.15.cloned.1.call-start = ((), (), s32[]{:S(2)}) async-start(), calls=%async_computation.13 | async-start | bytes 1327104 | tf_op jit(solution)/shard_map/all_gather | solution.py:207
  24.2 212.4 %all-gather.13.cloned.1.call-start = ((), (), s32[]{:S(2)}) async-start(), calls=%async_computation.12 | async-start | bytes 15728640 | tf_op jit(solution)/shard_map/all_gather | solution.py:231
  86.3 63.7 %copy-start.15 = (bf16[128,8,768]{2,0,1:T(8,128)(2,1)}, bf16[128,8,768]{2,0,1:T(8,128)(2,1)S(1)}, u32[]{:S(2)}) copy-start(bf16[128,8,768]{2,0,1:T(8,128)(2,1)S(1)} %all-to-all-done) | copy-start | bytes 4718596
  112.7 25.4 %copy-start.20 = (bf16[1024,1,768]{2,0,1:T(8,128)(2,1)S(1)}, bf16[1024,1,768]{2,0,1:T(8,128)(2,1)}, u32[]{:S(2)}) copy-start(bf16[1024,1,768]{2,0,1:T(8,128)(2,1)} %param.51) | copy-start | bytes 4718596
  112.7 27.7 %copy-start.63 = (s32[8]{0:T(128)S(1)}, s32[8]{0:T(128)}, u32[]{:S(2)}) copy-start(s32[8]{0:T(128)} %param.34) | copy-start | bytes 100
  112.7 538.9 %all-gather.17.cloned.1.call-start = ((), (), s32[]{:S(2)}) async-start(), calls=%async_computation.14 | async-start | bytes 1327104 | tf_op jit(solution)/shard_map/all_gather | solution.py:210
  113.3 543.8 %all-gather.19.cloned.1.call-start = ((), (), s32[]{:S(2)}) async-start(), calls=%async_computation.15 | async-start | bytes 5308416 | tf_op jit(solution)/shard_map/all_gather | solution.py:248
  113.9 556.9 %all-gather.21.cloned.1.call-start = ((), (), s32[]{:S(2)}) async-start(), calls=%async_computation.16 | async-start | bytes 5308416 | tf_op jit(solution)/shard_map/all_gather | solution.py:249
  114.6 1102.4 %reduce-scatter.9.cloned.1.call-start = ((), (), s32[]{:S(2)}) async-start(), calls=%async_computation.17 | async-start | bytes 7864320 | tf_op jit(solution)/shard_map/reduce_scatter | solution.py:315
  116.1 595.4 %copy-start.33 = (f32[768]{0:T(1024)}, f32[768]{0:T(1024)S(1)}, u32[]{:S(2)}) copy-start(f32[768]{0:T(1024)S(1)} %convert_element_type.288) | copy-start | bytes 9220
  116.1 554.7 %copy-start.42 = (f32[768]{0:T(1024)}, f32[768]{0:T(1024)S(1)}, u32[]{:S(2)}) copy-start(f32[768]{0:T(1024)S(1)} %convert_element_type.289) | copy-start | bytes 9220
  655.0 56.4 %copy-start.29 = (f32[1024]{0:T(1024)}, f32[1024]{0:T(1024)S(1)}, u32[]{:S(2)}) copy-start(f32[1024]{0:T(1024)S(1)} %broadcast_multiply_fusion.5) | copy-start | bytes 12292
  657.1 54.4 %copy-start.36 = (f32[1024]{0:T(1024)}, f32[1024]{0:T(1024)S(1)}, u32[]{:S(2)}) copy-start(f32[1024]{0:T(1024)S(1)} %add_rsqrt_fusion.1) | copy-start | bytes 12292
  657.1 13.7 copy-start.44
  683.8 18.0 slice-start
  687.1 14.7 copy-start.21
  687.1 14.7 copy-start.12
  687.1 14.7 slice-start.1
  730.2 211.1 %copy-start.5 = (bf16[512,1,12,64]{0,3,2,1:T(8,128)(2,1)S(1)}, bf16[512,1,12,64]{0,3,2,1:T(8,128)(2,1)}, u32[]{:S(2)}) copy-start(bf16[512,1,12,64]{0,3,2,1:T(8,128)(2,1)} %copy-done.4) | copy-start | bytes 2359300
  730.2 211.1 %copy-start.32 = (f32[1,12,512]{2,1,0:T(8,128)S(1)}, f32[1,12,512]{2,1,0:T(8,128)}, u32[]{:S(2)}) copy-start(f32[1,12,512]{2,1,0:T(8,128)} %copy-done.31) | copy-start | bytes 73732
  1159.6 118.0 %reduce-scatter.11.cloned.1.call-start = ((), (), s32[]{:S(2)}) async-start(), calls=%async_computation.18 | async-start | bytes 7864320 | tf_op jit(solution)/shard_map/reduce_scatter | solution.py:321
  1167.9 197.7 %reduce-scatter.13.cloned.1.call-start = ((), (), s32[]{:S(2)}) async-start(), calls=%async_computation.19 | async-start | bytes 2654208 | tf_op jit(solution)/shard_map/reduce_scatter | solution.py:364
  1174.6 263.8 %reduce-scatter.19.cloned.1.call-start = ((), (), s32[]{:S(2)}) async-start(), calls=%async_computation.22 | async-start | bytes 2654208 | tf_op jit(solution)/shard_map/reduce_scatter | solution.py:369
  1179.9 330.7 %reduce-scatter.15.cloned.1.call-start = ((), (), s32[]{:S(2)}) async-start(), calls=%async_computation.20 | async-start | bytes 2654208 | tf_op jit(solution)/shard_map/reduce_scatter | solution.py:366
  1221.8 60.6 %copy-start.30 = (f32[1024]{0:T(1024)S(1)}, f32[1024]{0:T(1024)}, u32[]{:S(2)}) copy-start(f32[1024]{0:T(1024)} %copy-done.29) | copy-start | bytes 12292
  1221.8 60.6 %copy-start.34 = (f32[768]{0:T(1024)S(1)}, f32[768]{0:T(1024)}, u32[]{:S(2)}) copy-start(f32[768]{0:T(1024)} %copy-done.33) | copy-start | bytes 9220
  1221.8 60.6 %copy-start.37 = (f32[1024]{0:T(1024)S(1)}, f32[1024]{0:T(1024)}, u32[]{:S(2)}) copy-start(f32[1024]{0:T(1024)} %copy-done.36) | copy-start | bytes 12292
  1221.8 60.6 %copy-start.43 = (f32[768]{0:T(1024)S(1)}, f32[768]{0:T(1024)}, u32[]{:S(2)}) copy-start(f32[768]{0:T(1024)} %copy-done.42) | copy-start | bytes 9220
  1221.8 361.2 %reduce-scatter.17.cloned.1.call-start = ((), (), s32[]{:S(2)}) async-start(), calls=%async_computation.21 | async-start | bytes 2654208 | tf_op jit(solution)/shard_map/reduce_scatter | solution.py:367
  1282.3 467.0 %reduce-scatter.21.cloned.1.call-start = ((), (), s32[]{:S(2)}) async-start(), calls=%async_computation.23 | async-start | bytes 10616832 | tf_op jit(solution)/shard_map/reduce_scatter | solution.py:286
  1293.0 620.9 %reduce-scatter.23.cloned.1.call-start = ((), (), s32[]{:S(2)}) async-start(), calls=%async_computation.24 | async-start | bytes 10616832 | tf_op jit(solution)/shard_map/reduce_scatter | solution.py:287
  1318.0 644.8 %all-to-all-start.1 = ((bf16[8,2,49152]{2,1,0:T(2,128)(2,1)}), bf16[8,2,49152]{2,1,0:T(2,128)(2,1)}, u32[]{:S(2)}, u32[]{:S(2)}) async-start(bf16[8,2,49152]{2,1,0:T(2,128)(2,1)} %reshape.676), calls=%async_computation.3 | async-start | bytes 3145728 | tf_op jit(solution)/shard_map/all_to_all | solution.py:346
  1323.5 650.9 %all-reduce.23.cloned.1.call-start = ((), (), s32[]{:S(2)}) async-start(), calls=%async_computation.25 | async-start | bytes 3538944 | tf_op jit(solution)/shard_map/psum | solution.py:375
  1440.0 476.1 %copy-start.9 = (bf16[1024,1,768]{0,2,1:T(8,128)(2,1)S(1)}, bf16[1024,1,768]{0,2,1:T(8,128)(2,1)}, u32[]{:S(2)}) copy-start(bf16[1024,1,768]{0,2,1:T(8,128)(2,1)} %copy.76) | copy-start | bytes 4718596
  1584.6 331.8 %copy-start.65 = (s32[8]{0:T(128)S(1)}, s32[8]{0:T(128)}, u32[]{:S(2)}) copy-start(s32[8]{0:T(128)} %copy-done.64) | copy-start | bytes 100
  1584.7 331.9 %copy-start.17 = (bf16[1024,1,768]{0,2,1:T(8,128)(2,1)S(1)}, bf16[1024,1,768]{0,2,1:T(8,128)(2,1)}, u32[]{:S(2)}) copy-start(bf16[1024,1,768]{0,2,1:T(8,128)(2,1)} %get-tuple-element.779) | copy-start | bytes 4718596
  1972.3 9.4 copy-start.1
  (59 other events, 224.3 us)
Sparse Core Ops, SparseCore 0:
  10.2 56.2 all-gather.8
  68.7 39.2 all-gather.10
  110.1 39.7 all-gather.14
  151.4 85.1 all-gather.12
  238.6 36.6 all-gather.16
  277.4 79.4 all-gather.18
  359.1 77.7 all-gather.20
  1159.7 57.3 reduce-scatter.8
  1219.6 57.8 reduce-scatter.10
  1280.9 84.6 reduce-scatter.12
  1369.1 69.2 reduce-scatter.18
  1441.7 68.8 reduce-scatter.14
  1514.1 68.8 reduce-scatter.16
  1586.5 162.7 reduce-scatter.20
  1752.7 161.1 reduce-scatter.22
  1917.7 46.9 all-reduce.22
where the time goes:
time: 2010 us; the launch traced here: 1990 us
  waiting for transfers between devices  787 us (39%)
  matrix products  743 us (37%)
  other arithmetic  177 us (9%)
  blocking collectives  119 us (6%)
  local copies, waits for them, and re-layouts  98.5 us (5%)
  loops' own time  34.2 us (2%)
    dot_general x32, matrix products, score_tile(): jnp.einsum('qshd,kshd->shqk', query_tile, key_tile, preferred_element_typ...  185 us
    reduce_scatter x1, waiting for transfers between devices, on_device(): lax.psum_scatter(grad_inner_w, 'fsdp', scatter_dimension=0, tiled=True)  165 us
    reduce_scatter x1, waiting for transfers between devices, on_device(): lax.psum_scatter(grad_outer_w, 'fsdp', scatter_dimension=0, tiled=True)  163 us
    reduce_sum x16, other arithmetic, measure(): jnp.sum(tile_mass, axis=-1)  115 us
    dot_general x16, matrix products, collect(): jnp.einsum('shqk,kshd->qshd', weights, value_tile, preferred_element_type...  102 us
    dot_general x16, matrix products, sweep(): jnp.einsum('shqk,qshd->kshd', score_grads, query_tile, preferred_element_...  92.8 us
    dot_general x16, matrix products, sweep(): jnp.einsum('shqk,kshd->qshd', score_grads, key_tile, preferred_element_ty...  91.7 us
    dot_general x16, matrix products, sweep(): jnp.einsum('qshd,kshd->shqk', grad_tile, value_tile, preferred_element_ty...  89.3 us
  transfers between devices with their start and end apart: 18, of which 11 were waited for; matrix products, arithmetic and copies ran while one was open for 26% of the time, Pallas kernels for 0%

commit v1 on v0

--- a/solution.py
+++ b/solution.py
@@ -1,13 +1,17 @@
+import functools
+
 import jax
 import jax.numpy as jnp
 from jax import lax
+from jax.experimental import pallas as pl
+from jax.experimental.pallas import tpu as pltpu
 from jax.sharding import PartitionSpec as P
 
-H = 12
-HD = 64
-QB = 512
-KB = 512
-
+SCALE = 64 ** (-0.5)
+LOG2E = 1.4426950408889634
+FORWARD_KEYS = 2048
+BACKWARD_KEYS = 1024
+VMEM_BYTES = 60 * 2**20
 
 NORM_EPSILON = 1e-12
 NEG_BIG = -1e30
@@ -41,137 +45,209 @@
     )
 
 
-def score_tile(query_tile, key_tile, tile_start, limits):
-    scores = jnp.einsum(
-        "qshd,kshd->shqk", query_tile, key_tile, preferred_element_type=jnp.float32
-    ) * HD ** (-0.5)
-    places = tile_start + jnp.arange(key_tile.shape[0], dtype=jnp.int32)
-    usable = places[None, :] < limits[:, None]
-    return (scores, usable[:, None, None, :])
-
-
-def attend_forward(query_heads, key_heads, value_heads, limits):
-    tile_count = key_heads.shape[0] // KB
-    attended_list = []
-    total_list = []
-    for first_row in range(0, query_heads.shape[0], QB):
-        query_tile = query_heads[first_row : first_row + QB]
-        stat_shape = (query_tile.shape[1], H, QB)
-
-        def measure(state_pair, tile_index):
-            top_now, mass_now = state_pair
-            tile_start = tile_index * KB
-            scores, usable = score_tile(
-                query_tile,
-                lax.dynamic_slice_in_dim(key_heads, tile_start, KB, 0),
-                tile_start,
-                limits,
-            )
-            top_next = jnp.maximum(top_now, jnp.max(jnp.where(usable, scores, NEG_BIG), axis=-1))
-            tile_mass = jnp.where(usable, jnp.exp(scores - top_next[..., None]), 0.0)
-            return (
-                (top_next, mass_now * jnp.exp(top_now - top_next) + jnp.sum(tile_mass, axis=-1)),
-                None,
-            )
-
-        start_pair = (
-            jnp.full(stat_shape, NEG_BIG, jnp.float32),
-            jnp.zeros(stat_shape, jnp.float32),
+def product(left, right, dims):
+    return lax.dot_general(left, right, (dims, ((), ())), preferred_element_type=jnp.float32)
+
+
+def lane_is_low():
+    return lax.broadcasted_iota(jnp.int32, (1, 128), 1) < 64
+
+
+def split_query(query_pair, low_half):
+    scaled = query_pair * (SCALE * LOG2E)
+    high = scaled.astype(jnp.bfloat16).astype(jnp.float32)
+    rest = pltpu.roll(scaled - high, 64, 1)
+    return (
+        jnp.where(low_half, high, rest).astype(jnp.bfloat16),
+        jnp.where(low_half, rest, high).astype(jnp.bfloat16),
+    )
+
+
+def twice(pair, low_half):
+    other = pltpu.roll(pair, 64, 1)
+    return (
+        jnp.where(low_half, pair, other).astype(jnp.bfloat16),
+        jnp.where(low_half, other, pair).astype(jnp.bfloat16),
+    )
+
+
+def forward_kernel(limit_ref, query_ref, key_ref, value_ref, attended_ref, lse_ref, *, key_rows):
+    low_half = lane_is_low()
+    limit = limit_ref[0]
+    queries = split_query(query_ref[...].astype(jnp.float32), low_half)
+    query_rows = query_ref.shape[0]
+
+    def step(tile, state):
+        start = pl.multiple_of(tile * key_rows, key_rows)
+        usable = start + lax.broadcasted_iota(jnp.int32, (key_rows, 1), 0) < limit
+        key_tile = key_ref[pl.ds(start, key_rows), :].astype(jnp.float32)
+        keys = twice(jnp.where(usable, key_tile, key_ref[0:1, :].astype(jnp.float32)), low_half)
+        value_tile = value_ref[pl.ds(start, key_rows), :].astype(jnp.float32)
+        value_tile = jnp.where(usable, value_tile, 0.0)
+        count = jnp.where(usable, 1.0, 0.0)
+        values = (
+            jnp.where(low_half, value_tile, count).astype(jnp.bfloat16),
+            jnp.where(low_half, count, value_tile).astype(jnp.bfloat16),
         )
-        (top_all, mass_all), _ = lax.scan(
-            measure, start_pair, jnp.arange(tile_count, dtype=jnp.int32)
+        fresh = []
+        for head in range(2):
+            top, total = state[head]
+            scores = product(queries[head], keys[head], ((1,), (1,)))
+            new_top = jnp.maximum(top, jnp.max(scores, axis=1, keepdims=True))
+            weights = jnp.exp2(scores - new_top).astype(jnp.bfloat16)
+            total = total * jnp.exp2(top - new_top) + product(weights, values[head], ((1,), (0,)))
+            fresh.append((new_top, total))
+        return tuple(fresh)
+
+    empty = (
+        jnp.full((query_rows, 1), NEG_BIG, jnp.float32),
+        jnp.zeros((query_rows, 128), jnp.float32),
+    )
+    (top_a, total_a), (top_b, total_b) = lax.fori_loop(
+        0, key_ref.shape[0] // key_rows, step, (empty, empty)
+    )
+    mass_a, mass_b = total_a[:, 64:65], total_b[:, 0:1]
+    attended_ref[...] = jnp.where(low_half, total_a / mass_a, total_b / mass_b)
+    lse = jnp.where(low_half, top_a + jnp.log2(mass_a), top_b + jnp.log2(mass_b)).T
+    lse_ref[0, 0:1, :] = lse[0:1, :]
+    lse_ref[0, 1:2, :] = lse[64:65, :]
+
+
+def backward_kernel(
+    limit_ref,
+    query_ref,
+    key_ref,
+    value_ref,
+    grad_ref,
+    attended_ref,
+    lse_ref,
+    d_query_ref,
+    d_key_ref,
+    d_value_ref,
+    query_sum,
+    *,
+    key_rows,
+):
+    low_half = lane_is_low()
+    high_half = jnp.logical_not(low_half)
+    lane = lax.broadcasted_iota(jnp.int32, (1, 128), 1)
+    limit = limit_ref[0]
+    query_pair = query_ref[...].astype(jnp.float32)
+    queries = split_query(query_pair, low_half)
+    scaled = query_pair * SCALE
+    grad_pair = grad_ref[...].astype(jnp.float32)
+    overlap = grad_pair * attended_ref[...]
+    own_query, own_grad, joined_grad = [], [], []
+    for head in range(2):
+        mine = low_half if head == 0 else high_half
+        own_query.append(jnp.where(mine, scaled, 0.0).astype(jnp.bfloat16))
+        own_grad.append(jnp.where(mine, grad_pair, 0.0).astype(jnp.bfloat16))
+        delta = -jnp.sum(jnp.where(mine, overlap, 0.0), axis=1, keepdims=True)
+        first = delta.astype(jnp.bfloat16).astype(jnp.float32)
+        second = (delta - first).astype(jnp.bfloat16).astype(jnp.float32)
+        third = delta - first - second
+        spare = 64 * (1 - head)
+        joined = jnp.where(lane == spare + 2, third, 0.0)
+        joined = jnp.where(lane == spare + 1, second, joined)
+        joined = jnp.where(lane == spare, first, joined)
+        joined_grad.append(jnp.where(mine, grad_pair, joined).astype(jnp.bfloat16))
+    query_sum[...] = jnp.zeros_like(query_sum)
+
+    def step(tile, carry):
+        start = pl.multiple_of(tile * key_rows, key_rows)
+        usable = start + lax.broadcasted_iota(jnp.int32, (key_rows, 1), 0) < limit
+        key_tile = key_ref[pl.ds(start, key_rows), :].astype(jnp.float32)
+        value_tile = value_ref[pl.ds(start, key_rows), :].astype(jnp.float32)
+        keys = twice(jnp.where(usable, key_tile, key_ref[0:1, :].astype(jnp.float32)), low_half)
+        own_tile = jnp.where(usable, key_tile * SCALE, 0.0)
+        key_piece = value_piece = None
+        for head in range(2):
+            mine = low_half if head == 0 else high_half
+            values = jnp.where(mine, value_tile, 1.0).astype(jnp.bfloat16)
+            own_key = jnp.where(mine, own_tile, 0.0).astype(jnp.bfloat16)
+            scores = product(keys[head], queries[head], ((1,), (1,)))
+            probs = jnp.exp2(scores - lse_ref[0, head : head + 1, :])
+            slopes = product(values, joined_grad[head], ((1,), (1,)))
+            score_grads = (probs * slopes).astype(jnp.bfloat16)
+            value_term = product(probs.astype(jnp.bfloat16), own_grad[head], ((1,), (0,)))
+            key_term = product(score_grads, own_query[head], ((1,), (0,)))
+            value_piece = value_term if value_piece is None else value_piece + value_term
+            key_piece = key_term if key_piece is None else key_piece + key_term
+            query_sum[...] += product(own_key, score_grads, ((0,), (0,)))
+        d_value_ref[pl.ds(start, key_rows), :] = jnp.where(usable, value_piece, 0.0).astype(
+            jnp.bfloat16
         )
-        log_total = top_all + jnp.log(mass_all)
-
-        def collect(running, tile_index):
-            tile_start = tile_index * KB
-            scores, usable = score_tile(
-                query_tile,
-                lax.dynamic_slice_in_dim(key_heads, tile_start, KB, 0),
-                tile_start,
-                limits,
-            )
-            weights = jnp.where(usable, jnp.exp(scores - log_total[..., None]), 0.0).astype(
-                jnp.bfloat16
-            )
-            value_tile = lax.dynamic_slice_in_dim(value_heads, tile_start, KB, 0)
-            return (
-                running
-                + jnp.einsum(
-                    "shqk,kshd->qshd", weights, value_tile, preferred_element_type=jnp.float32
-                ),
-                None,
-            )
-
-        start_sum = jnp.zeros(query_tile.shape, jnp.float32)
-        attended_tile, _ = lax.scan(collect, start_sum, jnp.arange(tile_count, dtype=jnp.int32))
-        attended_list.append(attended_tile)
-        total_list.append(log_total)
-    return (jnp.concatenate(attended_list, axis=0), total_list)
-
-
-def attend_backward(query_heads, key_heads, value_heads, limits, grad_heads, row_delta, total_list):
-    tile_count = key_heads.shape[0] // KB
-    scale_now = HD ** (-0.5)
-    key_terms = jnp.zeros(key_heads.shape, jnp.float32)
-    value_terms = jnp.zeros(value_heads.shape, jnp.float32)
-    query_list = []
-    for tile_number, first_row in enumerate(range(0, query_heads.shape[0], QB)):
-        query_tile = query_heads[first_row : first_row + QB]
-        grad_tile = grad_heads[first_row : first_row + QB]
-        delta_tile = jnp.transpose(row_delta[first_row : first_row + QB], (1, 2, 0))
-        log_total = total_list[tile_number]
-
-        def sweep(state_trio, tile_index):
-            query_grad, key_accum, value_accum = state_trio
-            tile_start = tile_index * KB
-            key_tile = lax.dynamic_slice_in_dim(key_heads, tile_start, KB, 0)
-            value_tile = lax.dynamic_slice_in_dim(value_heads, tile_start, KB, 0)
-            scores, usable = score_tile(query_tile, key_tile, tile_start, limits)
-            probs = jnp.where(usable, jnp.exp(scores - log_total[..., None]), 0.0)
-            slopes = jnp.einsum(
-                "qshd,kshd->shqk", grad_tile, value_tile, preferred_element_type=jnp.float32
-            )
-            score_grads = (probs * (slopes - delta_tile[..., None])).astype(jnp.bfloat16)
-            query_grad = (
-                query_grad
-                + jnp.einsum(
-                    "shqk,kshd->qshd", score_grads, key_tile, preferred_element_type=jnp.float32
-                )
-                * scale_now
-            )
-            key_piece = (
-                jnp.einsum(
-                    "shqk,qshd->kshd", score_grads, query_tile, preferred_element_type=jnp.float32
-                )
-                * scale_now
-            )
-            value_piece = jnp.einsum(
-                "shqk,qshd->kshd",
-                probs.astype(jnp.bfloat16),
-                grad_tile,
-                preferred_element_type=jnp.float32,
-            )
-            key_accum = lax.dynamic_update_slice_in_dim(
-                key_accum,
-                lax.dynamic_slice_in_dim(key_accum, tile_start, KB, 0) + key_piece,
-                tile_start,
-                0,
-            )
-            value_accum = lax.dynamic_update_slice_in_dim(
-                value_accum,
-                lax.dynamic_slice_in_dim(value_accum, tile_start, KB, 0) + value_piece,
-                tile_start,
-                0,
-            )
-            return ((query_grad, key_accum, value_accum), None)
-
-        start_trio = (jnp.zeros(query_tile.shape, jnp.float32), key_terms, value_terms)
-        (query_grad, key_terms, value_terms), _ = lax.scan(
-            sweep, start_trio, jnp.arange(tile_count, dtype=jnp.int32)
+        d_key_ref[pl.ds(start, key_rows), :] = jnp.where(usable, key_piece, 0.0).astype(
+            jnp.bfloat16
         )
-        query_list.append(query_grad)
-    return (jnp.concatenate(query_list, axis=0), key_terms, value_terms)
+        return carry
+
+    lax.fori_loop(0, key_ref.shape[0] // key_rows, step, 0)
+    d_query_ref[...] = query_sum[...].T.astype(jnp.bfloat16)
+
+
+def attend_forward(queries, joined, limit):
+    rows, width = queries.shape
+    full = joined.shape[0]
+    pairs = width // 128
+    row_spec = pl.BlockSpec((rows, 128), lambda pair, *_: (0, pair))
+    return pl.pallas_call(
+        functools.partial(forward_kernel, key_rows=FORWARD_KEYS),
+        grid_spec=pltpu.PrefetchScalarGridSpec(
+            num_scalar_prefetch=1,
+            grid=(pairs,),
+            in_specs=[
+                row_spec,
+                pl.BlockSpec((full, 128), lambda pair, *_: (0, pair)),
+                pl.BlockSpec((full, 128), lambda pair, *_: (0, pair + pairs)),
+            ],
+            out_specs=[row_spec, pl.BlockSpec((1, 2, rows), lambda pair, *_: (pair, 0, 0))],
+        ),
+        out_shape=[
+            jax.ShapeDtypeStruct((rows, width), jnp.float32),
+            jax.ShapeDtypeStruct((pairs, 2, rows), jnp.float32),
+        ],
+        compiler_params=pltpu.CompilerParams(vmem_limit_bytes=VMEM_BYTES),
+        cost_estimate=pl.CostEstimate(
+            flops=16 * rows * full * width, bytes_accessed=20_000_000, transcendentals=0
+        ),
+        name="attend_forward",
+    )(limit, queries, joined, joined)
+
+
+def attend_backward(queries, joined, limit, grad_rows, attended, lse):
+    rows, width = queries.shape
+    full = joined.shape[0]
+    pairs = width // 128
+    row_spec = pl.BlockSpec((rows, 128), lambda pair, *_: (0, pair))
+    key_spec = pl.BlockSpec((full, 128), lambda pair, *_: (0, pair))
+    return pl.pallas_call(
+        functools.partial(backward_kernel, key_rows=BACKWARD_KEYS),
+        grid_spec=pltpu.PrefetchScalarGridSpec(
+            num_scalar_prefetch=1,
+            grid=(pairs,),
+            in_specs=[
+                row_spec,
+                key_spec,
+                pl.BlockSpec((full, 128), lambda pair, *_: (0, pair + pairs)),
+                row_spec,
+                row_spec,
+                pl.BlockSpec((1, 2, rows), lambda pair, *_: (pair, 0, 0)),
+            ],
+            out_specs=[row_spec, key_spec, key_spec],
+            scratch_shapes=[pltpu.VMEM((128, rows), jnp.float32)],
+        ),
+        out_shape=[
+            jax.ShapeDtypeStruct((rows, width), jnp.bfloat16),
+            jax.ShapeDtypeStruct((full, width), jnp.bfloat16),
+            jax.ShapeDtypeStruct((full, width), jnp.bfloat16),
+        ],
+        compiler_params=pltpu.CompilerParams(vmem_limit_bytes=VMEM_BYTES),
+        cost_estimate=pl.CostEstimate(
+            flops=40 * rows * full * width, bytes_accessed=40_000_000, transcendentals=0
+        ),
+        name="attend_backward",
+    )(limit, queries, joined, joined, grad_rows, attended, lse)
 
 
 def on_device(
@@ -230,10 +306,8 @@
     )
     joined_all = lax.all_gather(joined, "ctx", axis=0, tiled=True)
     full_len = joined_all.shape[0]
-    key_heads = joined_all[:, :, :feat_width].reshape(full_len, per_group, H, HD)
-    value_heads = joined_all[:, :, feat_width:].reshape(full_len, per_group, H, HD)
-    query_heads = queries.reshape(local_len, per_group, H, HD)
-    attended, total_list = attend_forward(query_heads, key_heads, value_heads, limits)
+    joined_all = joined_all.reshape(full_len, 2 * feat_width)
+    attended, lse = attend_forward(queries, joined_all, limits)
     mixed_low = attended.reshape(row_count, feat_width).astype(jnp.bfloat16)
     branch = jnp.dot(mixed_low, w_output, preferred_element_type=jnp.float32) + b_output.astype(
         jnp.float32
@@ -283,12 +357,12 @@
         "tf,df->td", d_inner, back_inner, preferred_element_type=jnp.float32
     )
     part_inner_w, part_outer_w, part_inner_b, part_outer_b, part_gain_two, part_shift_two = (
-        lax.psum_scatter(grad_inner_w, "fsdp", scatter_dimension=0, tiled=True),
-        lax.psum_scatter(grad_outer_w, "fsdp", scatter_dimension=0, tiled=True),
-        lax.psum_scatter(grad_inner_b, "fsdp", scatter_dimension=0, tiled=True),
-        lax.psum_scatter(grad_outer_b, "fsdp", scatter_dimension=0, tiled=True),
-        lax.psum_scatter(grad_gain_two, "fsdp", scatter_dimension=0, tiled=True),
-        lax.psum_scatter(grad_shift_two, "fsdp", scatter_dimension=0, tiled=True),
+        lax.psum_scatter(grad_inner_w.astype(jnp.bfloat16), "fsdp", scatter_dimension=0, tiled=True),
+        lax.psum_scatter(grad_outer_w.astype(jnp.bfloat16), "fsdp", scatter_dimension=0, tiled=True),
+        lax.psum_scatter(grad_inner_b.astype(jnp.bfloat16), "fsdp", scatter_dimension=0, tiled=True),
+        lax.psum_scatter(grad_outer_b.astype(jnp.bfloat16), "fsdp", scatter_dimension=0, tiled=True),
+        lax.psum_scatter(grad_gain_two.astype(jnp.bfloat16), "fsdp", scatter_dimension=0, tiled=True),
+        lax.psum_scatter(grad_shift_two.astype(jnp.bfloat16), "fsdp", scatter_dimension=0, tiled=True),
     )
     back_query, back_key, back_value, back_output, back_gain_one = (
         lax.all_gather(query_weight, "fsdp", axis=0, tiled=True),
@@ -306,10 +380,8 @@
     d_mixed = jnp.einsum(
         "te,de->td", d_branch, back_output, preferred_element_type=jnp.float32
     ).astype(jnp.bfloat16)
-    grad_heads = d_mixed.reshape(local_len, per_group, H, HD)
-    row_delta = jnp.sum(grad_heads.astype(jnp.float32) * attended, axis=-1)
-    query_grads, key_terms, value_terms = attend_backward(
-        query_heads, key_heads, value_heads, limits, grad_heads, row_delta, total_list
+    d_query, key_terms, value_terms = attend_backward(
+        queries, joined_all, limits, d_mixed, attended, lse
     )
     key_sum, value_sum = (
         lax.psum_scatter(
@@ -325,7 +397,6 @@
             tiled=True,
         ).astype(jnp.float32),
     )
-    d_query = query_grads.reshape(row_count, feat_width).astype(jnp.bfloat16)
     d_keys = key_sum.reshape(row_count, feat_width).astype(jnp.bfloat16)
     d_values = value_sum.reshape(row_count, feat_width).astype(jnp.bfloat16)
     grad_query_w = jnp.einsum("td,te->de", token_rows, d_query, preferred_element_type=jnp.float32)
@@ -361,15 +432,15 @@
         part_gain_one,
         part_shift_one,
     ) = (
-        lax.psum_scatter(grad_query_w, "fsdp", scatter_dimension=0, tiled=True),
-        lax.psum_scatter(grad_query_b, "fsdp", scatter_dimension=0, tiled=True),
-        lax.psum_scatter(grad_key_w, "fsdp", scatter_dimension=0, tiled=True),
-        lax.psum_scatter(grad_value_w, "fsdp", scatter_dimension=0, tiled=True),
-        lax.psum_scatter(grad_value_b, "fsdp", scatter_dimension=0, tiled=True),
-        lax.psum_scatter(grad_output_w, "fsdp", scatter_dimension=0, tiled=True),
-        lax.psum_scatter(grad_output_b, "fsdp", scatter_dimension=0, tiled=True),
-        lax.psum_scatter(grad_gain_one, "fsdp", scatter_dimension=0, tiled=True),
-        lax.psum_scatter(grad_shift_one, "fsdp", scatter_dimension=0, tiled=True),
+        lax.psum_scatter(grad_query_w.astype(jnp.bfloat16), "fsdp", scatter_dimension=0, tiled=True),
+        lax.psum_scatter(grad_query_b.astype(jnp.bfloat16), "fsdp", scatter_dimension=0, tiled=True),
+        lax.psum_scatter(grad_key_w.astype(jnp.bfloat16), "fsdp", scatter_dimension=0, tiled=True),
+        lax.psum_scatter(grad_value_w.astype(jnp.bfloat16), "fsdp", scatter_dimension=0, tiled=True),
+        lax.psum_scatter(grad_value_b.astype(jnp.bfloat16), "fsdp", scatter_dimension=0, tiled=True),
+        lax.psum_scatter(grad_output_w.astype(jnp.bfloat16), "fsdp", scatter_dimension=0, tiled=True),
+        lax.psum_scatter(grad_output_b.astype(jnp.bfloat16), "fsdp", scatter_dimension=0, tiled=True),
+        lax.psum_scatter(grad_gain_one.astype(jnp.bfloat16), "fsdp", scatter_dimension=0, tiled=True),
+        lax.psum_scatter(grad_shift_one.astype(jnp.bfloat16), "fsdp", scatter_dimension=0, tiled=True),
     )
     summed = (
         lax.psum(part_query_w.astype(jnp.bfloat16), "ctx").astype(jnp.float32),

time: 2010 us -> 1310 us (0.65)
  matrix products: 743 us -> 116 us
  Pallas kernels: 0 us -> 202 us
  other arithmetic: 177 us -> 36.1 us
  local copies, waits for them, and re-layouts: 98.5 us -> 31 us
  loops' own time: 34.2 us -> 0 us
  waiting for transfers between devices: 787 us -> 760 us
    dot_general x112 -> x0, matrix products: 638 us -> none  [the longest x32 185 us: score_tile(): jnp.einsum('qshd,kshd->shqk', query_tile, key_tile, preferred_element_typ...]
    pallas_call x0 -> x2, Pallas kernels: none -> 202 us  [the longest x1 133 us: attend_backward(): pl.pallas_call(functools.partial(backward_kernel, key_rows=BACKWARD_KEYS)...]
    reduce_scatter x6, waiting for transfers between devices: 580 us -> 457 us  [the longest x1 101 us: on_device(): lax.psum_scatter(grad_inner_w.astype(jnp.bfloat16), 'fsdp', scatter_dimen...]
    reduce_sum x17 -> x0, other arithmetic: 116 us -> none  [the longest x16 115 us: measure(): jnp.sum(tile_mass, axis=-1)]
    all_gather x1, waiting for transfers between devices: 0.01 us -> 65.8 us  [on_device(): lax.all_gather(outer_weight, 'fsdp', axis=0, tiled=True)]
    all_gather x1, waiting for transfers between devices: 0.02 us -> 42.9 us  [on_device(): lax.all_gather(inner_weight, 'fsdp', axis=0, tiled=True)]
    another operation x6 -> x0, loops' own time: 34.2 us -> none  [the longest x2 11.7 us: attend_backward(): lax.scan(sweep, start_trio, jnp.arange(tile_count, dtype=jnp.int32))]
    convert_element_type x9 -> x0, other arithmetic: 30.6 us -> none  [the longest x1 8.26 us: on_device(): key_terms.reshape(full_len, per_group, feat_width).astype(jnp.bfloat16)]
  transfers between devices with their start and end apart: 18 -> 18, of which waited for: 11 -> 13; matrix products, arithmetic and copies ran while one was open for 26% -> 10% of each run, Pallas kernels for 0% -> 5%
where the time goes in v1:
time: 1310 us; the launch traced here: 1300 us
  waiting for transfers between devices  760 us (58%)
  Pallas kernels  202 us (15%)
  blocking collectives  121 us (9%)
  matrix products  116 us (9%)
  other arithmetic  36.1 us (3%)
  local copies, waits for them, and re-layouts  31 us (2%)
  between operations  18.5 us (1%)
    pallas_call x1, Pallas kernels, attend_backward(): pl.pallas_call(functools.partial(backward_kernel, key_rows=BACKWARD_KEYS)...  133 us
    reduce_scatter x1, waiting for transfers between devices, on_device(): lax.psum_scatter(grad_inner_w.astype(jnp.bfloat16), 'fsdp', scatter_dimen...  101 us
    reduce_scatter x1, waiting for transfers between devices, on_device(): lax.psum_scatter(grad_outer_w.astype(jnp.bfloat16), 'fsdp', scatter_dimen...  99 us
    unnamed x2, blocking collectives  85.5 us
    all_gather x1, waiting for transfers between devices, on_device(): joined_all = lax.all_gather(joined, 'ctx', axis=0, tiled=True)  82.7 us
    pallas_call x1, Pallas kernels, attend_forward(): pl.pallas_call(functools.partial(forward_kernel, key_rows=FORWARD_KEYS),...  69.6 us
    reduce_scatter x1, waiting for transfers between devices, on_device(): lax.psum_scatter(grad_value_w.astype(jnp.bfloat16), 'fsdp', scatter_dimen...  67.7 us
    reduce_scatter x1, waiting for transfers between devices, on_device(): lax.psum_scatter(grad_output_w.astype(jnp.bfloat16), 'fsdp', scatter_dime...  67.2 us
  transfers between devices with their start and end apart: 18, of which 13 were waited for; matrix products, arithmetic and copies ran while one was open for 10% of the time, Pallas kernels for 5%

profile of v1, /device:TPU:29, one launch (start us, length us, event | category | flops | bytes accessed | tf_op | source)
XLA Modules:
  0.0 1297.0 jit_solution(7857701645586272444)
XLA Ops:
  10.0 5.0 gather_fusion
  16.8 5.4 all-to-all-start
  25.9 59.8 %all-reduce.18 = (bf16[768]{0:T(1024)(128)(2,1)S(1)}, bf16[768]{0:T(1024)(128)(2,1)S(1)}, bf16[768]{0:T(1024)(128)(2,1)S(1)}, bf16[768]{0:T(1024)(128)(2,1)S(1)}...) all-reduce(bf16[768]{0:T(1024)(128)(2,1)S(1)} %dynamic-update-slice, ...), channel_id=1, replica_groups=mesh['ctx'=4,'fsdp'=8] {'fsdp'}, use_global_device_ids=true, to_apply=%add.2 | all-reduce | flops 5376 | bytes 21504
  85.8 3.2 fusion.31
  89.0 18.9 %all-gather.13.cloned.1.call-done = bf16[768,768]{1,0:T(8,128)(2,1)} async-done(((bf16[96,768]{1,0:T(8,128)(2,1)}), bf16[768,768]{1,0:T(8,128)(2,1)}) %all-gather.13.cloned.1.call-update) | async-done | bytes 1179664 | tf_op jit(solution)/shard_map/all_gather | solution.py:285
  107.9 2.7 fusion.32
  115.8 20.9 %all-gather = bf16[8,1,384]{2,1,0:T(2,128)(2,1)S(1)} all-gather(bf16[1,1,384]{2,1,0:T(2,128)(2,1)S(1)} %reshape.262), channel_id=1, replica_groups=mesh['ctx'=4,'fsdp'=8] {'fsdp'}, dimensions={0}, use_global_device_ids=true | all-gather | bytes 6912 | tf_op jit(solution)/shard_map/all_gather | solution.py:324
  138.8 2.6 copy.91
  141.4 8.7 all-gather.9.cloned.1.call-done
  150.1 3.8 add_convert_fusion.3.query_ref
  153.9 82.7 %all-gather.15.cloned.1.call-done = bf16[4096,1,1536]{2,0,1:T(8,128)(2,1)} async-done(((bf16[1024,1,1536]{2,0,1:T(8,128)(2,1)}), bf16[4096,1,1536]{2,0,1:T(8,128)(2,1)}) %all-gather.15.cloned.1.call-update) | async-done | bytes 12582928 | tf_op jit(solution)/shard_map/all_gather | solution.py:307
  236.7 69.6 %attend_forward.1 = (f32[1024,768]{1,0:T(8,128)}, f32[6,2,1024]{2,1,0:T(2,128)}) custom-call(s32[1]{0:T(128)S(6)} %select_n.28.limit_ref, bf16[1024,768]{1,0:T(8,128)(2,1)} %add_convert_fusion.3.query_ref, bf16[4096,1536]{1,0:T(8,128)(2,1)} %bitcast.96, bf16[4096,1536]{1,0:T(8,128)(2,1)} %bitcast.97), custom_call_target="tpu_custom_call" | custom-call | flops 51539607552 | bytes 20000000 | tf_op jit(solution)/shard_map/attend_forward/pallas_call | solution.py:194
  306.3 5.5 fusion.46
  311.8 2.3 multiply_reduce_fusion.3
  314.1 42.9 %all-gather.19.cloned.1.call-done = bf16[768,3072]{1,0:T(8,128)(2,1)} async-done(((bf16[96,3072]{1,0:T(8,128)(2,1)}), bf16[768,3072]{1,0:T(8,128)(2,1)}) %all-gather.19.cloned.1.call-update) | async-done | bytes 4718608 | tf_op jit(solution)/shard_map/all_gather | solution.py:322
  357.0 14.1 %multiply_convert_fusion = (bf16[1024,3072]{1,0:T(8,128)(2,1)}, f32[1024,3072]{1,0:T(8,128)}) fusion(f32[3072]{0:T(1024)S(1)} %bitcast.94, bf16[768,3072]{1,0:T(8,128)(2,1)} %all-gather.19.cloned.1.call-done, f32[1024,768]{0,1:T(8,128)} %get-tuple-element.164, f32[768]{0:T(1024)S(1)} %convert_element_type.178, f32[768]{0:T(1024)S(1)} %convert_element_type.177, ...), kind=kOutput, calls=%fused_computation.10 | convolution fusion | flops 4854644736 | bytes 26765312 | tf_op jit(solution)/shard_map/dot_general | solution.py:329
  371.1 65.8 %all-gather.21.cloned.1.call-done = bf16[3072,768]{1,0:T(8,128)(2,1)} async-done(((bf16[384,768]{1,0:T(8,128)(2,1)}), bf16[3072,768]{1,0:T(8,128)(2,1)}) %all-gather.21.cloned.1.call-update) | async-done | bytes 4718608 | tf_op jit(solution)/shard_map/all_gather | solution.py:323
  436.9 9.4 fusion.47
  450.5 13.1 %fusion.48 = (bf16[3072]{0:T(1024)(128)(2,1)}, bf16[1024,3072]{1,0:T(8,128)(2,1)S(1)}) fusion(f32[1024,3072]{1,0:T(8,128)} %get-tuple-element.166, f32[3072]{0:T(1024)S(1)} %bitcast.95, bf16[1024,768]{0,1:T(8,128)(2,1)S(1)} %get-tuple-element.158, bf16[3072,768]{1,0:T(8,128)(2,1)S(1)} %bitcast.103), kind=kOutput, calls=%fused_computation.87 | convolution fusion | flops 4869583872 | bytes 25184256 | tf_op jit(solution)/shard_map/td,fd->tf/dot_general | solution.py:352
  463.7 11.4 multiply_reduce_fusion
  475.1 3.7 convert_reduce_fusion
  478.9 2.6 convolution_convert_fusion.2.grad_ref
  481.4 132.5 %attend_backward.1 = (bf16[1024,768]{1,0:T(8,128)(2,1)}, bf16[4096,768]{1,0:T(8,128)(2,1)}, bf16[4096,768]{1,0:T(8,128)(2,1)}) custom-call(s32[1]{0:T(128)S(6)} %select_n.28.limit_ref, bf16[1024,768]{1,0:T(8,128)(2,1)} %add_convert_fusion.3.query_ref, bf16[4096,1536]{1,0:T(8,128)(2,1)} %bitcast.98, bf16[4096,1536]{1,0:T(8,128)(2,1)} %bitcast.99, ...), custom_call_target="tpu_custom_call" | custom-call | flops 128849018880 | bytes 40000000 | tf_op jit(solution)/shard_map/attend_backward/pallas_call | solution.py:224
  614.8 4.3 convolution_convert_fusion.5
  619.2 4.4 convolution_convert_fusion.4
  623.7 11.5 convolution_convert_fusion.1
  635.3 10.2 convolution_convert_fusion
  645.6 28.2 %reduce-scatter.9.cloned.1.call-done = bf16[1024,1,768]{2,0,1:T(8,128)(2,1)} async-done(((bf16[4096,1,768]{2,0,1:T(8,128)(2,1)}), bf16[1024,1,768]{2,0,1:T(8,128)(2,1)}) %reduce-scatter.9.cloned.1.call-update) | async-done | bytes 1572880 | tf_op jit(solution)/shard_map/reduce_scatter | solution.py:387
  673.8 4.3 fusion.22
  678.2 5.1 fusion.49
  683.2 52.0 %reduce-scatter.11.cloned.1.call-done = bf16[1024,1,768]{2,0,1:T(8,128)(2,1)} async-done(((bf16[4096,1,768]{2,0,1:T(8,128)(2,1)}), bf16[1024,1,768]{2,0,1:T(8,128)(2,1)}) %reduce-scatter.11.cloned.1.call-update) | async-done | bytes 1572880 | tf_op jit(solution)/shard_map/reduce_scatter | solution.py:393
  735.2 4.3 fusion.25
  739.6 3.3 fusion.20
  743.0 2.6 fusion.28
  746.2 3.3 reduce.8
  752.0 5.6 all-to-all-start.1
  758.4 56.1 %reduce-scatter.13.cloned.1.call-done = bf16[96,768]{1,0:T(8,128)(2,1)} async-done(((bf16[768,768]{1,0:T(8,128)(2,1)}), bf16[96,768]{1,0:T(8,128)(2,1)}) %reduce-scatter.13.cloned.1.call-update) | async-done | bytes 147472 | tf_op jit(solution)/shard_map/reduce_scatter | solution.py:435
  814.5 67.2 %reduce-scatter.19.cloned.1.call-done = bf16[96,768]{1,0:T(8,128)(2,1)} async-done(((bf16[768,768]{1,0:T(8,128)(2,1)}), bf16[96,768]{1,0:T(8,128)(2,1)}) %reduce-scatter.19.cloned.1.call-update) | async-done | bytes 147472 | tf_op jit(solution)/shard_map/reduce_scatter | solution.py:440
  881.7 101.0 %reduce-scatter.21.cloned.1.call-done = bf16[96,3072]{1,0:T(8,128)(2,1)} async-done(((bf16[768,3072]{1,0:T(8,128)(2,1)}), bf16[96,3072]{1,0:T(8,128)(2,1)}) %reduce-scatter.21.cloned.1.call-update) | async-done | bytes 589840 | tf_op jit(solution)/shard_map/reduce_scatter | solution.py:360
  982.8 99.0 %reduce-scatter.23.cloned.1.call-done = bf16[384,768]{1,0:T(8,128)(2,1)} async-done(((bf16[3072,768]{1,0:T(8,128)(2,1)}), bf16[384,768]{1,0:T(8,128)(2,1)}) %reduce-scatter.23.cloned.1.call-update) | async-done | bytes 589840 | tf_op jit(solution)/shard_map/reduce_scatter | solution.py:361
  1081.7 65.6 %reduce-scatter.15.cloned.1.call-done = bf16[96,768]{1,0:T(8,128)(2,1)} async-done(((bf16[768,768]{1,0:T(8,128)(2,1)}), bf16[96,768]{1,0:T(8,128)(2,1)}) %reduce-scatter.15.cloned.1.call-update) | async-done | bytes 147472 | tf_op jit(solution)/shard_map/reduce_scatter | solution.py:437
  1147.3 67.7 %reduce-scatter.17.cloned.1.call-done = bf16[96,768]{1,0:T(8,128)(2,1)} async-done(((bf16[768,768]{1,0:T(8,128)(2,1)}), bf16[96,768]{1,0:T(8,128)(2,1)}) %reduce-scatter.17.cloned.1.call-update) | async-done | bytes 147472 | tf_op jit(solution)/shard_map/reduce_scatter | solution.py:438
  1221.9 25.7 %all-reduce.17 = (bf16[768]{0:T(1024)(128)(2,1)S(1)}, bf16[768]{0:T(1024)(128)(2,1)S(1)}, bf16[768]{0:T(1024)(128)(2,1)S(1)}, bf16[768]{0:T(1024)(128)(2,1)S(1)}...) all-reduce(bf16[768]{0:T(1024)(128)(2,1)S(1)} %dynamic-update-slice, ...), channel_id=1, replica_groups=mesh['ctx'=4,'fsdp'=8] {'fsdp'}, use_global_device_ids=true, to_apply=%add.7 | all-reduce | flops 9984 | bytes 39936
  1248.3 15.0 %all-reduce.19 = (bf16[96]{0:T(256)(128)(2,1)S(1)}, bf16[96]{0:T(256)(128)(2,1)S(1)}, bf16[96]{0:T(256)(128)(2,1)S(1)}, bf16[96]{0:T(256)(128)(2,1)S(1)}, bf16[9...) all-reduce(bf16[96]{0:T(256)(128)(2,1)S(1)} %dynamic-slice.15, ...), channel_id=1, replica_groups=mesh['ctx'=4,'fsdp'=8] {'ctx'}, use_global_device_ids=true, to_apply=%region_15.17 | all-reduce | flops 1152 | bytes 4608 | tf_op jit(solution)/shard_map/psum | solution.py:447
  1269.7 2.6 copy.82
  1272.2 4.7 reshape.297
  1282.7 2.2 convert_element_type.211
  1284.9 2.2 convert_element_type.214
  (221 shorter events, 43.8 us)
Async XLA Ops:
  7.2 78.6 %all-gather.11.cloned.1.call-start = ((), (), s32[]{:S(2)}) async-start(), calls=%async_computation.11 | async-start | bytes 1327104 | tf_op jit(solution)/shard_map/all_gather | solution.py:284
  7.9 100.0 %all-gather.13.cloned.1.call-start = ((), (), s32[]{:S(2)}) async-start(), calls=%async_computation.12 | async-start | bytes 1327104 | tf_op jit(solution)/shard_map/all_gather | solution.py:285
  15.3 7.7 copy-start.30
  15.3 9.0 copy-start.34
  15.3 9.2 copy-start.35
  15.3 9.5 copy-start.36
  15.3 9.7 copy-start.37
  15.3 9.9 copy-start.38
  15.3 10.1 copy-start.39
  15.4 10.4 copy-start.40
  16.8 69.0 %all-to-all-start = ((bf16[128,8,768]{2,0,1:T(8,128)(2,1)}), bf16[128,8,768]{2,0,1:T(8,128)(2,1)S(1)}, u32[]{:S(2)}, u32[]{:S(2)}) async-start(bf16[128,8,768]{2,0,1:T(8,128)(2,1)} %copy.71), calls=%async_computation | async-start | bytes 3145728 | tf_op jit(solution)/shard_map/all_to_all | solution.py:277
  22.2 127.9 %all-gather.9.cloned.1.call-start = ((), (), s32[]{:S(2)}) async-start(), calls=%async_computation.10 | async-start | bytes 1327104 | tf_op jit(solution)/shard_map/all_gather | solution.py:283
  23.0 213.7 %all-gather.15.cloned.1.call-start = ((), (), s32[]{:S(2)}) async-start(), calls=%async_computation.13 | async-start | bytes 15728640 | tf_op jit(solution)/shard_map/all_gather | solution.py:307
  85.8 24.8 %copy-start.5 = (bf16[128,8,768]{2,0,1:T(8,128)(2,1)}, bf16[128,8,768]{2,0,1:T(8,128)(2,1)S(1)}, u32[]{:S(2)}) copy-start(bf16[128,8,768]{2,0,1:T(8,128)(2,1)S(1)} %all-to-all-done) | copy-start | bytes 4718596
  112.5 24.3 %copy-start.4 = (bf16[1024,1,768]{2,0,1:T(8,128)(2,1)S(1)}, bf16[1024,1,768]{2,0,1:T(8,128)(2,1)}, u32[]{:S(2)}) copy-start(bf16[1024,1,768]{2,0,1:T(8,128)(2,1)} %param.39) | copy-start | bytes 4718596
  112.5 25.1 %copy-start.42 = (s32[8]{0:T(128)S(1)}, s32[8]{0:T(128)}, u32[]{:S(2)}) copy-start(s32[8]{0:T(128)} %param.22) | copy-start | bytes 100
  112.5 193.8 %all-gather.17.cloned.1.call-start = ((), (), s32[]{:S(2)}) async-start(), calls=%async_computation.14 | async-start | bytes 1327104 | tf_op jit(solution)/shard_map/all_gather | solution.py:286
  113.1 243.9 %all-gather.19.cloned.1.call-start = ((), (), s32[]{:S(2)}) async-start(), calls=%async_computation.15 | async-start | bytes 5308416 | tf_op jit(solution)/shard_map/all_gather | solution.py:322
  113.7 323.2 %all-gather.21.cloned.1.call-start = ((), (), s32[]{:S(2)}) async-start(), calls=%async_computation.16 | async-start | bytes 5308416 | tf_op jit(solution)/shard_map/all_gather | solution.py:323
  114.4 559.3 %reduce-scatter.9.cloned.1.call-start = ((), (), s32[]{:S(2)}) async-start(), calls=%async_computation.17 | async-start | bytes 7864320 | tf_op jit(solution)/shard_map/reduce_scatter | solution.py:387
  115.8 321.1 %copy-start.26 = (f32[768]{0:T(1024)}, f32[768]{0:T(1024)S(1)}, u32[]{:S(2)}) copy-start(f32[768]{0:T(1024)S(1)} %convert_element_type.178) | copy-start | bytes 9220
  136.8 326.9 %copy-start.18 = (f32[768]{0:T(1024)}, f32[768]{0:T(1024)S(1)}, u32[]{:S(2)}) copy-start(f32[768]{0:T(1024)S(1)} %convert_element_type.183) | copy-start | bytes 9220
  137.5 12.6 copy-start.6
  236.7 69.6 %copy-start.9 = (bf16[1024,768]{0,1:T(8,128)(2,1)S(1)}, bf16[1024,768]{0,1:T(8,128)(2,1)}, u32[]{:S(2)}) copy-start(bf16[1024,768]{0,1:T(8,128)(2,1)} %copy.91) | copy-start | bytes 4718596
  446.3 17.3 %copy-start.2 = (f32[1024,768]{0,1:T(8,128)}, f32[1024,768]{0,1:T(8,128)S(1)}, u32[]{:S(2)}) copy-start(f32[1024,768]{0,1:T(8,128)S(1)} %get-tuple-element.168) | copy-start | bytes 9437188
  446.3 17.3 %copy-start.16 = (f32[1024]{0:T(1024)}, f32[1024]{0:T(1024)S(1)}, u32[]{:S(2)}) copy-start(f32[1024]{0:T(1024)S(1)} %broadcast_multiply_fusion.4) | copy-start | bytes 12292
  446.7 16.9 %copy-start.20 = (f32[1024]{0:T(1024)}, f32[1024]{0:T(1024)S(1)}, u32[]{:S(2)}) copy-start(f32[1024]{0:T(1024)S(1)} %add_rsqrt_fusion) | copy-start | bytes 12292
  448.7 15.0 %slice-start = ((s8[4718592]{0:T(1024)(128)(4,1)}), s8[4194304]{0:T(1024)(128)(4,1)S(1)}, s32[]{:S(2)}) async-start(s8[4718592]{0:T(1024)(128)(4,1)} %bitcast.100), calls=%async_computation.26 | async-start | bytes 8388608
  450.5 13.1 %copy-start.10 = (bf16[1024,768]{0,1:T(8,128)(2,1)}, bf16[1024,768]{0,1:T(8,128)(2,1)S(1)}, u32[]{:S(2)}) copy-start(bf16[1024,768]{0,1:T(8,128)(2,1)S(1)} %get-tuple-element.158) | copy-start | bytes 4718596
  450.5 13.1 %slice-start.1 = ((s8[4718592]{0:T(1024)(128)(4,1)}), s8[524288]{0:T(1024)(128)(4,1)S(1)}, s32[]{:S(2)}) async-start(s8[4718592]{0:T(1024)(128)(4,1)} %bitcast.100), calls=%async_computation.27 | async-start | bytes 1048576
  463.6 11.5 copy-start.44
  614.0 121.2 %reduce-scatter.11.cloned.1.call-start = ((), (), s32[]{:S(2)}) async-start(), calls=%async_computation.18 | async-start | bytes 7864320 | tf_op jit(solution)/shard_map/reduce_scatter | solution.py:393
  614.7 199.8 %reduce-scatter.13.cloned.1.call-start = ((), (), s32[]{:S(2)}) async-start(), calls=%async_computation.19 | async-start | bytes 1327104 | tf_op jit(solution)/shard_map/reduce_scatter | solution.py:435
  619.2 262.6 %reduce-scatter.19.cloned.1.call-start = ((), (), s32[]{:S(2)}) async-start(), calls=%async_computation.22 | async-start | bytes 1327104 | tf_op jit(solution)/shard_map/reduce_scatter | solution.py:440
  623.7 359.1 %reduce-scatter.21.cloned.1.call-start = ((), (), s32[]{:S(2)}) async-start(), calls=%async_computation.23 | async-start | bytes 5308416 | tf_op jit(solution)/shard_map/reduce_scatter | solution.py:360
  635.2 446.5 %reduce-scatter.23.cloned.1.call-start = ((), (), s32[]{:S(2)}) async-start(), calls=%async_computation.24 | async-start | bytes 5308416 | tf_op jit(solution)/shard_map/reduce_scatter | solution.py:361
  645.5 501.8 %reduce-scatter.15.cloned.1.call-start = ((), (), s32[]{:S(2)}) async-start(), calls=%async_computation.20 | async-start | bytes 1327104 | tf_op jit(solution)/shard_map/reduce_scatter | solution.py:437
  678.1 536.8 %reduce-scatter.17.cloned.1.call-start = ((), (), s32[]{:S(2)}) async-start(), calls=%async_computation.21 | async-start | bytes 1327104 | tf_op jit(solution)/shard_map/reduce_scatter | solution.py:438
  752.0 466.2 %copy-start.43 = (bf16[96]{0:T(256)(128)(2,1)S(1)}, bf16[96]{0:T(256)(128)(2,1)}, u32[]{:S(2)}) copy-start(bf16[96]{0:T(256)(128)(2,1)} %param.38) | copy-start | bytes 580
  752.0 520.2 %all-to-all-start.1 = ((bf16[8,2,49152]{2,1,0:T(2,128)(2,1)}), bf16[8,2,49152]{2,1,0:T(2,128)(2,1)}, u32[]{:S(2)}, u32[]{:S(2)}) async-start(bf16[8,2,49152]{2,1,0:T(2,128)(2,1)} %reshape.296), calls=%async_computation.3 | async-start | bytes 3145728 | tf_op jit(solution)/shard_map/all_to_all | solution.py:417
  757.6 525.0 %all-reduce.23.cloned.1.call-start = ((), (), s32[]{:S(2)}) async-start(), calls=%async_computation.25 | async-start | bytes 3538944 | tf_op jit(solution)/shard_map/psum | solution.py:446
  1215.0 6.9 copy-start.28
  1215.0 6.9 copy-start.29
  1215.0 53.0 %copy-start.3 = (f32[1024,768]{0,1:T(8,128)S(1)}, f32[1024,768]{0,1:T(8,128)}, u32[]{:S(2)}) copy-start(f32[1024,768]{0,1:T(8,128)} %copy-done.2) | copy-start | bytes 9437188
  1215.0 53.0 %copy-start.17 = (f32[1024]{0:T(1024)S(1)}, f32[1024]{0:T(1024)}, u32[]{:S(2)}) copy-start(f32[1024]{0:T(1024)} %copy-done.16) | copy-start | bytes 12292
  1215.0 53.0 %copy-start.19 = (f32[768]{0:T(1024)S(1)}, f32[768]{0:T(1024)}, u32[]{:S(2)}) copy-start(f32[768]{0:T(1024)} %copy-done.18) | copy-start | bytes 9220
  1215.0 53.0 %copy-start.21 = (f32[1024]{0:T(1024)S(1)}, f32[1024]{0:T(1024)}, u32[]{:S(2)}) copy-start(f32[1024]{0:T(1024)} %copy-done.20) | copy-start | bytes 12292
  1280.6 9.4 copy-start.1
  (19 other events, 85.0 us)
Sparse Core Ops, SparseCore 0:
  10.2 56.0 all-gather.10
  68.5 39.3 all-gather.12
  110.1 39.9 all-gather.8
  151.5 85.0 all-gather.14
  238.7 36.7 all-gather.16
  277.5 79.4 all-gather.18
  359.2 77.6 all-gather.20
  614.1 59.5 reduce-scatter.8
  676.3 58.8 reduce-scatter.10
  739.0 75.4 reduce-scatter.12
  817.9 63.7 reduce-scatter.18
  885.2 97.4 reduce-scatter.20
  986.4 95.2 reduce-scatter.22
  1085.6 61.6 reduce-scatter.14
  1151.1 63.7 reduce-scatter.16
  1217.6 49.1 all-reduce.22

commit v2 on v1

v2 whole, which is shorter than its diff:
```python
import functools

import jax
import jax.numpy as jnp
from jax import lax
from jax.experimental import pallas as pl
from jax.experimental.pallas import tpu as pltpu
from jax.sharding import PartitionSpec as P

SCALE = 64 ** (-0.5)
LOG2E = 1.4426950408889634
FORWARD_KEYS = 2048
BACKWARD_KEYS = 1024
VMEM_BYTES = 60 * 2**20

NORM_EPSILON = 1e-12
NEG_BIG = -1e30
ROOT_HALF = 0.7071067811865476
ROOT_TWO_PI = 2.5066282746310002


def norm_forward(source, gain_vec, shift_vec):
    centre = source - jnp.mean(source, axis=-1, keepdims=True)
    inv_scale = lax.rsqrt(jnp.mean(centre * centre, axis=-1, keepdims=True) + NORM_EPSILON)
    unit_rows = centre * inv_scale
    return (unit_rows * gain_vec + shift_vec, unit_rows, inv_scale)


def norm_backward(upstream, unit_rows, inv_scale, gain_vec):
    scaled = upstream * gain_vec
    plain_mean = jnp.mean(scaled, axis=-1, keepdims=True)
    cross_mean = jnp.mean(scaled * unit_rows, axis=-1, keepdims=True)
    d_source = inv_scale * (scaled - plain_mean - unit_rows * cross_mean)
    return (d_source, jnp.sum(upstream * unit_rows, axis=0), jnp.sum(upstream, axis=0))


def gelu_exact(source):
    return 0.5 * source * (1.0 + jax.scipy.special.erf(source * ROOT_HALF))


def gelu_slope(source):
    return (
        0.5 * (1.0 + jax.scipy.special.erf(source * ROOT_HALF))
        + source * jnp.exp(-0.5 * source * source) / ROOT_TWO_PI
    )


def product(left, right, dims):
    return lax.dot_general(left, right, (dims, ((), ())), preferred_element_type=jnp.float32)


def lane_is_low():
    return lax.broadcasted_iota(jnp.int32, (1, 128), 1) < 64


def split_query(query_pair, low_half):
    scaled = query_pair * (SCALE * LOG2E)
    high = scaled.astype(jnp.bfloat16).astype(jnp.float32)
    rest = pltpu.roll(scaled - high, 64, 1)
    return (
        jnp.where(low_half, high, rest).astype(jnp.bfloat16),
        jnp.where(low_half, rest, high).astype(jnp.bfloat16),
    )


def twice(pair, low_half):
    other = pltpu.roll(pair, 64, 1)
    return (
        jnp.where(low_half, pair, other).astype(jnp.bfloat16),
        jnp.where(low_half, other, pair).astype(jnp.bfloat16),
    )


def forward_kernel(limit_ref, query_ref, key_ref, value_ref, attended_ref, lse_ref, *, key_rows):
    low_half = lane_is_low()
    limit = limit_ref[0]
    queries = split_query(query_ref[...].astype(jnp.float32), low_half)
    query_rows = query_ref.shape[0]

    def step(tile, state):
        start = pl.multiple_of(tile * key_rows, key_rows)
        usable = start + lax.broadcasted_iota(jnp.int32, (key_rows, 1), 0) < limit
        key_tile = key_ref[pl.ds(start, key_rows), :].astype(jnp.float32)
        keys = twice(jnp.where(usable, key_tile, key_ref[0:1, :].astype(jnp.float32)), low_half)
        value_tile = value_ref[pl.ds(start, key_rows), :].astype(jnp.float32)
        value_tile = jnp.where(usable, value_tile, 0.0)
        count = jnp.where(usable, 1.0, 0.0)
        values = (
            jnp.where(low_half, value_tile, count).astype(jnp.bfloat16),
            jnp.where(low_half, count, value_tile).astype(jnp.bfloat16),
        )
        fresh = []
        for head in range(2):
            top, total = state[head]
            scores = product(queries[head], keys[head], ((1,), (1,)))
            new_top = jnp.maximum(top, jnp.max(scores, axis=1, keepdims=True))
            weights = jnp.exp2(scores - new_top).astype(jnp.bfloat16)
            total = total * jnp.exp2(top - new_top) + product(weights, values[head], ((1,), (0,)))
            fresh.append((new_top, total))
        return tuple(fresh)

    empty = (
        jnp.full((query_rows, 1), NEG_BIG, jnp.float32),
        jnp.zeros((query_rows, 128), jnp.float32),
    )
    (top_a, total_a), (top_b, total_b) = lax.fori_loop(
        0, key_ref.shape[0] // key_rows, step, (empty, empty)
    )
    mass_a, mass_b = total_a[:, 64:65], total_b[:, 0:1]
    attended_ref[...] = jnp.where(low_half, total_a / mass_a, total_b / mass_b)
    lse = jnp.where(low_half, top_a + jnp.log2(mass_a), top_b + jnp.log2(mass_b)).T
    lse_ref[0, 0:1, :] = lse[0:1, :]
    lse_ref[0, 1:2, :] = lse[64:65, :]


def backward_kernel(
    limit_ref,
    query_ref,
    key_ref,
    value_ref,
    grad_ref,
    attended_ref,
    lse_ref,
    d_query_ref,
    d_key_ref,
    d_value_ref,
    query_sum,
    *,
    key_rows,
):
    low_half = lane_is_low()
    high_half = jnp.logical_not(low_half)
    lane = lax.broadcasted_iota(jnp.int32, (1, 128), 1)
    limit = limit_ref[0]
    query_pair = query_ref[...].astype(jnp.float32)
    queries = split_query(query_pair, low_half)
    scaled = query_pair * SCALE
    grad_pair = grad_ref[...].astype(jnp.float32)
    overlap = grad_pair * attended_ref[...]
    own_query, own_grad, joined_grad = [], [], []
    for head in range(2):
        mine = low_half if head == 0 else high_half
        own_query.append(jnp.where(mine, scaled, 0.0).astype(jnp.bfloat16))
        own_grad.append(jnp.where(mine, grad_pair, 0.0).astype(jnp.bfloat16))
        delta = -jnp.sum(jnp.where(mine, overlap, 0.0), axis=1, keepdims=True)
        first = delta.astype(jnp.bfloat16).astype(jnp.float32)
        second = (delta - first).astype(jnp.bfloat16).astype(jnp.float32)
        third = delta - first - second
        spare = 64 * (1 - head)
        joined = jnp.where(lane == spare + 2, third, 0.0)
        joined = jnp.where(lane == spare + 1, second, joined)
        joined = jnp.where(lane == spare, first, joined)
        joined_grad.append(jnp.where(mine, grad_pair, joined).astype(jnp.bfloat16))
    query_sum[...] = jnp.zeros_like(query_sum)

    def step(tile, carry):
        start = pl.multiple_of(tile * key_rows, key_rows)
        usable = start + lax.broadcasted_iota(jnp.int32, (key_rows, 1), 0) < limit
        key_tile = key_ref[pl.ds(start, key_rows), :].astype(jnp.float32)
        value_tile = value_ref[pl.ds(start, key_rows), :].astype(jnp.float32)
        keys = twice(jnp.where(usable, key_tile, key_ref[0:1, :].astype(jnp.float32)), low_half)
        own_tile = jnp.where(usable, key_tile * SCALE, 0.0)
        key_piece = value_piece = None
        for head in range(2):
            mine = low_half if head == 0 else high_half
            values = jnp.where(mine, value_tile, 1.0).astype(jnp.bfloat16)
            own_key = jnp.where(mine, own_tile, 0.0).astype(jnp.bfloat16)
            scores = product(keys[head], queries[head], ((1,), (1,)))
            probs = jnp.exp2(scores - lse_ref[0, head : head + 1, :])
            slopes = product(values, joined_grad[head], ((1,), (1,)))
            score_grads = (probs * slopes).astype(jnp.bfloat16)
            value_term = product(probs.astype(jnp.bfloat16), own_grad[head], ((1,), (0,)))
            key_term = product(score_grads, own_query[head], ((1,), (0,)))
            value_piece = value_term if value_piece is None else value_piece + value_term
            key_piece = key_term if key_piece is None else key_piece + key_term
            query_sum[...] += product(own_key, score_grads, ((0,), (0,)))
        d_value_ref[pl.ds(start, key_rows), :] = jnp.where(usable, value_piece, 0.0).astype(
            jnp.bfloat16
        )
        d_key_ref[pl.ds(start, key_rows), :] = jnp.where(usable, key_piece, 0.0).astype(
            jnp.bfloat16
        )
        return carry

    lax.fori_loop(0, key_ref.shape[0] // key_rows, step, 0)
    d_query_ref[...] = query_sum[...].T.astype(jnp.bfloat16)


def attend_forward(queries, keys, values, limit):
    rows, width = queries.shape
    full = keys.shape[0]
    pairs = width // 128
    row_spec = pl.BlockSpec((rows, 128), lambda pair, *_: (0, pair))
    return pl.pallas_call(
        functools.partial(forward_kernel, key_rows=FORWARD_KEYS),
        grid_spec=pltpu.PrefetchScalarGridSpec(
            num_scalar_prefetch=1,
            grid=(pairs,),
            in_specs=[
                row_spec,
                pl.BlockSpec((full, 128), lambda pair, *_: (0, pair)),
                pl.BlockSpec((full, 128), lambda pair, *_: (0, pair)),
            ],
            out_specs=[row_spec, pl.BlockSpec((1, 2, rows), lambda pair, *_: (pair, 0, 0))],
        ),
        out_shape=[
            jax.ShapeDtypeStruct((rows, width), jnp.float32),
            jax.ShapeDtypeStruct((pairs, 2, rows), jnp.float32),
        ],
        compiler_params=pltpu.CompilerParams(vmem_limit_bytes=VMEM_BYTES),
        cost_estimate=pl.CostEstimate(
            flops=16 * rows * full * width, bytes_accessed=20_000_000, transcendentals=0
        ),
        name="attend_forward",
    )(limit, queries, keys, values)


def attend_backward(queries, keys, values, limit, grad_rows, attended, lse):
    rows, width = queries.shape
    full = keys.shape[0]
    pairs = width // 128
    row_spec = pl.BlockSpec((rows, 128), lambda pair, *_: (0, pair))
    key_spec = pl.BlockSpec((full, 128), lambda pair, *_: (0, pair))
    return pl.pallas_call(
        functools.partial(backward_kernel, key_rows=BACKWARD_KEYS),
        grid_spec=pltpu.PrefetchScalarGridSpec(
            num_scalar_prefetch=1,
            grid=(pairs,),
            in_specs=[
                row_spec,
                key_spec,
                pl.BlockSpec((full, 128), lambda pair, *_: (0, pair)),
                row_spec,
                row_spec,
                pl.BlockSpec((1, 2, rows), lambda pair, *_: (pair, 0, 0)),
            ],
            out_specs=[row_spec, key_spec, key_spec],
            scratch_shapes=[pltpu.VMEM((128, rows), jnp.float32)],
        ),
        out_shape=[
            jax.ShapeDtypeStruct((rows, width), jnp.bfloat16),
            jax.ShapeDtypeStruct((full, width), jnp.bfloat16),
            jax.ShapeDtypeStruct((full, width), jnp.bfloat16),
        ],
        compiler_params=pltpu.CompilerParams(vmem_limit_bytes=VMEM_BYTES),
        cost_estimate=pl.CostEstimate(
            flops=40 * rows * full * width, bytes_accessed=40_000_000, transcendentals=0
        ),
        name="attend_backward",
    )(limit, queries, keys, values, grad_rows, attended, lse)


MESH = pl.DeviceIdType.MESH
DMA = pltpu.SemaphoreType.DMA
ANY = pl.BlockSpec(memory_space=pl.ANY)
STAGES = ("start", "after_core", "after_across", "after_group", "finish")


def places():
    ctx, group = lax.axis_index("ctx"), lax.axis_index("fsdp")
    return ctx, group, lax.rem(ctx + 2, 4), ctx + 1 - 2 * lax.rem(ctx, 2)


def remote(source, target, send_sem, recv_sem, where):
    return pltpu.make_async_remote_copy(
        src_ref=source,
        dst_ref=target,
        send_sem=send_sem,
        recv_sem=recv_sem,
        device_id=where,
        device_id_type=MESH,
    )


def greet(count):
    ctx, group, _, _ = places()
    barrier = pltpu.get_barrier_semaphore()

    def one(step, carry):
        pl.semaphore_signal(
            barrier,
            inc=1,
            device_id={"fsdp": lax.rem(group + step, count)},
            device_id_type=MESH,
        )
        return carry

    lax.fori_loop(1, count, one, 0)
    for other in range(1, 4):
        pl.semaphore_signal(
            barrier, inc=1, device_id={"ctx": lax.rem(ctx + other, 4)}, device_id_type=MESH
        )
    pl.semaphore_wait(barrier, count - 1 + 3)


def arrival_kernel(
    placed,
    weights,
    small,
    tokens,
    gathered,
    small_all,
    tok_stage,
    w_stage,
    small_stage,
    local_sem,
    tok_send,
    tok_recv,
    w_send,
    w_recv,
    small_send,
    small_recv,
    x_send,
    x_recv,
    s_send,
    s_recv,
    r_send,
    r_recv,
    *,
    count,
):
    ctx, group, across, sibling = places()
    own_tok = pltpu.make_async_copy(placed.at[group], tok_stage, local_sem.at[0])
    own_w = pltpu.make_async_copy(weights.at[ctx], w_stage, local_sem.at[1])
    own_small = pltpu.make_async_copy(small, small_stage, local_sem.at[2])
    own_tok.start()
    own_w.start()
    own_small.start()
    greet(count)

    def tok_copy(peer, step):
        return remote(
            placed.at[peer],
            tokens.at[ctx, group],
            tok_send.at[step],
            tok_recv.at[step],
            {"fsdp": peer},
        )

    def w_copy(peer, step):
        return remote(
            weights.at[ctx],
            gathered.at[ctx, group],
            w_send.at[step],
            w_recv.at[step],
            {"fsdp": peer},
        )

    def small_copy(peer, step):
        return remote(
            small, small_all.at[group], small_send.at[step], small_recv.at[step], {"fsdp": peer}
        )

    def send(step, carry):
        peer = lax.rem(group + step, count)
        w_copy(peer, step).start()
        tok_copy(peer, step).start()
        small_copy(peer, step).start()
        return carry

    lax.fori_loop(1, count, send, 0)
    own_tok.wait()
    own_w.wait()
    own_small.wait()
    put_tok = pltpu.make_async_copy(tok_stage, tokens.at[ctx, group], local_sem.at[0])
    put_w = pltpu.make_async_copy(w_stage, gathered.at[ctx, group], local_sem.at[1])
    put_small = pltpu.make_async_copy(small_stage, small_all.at[group], local_sem.at[2])
    put_tok.start()
    put_w.start()
    put_small.start()

    def across_copy(kind, block):
        where = gathered if kind == 0 else tokens
        return remote(
            where.at[ctx, block],
            where.at[ctx, block],
            x_send.at[kind, block],
            x_recv.at[kind, block],
            {"ctx": across},
        )

    def sibling_copy(kind, block):
        where = gathered if kind == 0 else tokens
        return remote(
            where.at[ctx, block],
            where.at[ctx, block],
            s_send.at[kind, block],
            s_recv.at[kind, block],
            {"ctx": sibling},
        )

    def relay_copy(kind, block):
        where = gathered if kind == 0 else tokens
        return remote(
            where.at[across, block],
            where.at[across, block],
            r_send.at[kind, block],
            r_recv.at[kind, block],
            {"ctx": sibling},
        )

    put_w.wait()
    across_copy(0, group).start()
    sibling_copy(0, group).start()
    put_tok.wait()
    across_copy(1, group).start()
    sibling_copy(1, group).start()
    put_small.wait()

    def arrive(step, carry):
        origin = lax.rem(group - step + count, count)
        w_copy(origin, step).wait_recv()
        across_copy(0, origin).start()
        sibling_copy(0, origin).start()
        tok_copy(origin, step).wait_recv()
        across_copy(1, origin).start()
        sibling_copy(1, origin).start()
        return carry

    lax.fori_loop(1, count, arrive, 0)

    def passed(step, carry):
        origin = lax.rem(group - step + count, count)
        for kind in range(2):
            across_copy(kind, origin).wait_recv()
            relay_copy(kind, origin).start()
        return carry

    lax.fori_loop(0, count, passed, 0)

    def finish(step, carry):
        origin = lax.rem(group - step + count, count)
        for kind in range(2):
            across_copy(kind, origin).wait_send()
            sibling_copy(kind, origin).wait()
            relay_copy(kind, origin).wait()
        return carry

    lax.fori_loop(0, count, finish, 0)

    def sent(step, carry):
        peer = lax.rem(group + step, count)
        w_copy(peer, step).wait_send()
        tok_copy(peer, step).wait_send()
        small_copy(peer, step).wait()
        return carry

    lax.fori_loop(1, count, sent, 0)


def bring_in(placed, weights, small):
    count, rows, width = placed.shape
    return pl.pallas_call(
        functools.partial(arrival_kernel, count=count),
        in_specs=[ANY] * 3,
        out_specs=[ANY] * 3,
        out_shape=[
            jax.ShapeDtypeStruct((4, count, rows, width), jnp.bfloat16),
            jax.ShapeDtypeStruct((4, count) + weights.shape[1:], jnp.bfloat16),
            jax.ShapeDtypeStruct((count,) + small.shape, jnp.bfloat16),
        ],
        scratch_shapes=[
            pltpu.VMEM((rows, width), jnp.bfloat16),
            pltpu.VMEM(weights.shape[1:], jnp.bfloat16),
            pltpu.VMEM(small.shape, jnp.bfloat16),
            DMA((3,)),
        ]
        + [DMA((count,))] * 6
        + [DMA((2, count))] * 6,
        compiler_params=pltpu.CompilerParams(
            collective_id=0, has_side_effects=True, vmem_limit_bytes=8 * 2**20
        ),
        name="bring_in",
    )(placed, weights, small)


class Sum:
    SCRATCH = 16

    def __init__(self, kind, ref, out, scratch, count):
        self.kind, self.ref, self.out, self.count = kind, ref, out, count
        self.near, self.far, self.got_near, self.got_far = scratch[:4]
        self.got_across, self.got_group, self.done = scratch[4:7]
        self.load, self.c_send, self.c_recv, self.x_send, self.x_recv = scratch[7:12]
        self.g_send, self.g_recv, self.o_send, self.o_recv = scratch[12:16]
        self.ctx, self.group, self.across, self.sibling = places()
        self.width = self.near.shape[-1]

    @staticmethod
    def scratch(count, rows, width):
        return (
            [pltpu.VMEM((count, rows, width), jnp.bfloat16)] * 6
            + [pltpu.VMEM((rows, width), jnp.bfloat16)]
            + [DMA((2,))] * 3
            + [DMA((count,))] * 4
            + [DMA((4,))] * 2
        )

    def quarter(self, index):
        if self.kind == 0:
            return self.ref.at[index]
        if self.kind == 1:
            start = pl.multiple_of(index * self.width, self.width)
            return self.ref.at[:, :, pl.ds(start, self.width)]
        return self.ref.at[:, index]

    def loads(self):
        return (
            pltpu.make_async_copy(self.quarter(self.across), self.far, self.load.at[0]),
            pltpu.make_async_copy(self.quarter(self.ctx), self.near, self.load.at[1]),
        )

    def cores(self):
        beyond = lax.rem(self.sibling + 2, 4)
        there = {"ctx": self.sibling}
        return (
            remote(self.quarter(beyond), self.got_far, self.c_send.at[0], self.c_recv.at[0], there),
            remote(
                self.quarter(self.sibling),
                self.got_near,
                self.c_send.at[1],
                self.c_recv.at[1],
                there,
            ),
        )

    def x_copy(self, block):
        return remote(
            self.far.at[block],
            self.got_across.at[block],
            self.x_send.at[block],
            self.x_recv.at[block],
            {"ctx": self.across},
        )

    def g_copy(self, peer, step):
        return remote(
            self.near.at[peer],
            self.got_group.at[step],
            self.g_send.at[step],
            self.g_recv.at[step],
            {"fsdp": peer},
        )

    def o_copy(self, other):
        return remote(
            self.done,
            self.out.at[self.ctx],
            self.o_send.at[other],
            self.o_recv.at[other],
            {"ctx": lax.rem(self.ctx + other, 4)},
        )

    def own_out(self):
        return pltpu.make_async_copy(self.done, self.out.at[self.ctx], self.load.at[0])

    def add(self, total, other):
        def one(block, carry):
            both = total[block].astype(jnp.float32) + other[block].astype(jnp.float32)
            total[block] = both.astype(jnp.bfloat16)
            return carry

        lax.fori_loop(0, self.count, one, 0)

    def start(self):
        for copy in self.loads() + self.cores():
            copy.start()

    def after_core(self):
        loads, cores = self.loads(), self.cores()
        loads[0].wait()
        cores[0].wait_recv()
        self.add(self.far, self.got_far)

        def send(step, carry):
            self.x_copy(lax.rem(self.group + 1 + step, self.count)).start()
            return carry

        lax.fori_loop(0, self.count, send, 0)
        loads[1].wait()
        cores[1].wait_recv()
        self.add(self.near, self.got_near)
        cores[0].wait_send()
        cores[1].wait_send()

    def after_across(self):
        def one(step, carry):
            block = lax.rem(self.group + step, self.count)
            self.x_copy(block).wait()
            both = self.near[block].astype(jnp.float32) + self.got_across[block].astype(jnp.float32)
            self.near[block] = both.astype(jnp.bfloat16)
            self.g_copy(block, step).start()
            return carry

        lax.fori_loop(1, self.count, one, 0)
        self.x_copy(self.group).wait()

    def after_group(self):
        group = self.group
        total = self.near[group].astype(jnp.float32) + self.got_across[group].astype(jnp.float32)

        def one(step, total):
            self.g_copy(lax.rem(group + step, self.count), step).wait()
            return total + self.got_group[step].astype(jnp.float32)

        self.done[...] = lax.fori_loop(1, self.count, one, total).astype(jnp.bfloat16)
        self.own_out().start()
        for other in range(1, 4):
            self.o_copy(other).start()

    def finish(self):
        self.own_out().wait()
        for other in range(1, 4):
            self.o_copy(other).wait()


class VectorSum:
    SCRATCH = 9

    def __init__(self, ref, out, scratch, count):
        self.ref, self.out, self.count = ref, out, count
        self.total, self.got_ctx, self.got_group = scratch[:3]
        self.load, self.c_send, self.c_recv, self.g_send, self.g_recv = scratch[3:8]
        self.result = scratch[8]
        self.ctx, self.group, _, _ = places()

    @staticmethod
    def scratch(count, rows, width):
        return [
            pltpu.VMEM((rows, width), jnp.float32),
            pltpu.VMEM((4, rows, width), jnp.float32),
            pltpu.VMEM((count, rows, width), jnp.float32),
            DMA((2,)),
            DMA((4,)),
            DMA((4,)),
            DMA((count,)),
            DMA((count,)),
            pltpu.VMEM((rows, width), jnp.float32),
        ]

    def own(self):
        return pltpu.make_async_copy(self.ref, self.total, self.load.at[0])

    def own_out(self):
        return pltpu.make_async_copy(self.result, self.out, self.load.at[1])

    def c_copy(self, other):
        return remote(
            self.ref,
            self.got_ctx.at[other],
            self.c_send.at[other],
            self.c_recv.at[other],
            {"ctx": lax.rem(self.ctx + other, 4)},
        )

    def g_copy(self, step):
        return remote(
            self.total,
            self.got_group.at[step],
            self.g_send.at[step],
            self.g_recv.at[step],
            {"fsdp": lax.rem(self.group + step, self.count)},
        )

    def start(self):
        self.own().start()
        for other in range(1, 4):
            self.c_copy(other).start()

    def after_core(self):
        self.own().wait()
        total = self.total[...]
        for other in range(1, 4):
            self.c_copy(other).wait()
            total = total + self.got_ctx[other]
        self.total[...] = total

        def one(step, carry):
            self.g_copy(step).start()
            return carry

        lax.fori_loop(1, self.count, one, 0)

    def after_across(self):
        pass

    def after_group(self):
        def one(step, total):
            self.g_copy(step).wait()
            return total + self.got_group[step]

        self.result[...] = lax.fori_loop(1, self.count, one, self.total[...])
        self.own_out().start()

    def finish(self):
        self.own_out().wait()


def sums_kernel(*refs, kinds, count):
    parts = len(kinds)
    ins, outs, rest = refs[: parts + 1], refs[parts + 1 : 2 * parts + 2], refs[2 * parts + 2 :]
    jobs = [VectorSum(ins[parts], outs[parts], rest[: VectorSum.SCRATCH], count)]
    rest = rest[VectorSum.SCRATCH :]
    for index, kind in enumerate(kinds):
        own = rest[index * Sum.SCRATCH : (index + 1) * Sum.SCRATCH]
        jobs.append(Sum(kind, ins[index], outs[index], own, count))
    greet(count)
    for stage in STAGES:
        for job in jobs:
            getattr(job, stage)()


def sum_gradients(parts, kinds, vectors, rows, width, count):
    scratch = VectorSum.scratch(count, *vectors.shape)
    for _ in kinds:
        scratch += Sum.scratch(count, rows, width)
    return pl.pallas_call(
        functools.partial(sums_kernel, kinds=kinds, count=count),
        in_specs=[ANY] * (len(kinds) + 1),
        out_specs=[ANY] * (len(kinds) + 1),
        out_shape=[jax.ShapeDtypeStruct((4, rows, width), jnp.bfloat16)] * len(kinds)
        + [jax.ShapeDtypeStruct(vectors.shape, jnp.float32)],
        scratch_shapes=scratch,
        compiler_params=pltpu.CompilerParams(
            collective_id=1, has_side_effects=True, vmem_limit_bytes=VMEM_BYTES
        ),
        name="sum_gradients",
    )(*parts, vectors)


def on_device(
    hidden_in,
    lengths,
    seq_order,
    query_weight,
    query_bias,
    key_weight,
    value_weight,
    value_bias,
    output_weight,
    output_bias,
    norm1_gain,
    norm1_shift,
    inner_weight,
    inner_bias,
    outer_weight,
    outer_bias,
    norm2_gain,
    norm2_shift,
    cotangent,
):
    width = hidden_in.shape[2]
    count = lax.axis_size("fsdp")
    group = lax.axis_index("fsdp")
    shard = query_bias.shape[0]
    low = jnp.bfloat16
    placed = jnp.swapaxes(jnp.take(hidden_in, seq_order, axis=1), 0, 1)
    vectors = jnp.concatenate(
        (
            jnp.stack(
                (
                    query_bias,
                    value_bias,
                    output_bias,
                    norm1_gain,
                    norm1_shift,
                    outer_bias,
                    norm2_gain,
                    norm2_shift,
                )
            ),
            inner_bias.reshape(4, shard),
        )
    )
    vectors = jnp.pad(vectors, ((0, 4), (0, 128 - shard)))
    weights = jnp.stack((query_weight, key_weight, value_weight, output_weight))
    tokens, weights, vectors = bring_in(placed, weights, vectors)
    w_inner = lax.all_gather(inner_weight, "fsdp", axis=0, tiled=True)
    w_outer = lax.all_gather(outer_weight, "fsdp", axis=0, tiled=True)
    w_query, w_key, w_value, w_output = (weights[i].reshape(width, width) for i in range(4))
    vectors = vectors[:, :12, :shard].astype(jnp.float32)
    b_query, b_value, b_output, gain_one, shift_one, b_outer, gain_two, shift_two = (
        vectors[:, i].reshape(width) for i in range(8)
    )
    b_inner = vectors[:, 8:].reshape(-1)
    limits = jnp.take(lengths, jnp.take(seq_order, group[None]))
    all_rows = tokens.reshape(-1, width)
    local_len = all_rows.shape[0] // 4
    token_rows = lax.dynamic_index_in_dim(tokens, lax.axis_index("ctx"), 0, False)
    token_rows = token_rows.reshape(local_len, width)
    queries = (product(token_rows, w_query, ((1,), (0,))) + b_query).astype(low)
    keys = product(all_rows, w_key, ((1,), (0,))).astype(low)
    values = (product(all_rows, w_value, ((1,), (0,))) + b_value).astype(low)
    attended, lse = attend_forward(queries, keys, values, limits)
    mixed_low = attended.astype(low)
    branch = product(mixed_low, w_output, ((1,), (0,))) + b_output
    normed, unit_one, scale_one = norm_forward(
        token_rows.astype(jnp.float32) + branch, gain_one, shift_one
    )
    normed_low = normed.astype(low)
    inner_pre = product(normed_low, w_inner, ((1,), (0,))) + b_inner
    activated = gelu_exact(inner_pre).astype(low)
    outer_out = product(activated, w_outer, ((1,), (0,))) + b_outer
    second, unit_two, scale_two = norm_forward(normed + outer_out, gain_two, shift_two)
    layer_out = second.astype(low).reshape(local_len, 1, width)
    upstream = cotangent.reshape(local_len, width).astype(jnp.float32)
    d_second, grad_gain_two, grad_shift_two = norm_backward(upstream, unit_two, scale_two, gain_two)
    d_outer = d_second.astype(low)
    grad_outer_w = product(activated, d_outer, ((0,), (0,))).astype(low)
    grad_outer_b = jnp.sum(d_outer.astype(jnp.float32), axis=0)
    inner_grad = product(d_outer, w_outer, ((1,), (1,)))
    d_inner = (inner_grad * gelu_slope(inner_pre)).astype(low)
    grad_inner_w = product(normed_low, d_inner, ((0,), (0,))).astype(low)
    grad_inner_b = jnp.sum(d_inner.astype(jnp.float32), axis=0)
    d_normed = d_second + product(d_inner, w_inner, ((1,), (1,)))
    d_res, grad_gain_one, grad_shift_one = norm_backward(d_normed, unit_one, scale_one, gain_one)
    d_branch = d_res.astype(low)
    grad_output_w = product(mixed_low, d_branch, ((0,), (0,))).astype(low)
    grad_output_b = jnp.sum(d_branch.astype(jnp.float32), axis=0)
    d_mixed = product(d_branch, w_output, ((1,), (1,))).astype(low)
    d_query, key_terms, value_terms = attend_backward(
        queries, keys, values, limits, d_mixed, attended, lse
    )
    d_keys = lax.psum_scatter(key_terms, "ctx", scatter_dimension=0, tiled=True)
    d_values = lax.psum_scatter(value_terms, "ctx", scatter_dimension=0, tiled=True)
    grad_query_w = product(token_rows, d_query, ((0,), (0,))).astype(low)
    grad_query_b = jnp.sum(d_query.astype(jnp.float32), axis=0)
    grad_key_w = product(token_rows, d_keys, ((0,), (0,))).astype(low)
    grad_value_w = product(token_rows, d_values, ((0,), (0,))).astype(low)
    grad_value_b = jnp.sum(d_values.astype(jnp.float32), axis=0)
    d_placed = d_res + product(d_query, w_query, ((1,), (1,)))
    d_placed = d_placed + product(d_keys, w_key, ((1,), (1,)))
    d_placed = d_placed + product(d_values, w_value, ((1,), (1,)))
    back_rows = d_placed.astype(low).reshape(count, local_len // count, width)
    returned = lax.all_to_all(back_rows, "fsdp", split_axis=0, concat_axis=0, tiled=True)
    inverse = jnp.argmax(seq_order[:, None] == jnp.arange(count), axis=0)
    grad_in = jnp.take(jnp.swapaxes(returned, 0, 1), inverse, axis=1)
    attention_w = jnp.stack((grad_query_w, grad_key_w, grad_value_w, grad_output_w))
    small_sums = jnp.concatenate(
        (
            jnp.stack(
                (
                    grad_query_b,
                    grad_value_b,
                    grad_output_b,
                    grad_gain_one,
                    grad_shift_one,
                    grad_outer_b,
                    grad_gain_two,
                    grad_shift_two,
                )
            ),
            grad_inner_b.reshape(4, width),
            jnp.zeros((4, width), jnp.float32),
        )
    )
    attention_w, inner_w, outer_w, small_sums = sum_gradients(
        (
            attention_w.reshape(4, count, shard, width),
            grad_inner_w.reshape(count, shard, 4 * width),
            grad_outer_w.reshape(count, 4, shard, width),
        ),
        (0, 1, 2),
        small_sums,
        shard,
        width,
        count,
    )
    attention_w = attention_w.astype(jnp.float32)
    inner_w = jnp.swapaxes(inner_w, 0, 1).reshape(shard, 4 * width).astype(jnp.float32)
    outer_w = outer_w.reshape(4 * shard, width).astype(jnp.float32)
    small = lax.dynamic_slice_in_dim(small_sums[:8], group * shard, shard, axis=1)
    inner_b = lax.dynamic_slice_in_dim(
        small_sums[8:12].reshape(-1), group * 4 * shard, 4 * shard, axis=0
    )
    return (
        layer_out,
        grad_in,
        attention_w[0],
        small[0],
        attention_w[1],
        attention_w[2],
        small[1],
        attention_w[3],
        small[2],
        small[3],
        small[4],
        inner_w,
        inner_b,
        outer_w,
        small[5],
        small[6],
        small[7],
    )


def solution(mesh):
    placed = (
        P(("ctx", "fsdp"), None, None),
        P(),
        P(),
        P("fsdp", None),
        P("fsdp"),
        P("fsdp", None),
        P("fsdp", None),
        P("fsdp"),
        P("fsdp", None),
        P("fsdp"),
        P("fsdp"),
        P("fsdp"),
        P("fsdp", None),
        P("fsdp"),
        P("fsdp", None),
        P("fsdp"),
        P("fsdp"),
        P("fsdp"),
        P("ctx", "fsdp", None),
    )
    return jax.shard_map(
        on_device,
        mesh=mesh,
        in_specs=placed,
        out_specs=(
            P("ctx", "fsdp", None),
            P(("ctx", "fsdp"), None, None),
            P("fsdp", None),
            P("fsdp"),
            P("fsdp", None),
            P("fsdp", None),
            P("fsdp"),
            P("fsdp", None),
            P("fsdp"),
            P("fsdp"),
            P("fsdp"),
            P("fsdp", None),
            P("fsdp"),
            P("fsdp", None),
            P("fsdp"),
            P("fsdp"),
            P("fsdp"),
        ),
        check_vma=False,
    )
```

time: 1310 us -> 743 us (0.57)
  waiting for transfers between devices: 760 us -> 88.2 us
  Pallas kernels: 202 us -> 454 us
  blocking collectives: 121 us -> 0 us
  other arithmetic: 36.1 us -> 20.2 us
    reduce_scatter x8 -> x2, waiting for transfers between devices: 537 us -> 86.3 us  [the longest x1 56.7 us: on_device(): lax.psum_scatter(value_terms, 'ctx', scatter_dimension=0, tiled=True)]
    pallas_call x0 -> x2, Pallas kernels: none -> 252 us  [the longest x1 136 us: bring_in(): pl.pallas_call(functools.partial(arrival_kernel, count=count), in_specs=[...]
    all_gather x7 -> x2, waiting for transfers between devices: 219 us -> 0.02 us  [the longest x1 0.02 us: on_device(): w_inner = lax.all_gather(inner_weight, 'fsdp', axis=0, tiled=True)]
    unnamed x2 -> x0, blocking collectives: 85.5 us -> none
    all_gather x1 -> x0, blocking collectives: 20.9 us -> none  [on_device(): lax.all_gather(inner_bias, 'fsdp', axis=0, tiled=True)]
    psum x1 -> x0, blocking collectives: 15 us -> none  [on_device(): lax.psum(part_query_b.astype(jnp.bfloat16), 'ctx').astype(jnp.float32)]
  transfers between devices with their start and end apart: 18 -> 5, of which waited for: 13 -> 2; matrix products, arithmetic and copies ran while one was open for 10% -> 14% of each run, Pallas kernels for 5% -> 44%
where the time goes in v2:
time: 743 us; the launch traced here: 738 us
  Pallas kernels  454 us (61%)
  matrix products  125 us (17%)
  waiting for transfers between devices  88.2 us (12%)
  local copies, waits for them, and re-layouts  27.7 us (4%)
  other arithmetic  20.2 us (3%)
  between operations  16.2 us (2%)
    pallas_call x1, Pallas kernels, bring_in(): pl.pallas_call(functools.partial(arrival_kernel, count=count), in_specs=[...  136 us
    pallas_call x1, Pallas kernels, attend_backward(): pl.pallas_call(functools.partial(backward_kernel, key_rows=BACKWARD_KEYS)...  132 us
    dot_general x18, matrix products, product(): lax.dot_general(left, right, (dims, ((), ())), preferred_element_type=jnp...  125 us
    pallas_call x1, Pallas kernels, sum_gradients(): pl.pallas_call(functools.partial(sums_kernel, kinds=kinds, count=count),...  116 us
    pallas_call x1, Pallas kernels, attend_forward(): pl.pallas_call(functools.partial(forward_kernel, key_rows=FORWARD_KEYS),...  69.6 us
    reduce_scatter x1, waiting for transfers between devices, on_device(): lax.psum_scatter(value_terms, 'ctx', scatter_dimension=0, tiled=True)  56.7 us
    reduce_scatter x1, waiting for transfers between devices, on_device(): d_keys = lax.psum_scatter(key_terms, 'ctx', scatter_dimension=0, tiled=True)  29.6 us
  transfers between devices with their start and end apart: 5, of which 2 were waited for; matrix products, arithmetic and copies ran while one was open for 14% of the time, Pallas kernels for 44%

profile of v2, /device:TPU:29, one launch (start us, length us, event | category | flops | bytes accessed | tf_op | source)
XLA Modules:
  0.0 737.6 jit_solution(18113946446289479226)
XLA Ops:
  10.1 0.8 reshape.136
  10.8 5.0 gather_fusion
  17.0 1.1 pad_maximum_fusion.1.weights
  18.0 136.4 %bring_in.1 = (bf16[4,8,128,768]{3,2,1,0:T(8,128)(2,1)S(1)}, bf16[4,8,96,768]{3,2,1,0:T(8,128)(2,1)S(1)}, bf16[8,16,128]{2,1,0:T(8,128)(2,1)S(1)}) custom-call(bf16[8,128,768]{2,1,0:T(8,128)(2,1)S(1)} %copy_select_fusion.placed, bf16[4,96,768]{2,1,0:T(8,128)(2,1)S(1)} %pad_maximum_fusion.1.weights, bf16[16,128]{1,0:T(8,128)(2,1)S(1)} %pad.4.small), custom_call_target="tpu_custom_call" | custom-call | tf_op jit(solution)/shard_map/bring_in/pallas_call | solution.py:453
  154.4 2.7 copy-done.2
  157.2 1.8 fusion.27
  159.0 10.5 %add_convert_fusion.value_ref = bf16[4096,768]{1,0:T(8,128)(2,1)} fusion(f32[768]{0:T(1024)S(1)} %add.143, bf16[4096,768]{1,0:T(8,128)(2,1)} %bitcast.116, bf16[768,768]{1,0:T(8,128)(2,1)S(1)} %bitcast.119), kind=kOutput, calls=%fused_computation.12 | convolution fusion | flops 4838129664 | bytes 13765632 | tf_op jit(solution)/shard_map/dot_general | solution.py:49
  169.6 7.0 convolution_convert_fusion.key_ref
  179.7 1.5 constant_dynamic-slice_fusion.1
  181.2 2.5 add_convert_fusion.3.query_ref
  183.7 69.6 %attend_forward.1 = (f32[1024,768]{1,0:T(8,128)}, f32[6,2,1024]{2,1,0:T(2,128)}) custom-call(s32[1]{0:T(128)S(6)} %select_n.40.limit_ref, bf16[1024,768]{1,0:T(8,128)(2,1)} %add_convert_fusion.3.query_ref, bf16[4096,768]{1,0:T(8,128)(2,1)} %convolution_convert_fusion.key_ref, bf16[4096,768]{1,0:T(8,128)(2,1)} %add_convert_fusion.value_ref), custom_call_target="tpu_custom_call" | custom-call | flops 51539607552 | bytes 20000000 | tf_op jit(solution)/shard_map/attend_forward/pallas_call | solution.py:194
  253.4 3.4 fusion.28
  256.8 1.6 copy-done.6
  259.0 12.4 %multiply_convert_fusion = (bf16[1024,3072]{1,0:T(8,128)(2,1)}, f32[1024,3072]{1,0:T(8,128)}) fusion(f32[3072]{0:T(1024)S(1)} %add.154, bf16[768,3072]{1,0:T(8,128)(2,1)} %all-gather.3.cloned.1.call-done, f32[1024,768]{1,0:T(8,128)} %copy-done.6, f32[768]{0:T(1024)S(1)} %add.151, f32[768]{0:T(1024)S(1)} %mul.132, f32[1024]{0:T(1024)S(1)} %add_rsqrt_fusion.1, ...), kind=kOutput, calls=%fused_computation.10 | convolution fusion | flops 4854644736 | bytes 26765312 | tf_op jit(solution)/shard_map/dot_general | solution.py:49
  271.4 20.5 %fusion.29 = (f32[1024]{0:T(1024)S(1)}, f32[1024,768]{1,0:T(8,128)S(1)}) fusion(f32[768]{0:T(1024)S(1)} %add.158, bf16[1024,3072]{1,0:T(8,128)(2,1)} %get-tuple-element.138, bf16[3072,768]{1,0:T(8,128)(2,1)} %all-gather.5.cloned.1.call-done, f32[768]{0:T(1024)S(1)} %add.151, f32[768]{0:T(1024)S(1)} %mul.132, f32[1024]{0:T(1024)S(1)} %add_rsqrt_fusion.1, ...), kind=kOutput, calls=%fused_computation.107 | convolution fusion | flops 4837342208 | bytes 17323008 | tf_op jit(solution)/shard_map/dot_general | solution.py:49
  292.5 0.9 copy-done.4
  293.4 1.9 fusion.14
  295.3 2.9 convert_reduce_fusion.2
  298.2 13.7 %convert_reduce_fusion = (f32[3072]{0:T(1024)}, bf16[1024,3072]{1,0:T(8,128)(2,1)S(1)}) fusion(f32[1024,3072]{1,0:T(8,128)} %get-tuple-element.139, f32[3072]{0:T(1024)S(1)} %add.154, bf16[3072,768]{1,0:T(8,128)(2,1)S(1)} %copy-done.40, f32[1024,768]{1,0:T(8,128)S(1)} %get-tuple-element.116), kind=kOutput, calls=%fused_computation.9 | convolution fusion | flops 4873516032 | bytes 26763264 | tf_op jit(solution)/shard_map/dot_general | solution.py:49
  312.0 6.0 multiply_reduce_fusion
  318.1 1.1 convert_reduce_fusion.3
  319.2 2.7 convolution_convert_fusion.3.grad_ref
  321.8 132.3 %attend_backward.1 = (bf16[1024,768]{1,0:T(8,128)(2,1)}, bf16[4096,768]{1,0:T(8,128)(2,1)}, bf16[4096,768]{1,0:T(8,128)(2,1)}) custom-call(s32[1]{0:T(128)S(6)} %select_n.40.limit_ref, bf16[1024,768]{1,0:T(8,128)(2,1)} %add_convert_fusion.3.query_ref, bf16[4096,768]{1,0:T(8,128)(2,1)} %convolution_convert_fusion.key_ref, ...), custom_call_target="tpu_custom_call" | custom-call | flops 128849018880 | bytes 40000000 | tf_op jit(solution)/shard_map/attend_backward/pallas_call | solution.py:224
  454.8 0.9 copy-done.5
  455.9 0.8 iota_reduce_fusion
  457.2 4.5 fusion.30
  461.8 2.5 convolution_convert_fusion.4
  464.3 11.8 %convolution_convert_fusion.2 = bf16[768,3072]{1,0:T(8,128)(2,1)} fusion(bf16[1024,3072]{1,0:T(8,128)(2,1)} %copy-done.45, f32[1024,768]{1,0:T(8,128)S(1)} %copy-done.8, f32[768]{0:T(1024)S(1)} %copy-done.31, f32[768]{0:T(1024)S(1)} %mul.132, f32[1024]{0:T(1024)S(1)} %add_rsqrt_fusion.1, f32[1024]{0:T(1024)S(1)} %broadcast_multiply_fusion.5), kind=kOutput, calls=%fused_computation.15 | convolution fusion | flops 4838129664 | bytes 14170112 | tf_op jit(solution)/shard_map/dot_general | solution.py:49
  476.1 7.0 convolution_convert_fusion.1
  483.1 29.6 %reduce-scatter.3.cloned.1.call-done = bf16[1024,768]{1,0:T(8,128)(2,1)} async-done(((bf16[4096,768]{1,0:T(8,128)(2,1)}), bf16[1024,768]{1,0:T(8,128)(2,1)}) %reduce-scatter.3.cloned.1.call-update) | async-done | bytes 1572880 | tf_op jit(solution)/shard_map/reduce_scatter | solution.py:824
  512.7 4.5 fusion.31
  517.2 56.7 %reduce-scatter.5.cloned.1.call-done = bf16[1024,768]{1,0:T(8,128)(2,1)} async-done(((bf16[4096,768]{1,0:T(8,128)(2,1)}), bf16[1024,768]{1,0:T(8,128)(2,1)}) %reduce-scatter.5.cloned.1.call-update) | async-done | bytes 1572880 | tf_op jit(solution)/shard_map/reduce_scatter | solution.py:825
  573.9 6.8 add_convert_fusion.1
  580.8 5.7 all-to-all-start
  586.5 4.5 convolution_convert_fusion.7
  591.2 1.3 concatenate.8.refs_3_
  592.5 3.4 convolution_convert_fusion.6
  596.0 1.5 convolution_convert_fusion.5
  597.6 2.4 pad_maximum_fusion.refs_0_
  600.0 115.8 %sum_gradients.1 = (bf16[4,96,768]{2,1,0:T(8,128)(2,1)}, bf16[4,96,768]{2,1,0:T(8,128)(2,1)}, bf16[4,96,768]{2,1,0:T(8,128)(2,1)}, f32[16,768]{1,0:T(8,128)}) custom-call(bf16[4,8,96,768]{3,2,1,0:T(8,128)(2,1)} %pad_maximum_fusion.refs_0_, bf16[8,96,3072]{2,1,0:T(8,128)(2,1)} %bitcast.121, bf16[8,4,96,768]{3,2,1,0:T(8,128)(2,1)} %bitcast.122, ...), custom_call_target="tpu_custom_call" | custom-call | tf_op jit(solution)/shard_map/sum_gradients/pallas_call | solution.py:717
  717.3 1.2 convert_element_type.128
  718.5 1.2 convert_bitcast_fusion.1
  719.6 1.1 copy.42
  722.0 1.0 slice_bitcast_fusion
  723.1 2.2 bitcast_convert_fusion
  725.2 1.8 gather_fusion.1
  727.0 1.6 select_bitcast_fusion
  728.6 2.0 copy.41
  (160 shorter events, 11.3 us)
Async XLA Ops:
  7.2 3.6 copy-start
  7.2 251.8 %all-gather.3.cloned.1.call-start = ((), (), s32[]{:S(2)}) async-start(), calls=%async_computation.3 | async-start | bytes 5308416 | tf_op jit(solution)/shard_map/all_gather | solution.py:778
  7.9 263.5 %all-gather.5.cloned.1.call-start = ((), (), s32[]{:S(2)}) async-start(), calls=%async_computation.4 | async-start | bytes 5308416 | tf_op jit(solution)/shard_map/all_gather | solution.py:779
  8.7 504.0 %reduce-scatter.3.cloned.1.call-start = ((), (), s32[]{:S(2)}) async-start(), calls=%async_computation.5 | async-start | bytes 7864320 | tf_op jit(solution)/shard_map/reduce_scatter | solution.py:824
  15.9 0.7 copy-start.32
  16.0 0.9 copy-start.25
  16.0 1.0 copy-start.26
  154.4 2.7 copy-start.2
  159.0 10.6 %copy-start.12 = (bf16[1,8,96,768]{3,2,1,0:T(8,128)(2,1)}, bf16[1,8,96,768]{3,2,1,0:T(8,128)(2,1)S(1)}, u32[]{:S(2)}) copy-start(bf16[1,8,96,768]{3,2,1,0:T(8,128)(2,1)S(1)} %get-tuple-element.119) | copy-start | bytes 3538948
  159.0 10.6 %copy-start.19 = (bf16[1,8,96,768]{3,2,1,0:T(8,128)(2,1)}, bf16[1,8,96,768]{3,2,1,0:T(8,128)(2,1)S(1)}, u32[]{:S(2)}) copy-start(bf16[1,8,96,768]{3,2,1,0:T(8,128)(2,1)S(1)} %get-tuple-element.121) | copy-start | bytes 3538948
  159.0 10.5 %copy-start.3 = (bf16[4,8,128,768]{3,2,1,0:T(8,128)(2,1)S(1)}, bf16[4,8,128,768]{3,2,1,0:T(8,128)(2,1)}, u32[]{:S(2)}) copy-start(bf16[4,8,128,768]{3,2,1,0:T(8,128)(2,1)} %copy-done.2) | copy-start | bytes 18874372
  169.5 7.0 copy-start.42
  169.5 8.9 %copy-start.41 = (s32[8]{0:T(128)S(1)}, s32[8]{0:T(128)}, u32[]{:S(2)}) copy-start(s32[8]{0:T(128)} %param.22) | copy-start | bytes 100
  176.6 4.6 copy-start.21
  178.1 93.3 %copy-start.30 = (f32[768]{0:T(1024)}, f32[768]{0:T(1024)S(1)}, u32[]{:S(2)}) copy-start(f32[768]{0:T(1024)S(1)} %add.151) | copy-start | bytes 9220
  181.2 72.2 %copy-start.17 = (bf16[1,8,128,768]{3,2,1,0:T(8,128)(2,1)}, bf16[1,8,128,768]{3,2,1,0:T(8,128)(2,1)S(1)}, u32[]{:S(2)}) copy-start(bf16[1,8,128,768]{3,2,1,0:T(8,128)(2,1)S(1)} %constant_dynamic-slice_fusion.1) | copy-start | bytes 4718596
  183.7 69.6 %copy-start.22 = (bf16[1,8,96,768]{3,2,1,0:T(8,128)(2,1)S(1)}, bf16[1,8,96,768]{3,2,1,0:T(8,128)(2,1)}, u32[]{:S(2)}) copy-start(bf16[1,8,96,768]{3,2,1,0:T(8,128)(2,1)} %get-tuple-element.120) | copy-start | bytes 3538948
  256.8 1.6 copy-start.6
  292.0 1.4 copy-start.4
  295.3 2.9 copy-start.40
  295.3 16.6 %slice-start = ((s8[4718592]{0:T(1024)(128)(4,1)}), s8[4194304]{0:T(1024)(128)(4,1)S(1)}, s32[]{:S(2)}) async-start(s8[4718592]{0:T(1024)(128)(4,1)} %bitcast.151), calls=%async_computation.7 | async-start | bytes 8388608
  298.2 13.7 %copy-start.14 = (f32[1024,768]{1,0:T(8,128)}, f32[1024,768]{1,0:T(8,128)S(1)}, u32[]{:S(2)}) copy-start(f32[1024,768]{1,0:T(8,128)S(1)} %get-tuple-element.116) | copy-start | bytes 9437188
  298.2 13.7 %copy-start.7 = (f32[1024,768]{1,0:T(8,128)S(1)}, f32[1024,768]{1,0:T(8,128)}, u32[]{:S(2)}) copy-start(f32[1024,768]{1,0:T(8,128)} %copy-done.6) | copy-start | bytes 9437188
  298.2 13.7 %slice-start.1 = ((s8[4718592]{0:T(1024)(128)(4,1)}), s8[524288]{0:T(1024)(128)(4,1)S(1)}, s32[]{:S(2)}) async-start(s8[4718592]{0:T(1024)(128)(4,1)} %bitcast.151), calls=%async_computation.8 | async-start | bytes 1048576
  311.9 6.1 copy-start.45
  319.2 2.7 copy-start.9
  454.2 119.8 %reduce-scatter.5.cloned.1.call-start = ((), (), s32[]{:S(2)}) async-start(), calls=%async_computation.6 | async-start | bytes 7864320 | tf_op jit(solution)/shard_map/reduce_scatter | solution.py:825
  454.2 1.4 copy-start.5
  454.2 1.7 copy-start.43
  454.3 2.5 copy-start.16
  455.6 1.5 copy-start.29
  455.6 1.5 copy-start.27
  455.6 1.5 copy-start.28
  457.2 4.6 copy-start.10
  457.2 4.6 copy-start.44
  461.8 2.5 copy-start.8
  461.8 2.5 copy-start.31
  461.8 14.3 %slice-start.2 = ((s8[6291456]{0:T(1024)(128)(4,1)}), s8[4194304]{0:T(1024)(128)(4,1)S(1)}, s32[]{:S(2)}) async-start(s8[6291456]{0:T(1024)(128)(4,1)} %bitcast.153), calls=%async_computation.9 | async-start | bytes 8388608
  464.3 11.8 %copy-start.15 = (f32[1024,768]{1,0:T(8,128)S(1)}, f32[1024,768]{1,0:T(8,128)}, u32[]{:S(2)}) copy-start(f32[1024,768]{1,0:T(8,128)} %copy-done.14) | copy-start | bytes 9437188
  464.3 11.8 %slice-start.3 = ((s8[6291456]{0:T(1024)(128)(4,1)}), s8[2097152]{0:T(1024)(128)(4,1)S(1)}, s32[]{:S(2)}) async-start(s8[6291456]{0:T(1024)(128)(4,1)} %bitcast.153), calls=%async_computation.10 | async-start | bytes 4194304
  476.1 36.6 %copy-start.20 = (bf16[1,8,96,768]{3,2,1,0:T(8,128)(2,1)S(1)}, bf16[1,8,96,768]{3,2,1,0:T(8,128)(2,1)}, u32[]{:S(2)}) copy-start(bf16[1,8,96,768]{3,2,1,0:T(8,128)(2,1)} %copy-done.19) | copy-start | bytes 3538948
  483.1 90.8 %copy-start.13 = (bf16[1,8,96,768]{3,2,1,0:T(8,128)(2,1)S(1)}, bf16[1,8,96,768]{3,2,1,0:T(8,128)(2,1)}, u32[]{:S(2)}) copy-start(bf16[1,8,96,768]{3,2,1,0:T(8,128)(2,1)} %copy-done.12) | copy-start | bytes 3538948
  580.8 144.5 %all-to-all-start = ((bf16[8,128,768]{2,1,0:T(8,128)(2,1)}), bf16[8,128,768]{2,1,0:T(8,128)(2,1)S(1)}, u32[]{:S(2)}, u32[]{:S(2)}) async-start(bf16[8,128,768]{2,1,0:T(8,128)(2,1)} %bitcast.25), calls=%async_computation.2 | async-start | bytes 3145728 | tf_op jit(solution)/shard_map/all_to_all | solution.py:835
  586.5 4.5 copy-start.11
  592.5 3.5 copy-start.18
  596.0 1.5 copy-start.23
  596.0 1.6 copy-start.24
  725.2 5.4 copy-start.1
  (7 other events, 5.1 us)
Sparse Core Ops, SparseCore 0:
  10.2 128.3 all-gather.2
  140.8 77.4 all-gather.4
  454.3 58.3 reduce-scatter.2
  515.1 58.8 reduce-scatter.4

commit v3 on v2

--- a/solution.py
+++ b/solution.py
@@ -10,7 +10,6 @@
 SCALE = 64 ** (-0.5)
 LOG2E = 1.4426950408889634
 FORWARD_KEYS = 2048
-BACKWARD_KEYS = 1024
 VMEM_BYTES = 60 * 2**20
 
 NORM_EPSILON = 1e-12
@@ -111,79 +110,6 @@
     lse = jnp.where(low_half, top_a + jnp.log2(mass_a), top_b + jnp.log2(mass_b)).T
     lse_ref[0, 0:1, :] = lse[0:1, :]
     lse_ref[0, 1:2, :] = lse[64:65, :]
-
-
-def backward_kernel(
-    limit_ref,
-    query_ref,
-    key_ref,
-    value_ref,
-    grad_ref,
-    attended_ref,
-    lse_ref,
-    d_query_ref,
-    d_key_ref,
-    d_value_ref,
-    query_sum,
-    *,
-    key_rows,
-):
-    low_half = lane_is_low()
-    high_half = jnp.logical_not(low_half)
-    lane = lax.broadcasted_iota(jnp.int32, (1, 128), 1)
-    limit = limit_ref[0]
-    query_pair = query_ref[...].astype(jnp.float32)
-    queries = split_query(query_pair, low_half)
-    scaled = query_pair * SCALE
-    grad_pair = grad_ref[...].astype(jnp.float32)
-    overlap = grad_pair * attended_ref[...]
-    own_query, own_grad, joined_grad = [], [], []
-    for head in range(2):
-        mine = low_half if head == 0 else high_half
-        own_query.append(jnp.where(mine, scaled, 0.0).astype(jnp.bfloat16))
-        own_grad.append(jnp.where(mine, grad_pair, 0.0).astype(jnp.bfloat16))
-        delta = -jnp.sum(jnp.where(mine, overlap, 0.0), axis=1, keepdims=True)
-        first = delta.astype(jnp.bfloat16).astype(jnp.float32)
-        second = (delta - first).astype(jnp.bfloat16).astype(jnp.float32)
-        third = delta - first - second
-        spare = 64 * (1 - head)
-        joined = jnp.where(lane == spare + 2, third, 0.0)
-        joined = jnp.where(lane == spare + 1, second, joined)
-        joined = jnp.where(lane == spare, first, joined)
-        joined_grad.append(jnp.where(mine, grad_pair, joined).astype(jnp.bfloat16))
-    query_sum[...] = jnp.zeros_like(query_sum)
-
-    def step(tile, carry):
-        start = pl.multiple_of(tile * key_rows, key_rows)
-        usable = start + lax.broadcasted_iota(jnp.int32, (key_rows, 1), 0) < limit
-        key_tile = key_ref[pl.ds(start, key_rows), :].astype(jnp.float32)
-        value_tile = value_ref[pl.ds(start, key_rows), :].astype(jnp.float32)
-        keys = twice(jnp.where(usable, key_tile, key_ref[0:1, :].astype(jnp.float32)), low_half)
-        own_tile = jnp.where(usable, key_tile * SCALE, 0.0)
-        key_piece = value_piece = None
-        for head in range(2):
-            mine = low_half if head == 0 else high_half
-            values = jnp.where(mine, value_tile, 1.0).astype(jnp.bfloat16)
-            own_key = jnp.where(mine, own_tile, 0.0).astype(jnp.bfloat16)
-            scores = product(keys[head], queries[head], ((1,), (1,)))
-            probs = jnp.exp2(scores - lse_ref[0, head : head + 1, :])
-            slopes = product(values, joined_grad[head], ((1,), (1,)))
-            score_grads = (probs * slopes).astype(jnp.bfloat16)
-            value_term = product(probs.astype(jnp.bfloat16), own_grad[head], ((1,), (0,)))
-            key_term = product(score_grads, own_query[head], ((1,), (0,)))
-            value_piece = value_term if value_piece is None else value_piece + value_term
-            key_piece = key_term if key_piece is None else key_piece + key_term
-            query_sum[...] += product(own_key, score_grads, ((0,), (0,)))
-        d_value_ref[pl.ds(start, key_rows), :] = jnp.where(usable, value_piece, 0.0).astype(
-            jnp.bfloat16
-        )
-        d_key_ref[pl.ds(start, key_rows), :] = jnp.where(usable, key_piece, 0.0).astype(
-            jnp.bfloat16
-        )
-        return carry
-
-    lax.fori_loop(0, key_ref.shape[0] // key_rows, step, 0)
-    d_query_ref[...] = query_sum[...].T.astype(jnp.bfloat16)
 
 
 def attend_forward(queries, keys, values, limit):
@@ -213,41 +139,6 @@
         ),
         name="attend_forward",
     )(limit, queries, keys, values)
-
-
-def attend_backward(queries, keys, values, limit, grad_rows, attended, lse):
-    rows, width = queries.shape
-    full = keys.shape[0]
-    pairs = width // 128
-    row_spec = pl.BlockSpec((rows, 128), lambda pair, *_: (0, pair))
-    key_spec = pl.BlockSpec((full, 128), lambda pair, *_: (0, pair))
-    return pl.pallas_call(
-        functools.partial(backward_kernel, key_rows=BACKWARD_KEYS),
-        grid_spec=pltpu.PrefetchScalarGridSpec(
-            num_scalar_prefetch=1,
-            grid=(pairs,),
-            in_specs=[
-                row_spec,
-                key_spec,
-                pl.BlockSpec((full, 128), lambda pair, *_: (0, pair)),
-                row_spec,
-                row_spec,
-                pl.BlockSpec((1, 2, rows), lambda pair, *_: (pair, 0, 0)),
-            ],
-            out_specs=[row_spec, key_spec, key_spec],
-            scratch_shapes=[pltpu.VMEM((128, rows), jnp.float32)],
-        ),
-        out_shape=[
-            jax.ShapeDtypeStruct((rows, width), jnp.bfloat16),
-            jax.ShapeDtypeStruct((full, width), jnp.bfloat16),
-            jax.ShapeDtypeStruct((full, width), jnp.bfloat16),
-        ],
-        compiler_params=pltpu.CompilerParams(vmem_limit_bytes=VMEM_BYTES),
-        cost_estimate=pl.CostEstimate(
-            flops=40 * rows * full * width, bytes_accessed=40_000_000, transcendentals=0
-        ),
-        name="attend_backward",
-    )(limit, queries, keys, values, grad_rows, attended, lse)
 
 
 MESH = pl.DeviceIdType.MESH
@@ -696,6 +587,124 @@
         self.own_out().wait()
 
 
+class LateSum:
+    SCRATCH = 16
+
+    def __init__(self, kind, ref, out, scratch, count):
+        self.kind, self.ref, self.out, self.count = kind, ref, out, count
+        self.near, self.got, self.got_group, self.half, self.got_across, self.done = scratch[:6]
+        self.load, self.c_send, self.c_recv, self.g_send, self.g_recv = scratch[6:11]
+        self.x_send, self.x_recv, self.o_send, self.o_recv, self.put = scratch[11:16]
+        self.ctx, self.group, self.across, self.sibling = places()
+        self.core = lax.rem(self.ctx, 2)
+        self.width = self.near.shape[-1]
+
+    @staticmethod
+    def scratch(count, rows, width):
+        return (
+            [pltpu.VMEM((count, 2, rows, width), jnp.bfloat16)] * 3
+            + [pltpu.VMEM((2, rows, width), jnp.bfloat16)] * 3
+            + [DMA((2,))] * 3
+            + [DMA((count,))] * 2
+            + [DMA((2,))] * 5
+        )
+
+    def quarter(self, index):
+        if self.kind == 1:
+            start = pl.multiple_of(index * self.width, self.width)
+            return self.ref.at[:, :, pl.ds(start, self.width)]
+        return self.ref.at[:, index]
+
+    def load_copy(self, half):
+        return pltpu.make_async_copy(
+            self.quarter(2 * half + self.core), self.near.at[:, half], self.load.at[half]
+        )
+
+    def core_copy(self, half):
+        return remote(
+            self.quarter(2 * half + 1 - self.core),
+            self.got.at[:, half],
+            self.c_send.at[half],
+            self.c_recv.at[half],
+            {"ctx": self.sibling},
+        )
+
+    def group_copy(self, step):
+        peer = lax.rem(self.group + step, self.count)
+        return remote(
+            self.near.at[peer],
+            self.got_group.at[step],
+            self.g_send.at[step],
+            self.g_recv.at[step],
+            {"fsdp": peer},
+        )
+
+    def x_copy(self):
+        return remote(
+            self.half, self.got_across, self.x_send.at[0], self.x_recv.at[0], {"ctx": self.across}
+        )
+
+    def out_copy(self, half):
+        return remote(
+            self.done.at[half],
+            self.out.at[2 * half + self.core],
+            self.o_send.at[half],
+            self.o_recv.at[half],
+            {"ctx": self.sibling},
+        )
+
+    def own_out(self, half):
+        return pltpu.make_async_copy(
+            self.done.at[half], self.out.at[2 * half + self.core], self.put.at[half]
+        )
+
+    def start(self):
+        for half in range(2):
+            self.load_copy(half).start()
+            self.core_copy(half).start()
+
+    def after_core(self):
+        for half in range(2):
+            self.load_copy(half).wait()
+            self.core_copy(half).wait()
+
+        def one(step, carry):
+            block = lax.rem(self.group + step, self.count)
+            both = self.near[block].astype(jnp.float32) + self.got[block].astype(jnp.float32)
+            self.near[block] = both.astype(jnp.bfloat16)
+            return carry
+
+        lax.fori_loop(0, self.count, one, 0)
+
+        def send(step, carry):
+            self.group_copy(step).start()
+            return carry
+
+        lax.fori_loop(1, self.count, send, 0)
+
+    def after_group(self):
+        def one(step, total):
+            self.group_copy(step).wait()
+            return total + self.got_group[step].astype(jnp.float32)
+
+        total = lax.fori_loop(1, self.count, one, self.near[self.group].astype(jnp.float32))
+        self.half[...] = total.astype(jnp.bfloat16)
+        self.x_copy().start()
+
+    def after_across(self):
+        self.x_copy().wait()
+        both = self.half[...].astype(jnp.float32) + self.got_across[...].astype(jnp.float32)
+        self.done[...] = both.astype(jnp.bfloat16)
+        for half in range(2):
+            self.own_out(half).start()
+            self.out_copy(half).start()
+
+    def finish(self):
+        for half in range(2):
+            self.own_out(half).wait()
+            self.out_copy(half).wait()
+
+
 def sums_kernel(*refs, kinds, count):
     parts = len(kinds)
     ins, outs, rest = refs[: parts + 1], refs[parts + 1 : 2 * parts + 2], refs[2 * parts + 2 :]
@@ -726,6 +735,225 @@
         ),
         name="sum_gradients",
     )(*parts, vectors)
+
+
+def backward_kernel(
+    limit_ref,
+    query_ref,
+    key_ref,
+    value_ref,
+    grad_ref,
+    attended_ref,
+    lse_ref,
+    inner_ref,
+    outer_ref,
+    d_query_ref,
+    d_key_ref,
+    d_value_ref,
+    inner_out,
+    outer_out,
+    query_sum,
+    part,
+    got_core,
+    far,
+    near,
+    got_x,
+    core_send,
+    core_recv,
+    x_send,
+    x_recv,
+    *rest,
+    count,
+):
+    pair = pl.program_id(0)
+    pairs = pl.num_programs(0) - 1
+    slot = lax.rem(pair, 2)
+    ctx, _, across, sibling = places()
+    key_rows = query_ref.shape[0]
+    jobs = [
+        LateSum(1, inner_ref, inner_out, rest[: LateSum.SCRATCH], count),
+        LateSum(2, outer_ref, outer_out, rest[LateSum.SCRATCH :], count),
+    ]
+
+    def core_copy(which):
+        return remote(
+            part.at[which],
+            got_core.at[slot, which],
+            core_send.at[which],
+            core_recv.at[slot, which],
+            {"ctx": sibling},
+        )
+
+    def x_copy(where):
+        return remote(
+            far.at[where], got_x.at[where], x_send.at[where], x_recv.at[where], {"ctx": across}
+        )
+
+    def settle():
+        where = 1 - slot
+        x_copy(where).wait()
+        for kind, ref in enumerate((d_key_ref, d_value_ref)):
+            both = near[where, kind].astype(jnp.float32) + got_x[where, kind].astype(jnp.float32)
+            ref[...] = both.astype(jnp.bfloat16)
+
+    @pl.when(pair == 0)
+    def _():
+        greet(count)
+        for job in jobs:
+            job.start()
+
+    @pl.when(pair == 1)
+    def _():
+        for job in jobs:
+            job.after_core()
+
+    @pl.when(pair < pairs)
+    def _():
+        low_half = lane_is_low()
+        high_half = jnp.logical_not(low_half)
+        lane = lax.broadcasted_iota(jnp.int32, (1, 128), 1)
+        limit = limit_ref[0]
+        query_pair = query_ref[...].astype(jnp.float32)
+        queries = split_query(query_pair, low_half)
+        scaled = query_pair * SCALE
+        grad_pair = grad_ref[...].astype(jnp.float32)
+        overlap = grad_pair * attended_ref[...]
+        own_query, own_grad, joined_grad = [], [], []
+        for head in range(2):
+            mine = low_half if head == 0 else high_half
+            own_query.append(jnp.where(mine, scaled, 0.0).astype(jnp.bfloat16))
+            own_grad.append(jnp.where(mine, grad_pair, 0.0).astype(jnp.bfloat16))
+            delta = -jnp.sum(jnp.where(mine, overlap, 0.0), axis=1, keepdims=True)
+            first = delta.astype(jnp.bfloat16).astype(jnp.float32)
+            second = (delta - first).astype(jnp.bfloat16).astype(jnp.float32)
+            third = delta - first - second
+            spare = 64 * (1 - head)
+            joined = jnp.where(lane == spare + 2, third, 0.0)
+            joined = jnp.where(lane == spare + 1, second, joined)
+            joined = jnp.where(lane == spare, first, joined)
+            joined_grad.append(jnp.where(mine, grad_pair, joined).astype(jnp.bfloat16))
+        query_sum[...] = jnp.zeros_like(query_sum)
+
+        def step(tile, carry):
+            odd = lax.rem(tile, 2)
+            quarter = lax.rem(sibling + odd * (ctx - sibling) + 2 * (1 - tile // 2), 4)
+            start = pl.multiple_of(quarter * key_rows, key_rows)
+            usable = start + lax.broadcasted_iota(jnp.int32, (key_rows, 1), 0) < limit
+            key_tile = key_ref[pl.ds(start, key_rows), :].astype(jnp.float32)
+            value_tile = value_ref[pl.ds(start, key_rows), :].astype(jnp.float32)
+            keys = twice(jnp.where(usable, key_tile, key_ref[0:1, :].astype(jnp.float32)), low_half)
+            own_tile = jnp.where(usable, key_tile * SCALE, 0.0)
+            key_piece = value_piece = None
+            for head in range(2):
+                mine = low_half if head == 0 else high_half
+                values = jnp.where(mine, value_tile, 1.0).astype(jnp.bfloat16)
+                own_key = jnp.where(mine, own_tile, 0.0).astype(jnp.bfloat16)
+                scores = product(keys[head], queries[head], ((1,), (1,)))
+                probs = jnp.exp2(scores - lse_ref[0, head : head + 1, :])
+                slopes = product(values, joined_grad[head], ((1,), (1,)))
+                score_grads = (probs * slopes).astype(jnp.bfloat16)
+                value_term = product(probs.astype(jnp.bfloat16), own_grad[head], ((1,), (0,)))
+                key_term = product(score_grads, own_query[head], ((1,), (0,)))
+                value_piece = value_term if value_piece is None else value_piece + value_term
+                key_piece = key_term if key_piece is None else key_piece + key_term
+                query_sum[...] += product(own_key, score_grads, ((0,), (0,)))
+            pieces = (jnp.where(usable, key_piece, 0.0), jnp.where(usable, value_piece, 0.0))
+
+            @pl.when(odd == 0)
+            def _():
+                which = tile // 2
+                for kind in range(2):
+                    part[which, kind] = pieces[kind].astype(jnp.bfloat16)
+                core_copy(which).start()
+
+            @pl.when(tile == 1)
+            def _():
+                @pl.when(pair > 0)
+                def _():
+                    settle()
+
+                core_copy(0).wait_recv()
+                for kind in range(2):
+                    both = pieces[kind] + got_core[slot, 0, kind].astype(jnp.float32)
+                    far[slot, kind] = both.astype(jnp.bfloat16)
+                x_copy(slot).start()
+
+            @pl.when(tile == 3)
+            def _():
+                core_copy(1).wait_recv()
+                for kind in range(2):
+                    both = pieces[kind] + got_core[slot, 1, kind].astype(jnp.float32)
+                    near[slot, kind] = both.astype(jnp.bfloat16)
+                core_copy(0).wait_send()
+                core_copy(1).wait_send()
+
+            return carry
+
+        lax.fori_loop(0, 4, step, 0)
+        d_query_ref[...] = query_sum[...].T.astype(jnp.bfloat16)
+
+    @pl.when(pair == pairs)
+    def _():
+        for job in jobs:
+            job.after_group()
+        settle()
+        for job in jobs:
+            job.after_across()
+        for job in jobs:
+            job.finish()
+
+
+def attend_backward(queries, keys, values, limit, grad_rows, attended, lse, inner_part, outer_part):
+    rows, width = queries.shape
+    full = keys.shape[0]
+    pairs = width // 128
+    count, shard = inner_part.shape[:2]
+    now = lambda pair, *_: (0, jnp.minimum(pair, pairs - 1))
+    before = lambda pair, *_: (0, jnp.maximum(pair - 1, 0))
+    row_spec = pl.BlockSpec((rows, 128), now)
+    key_spec = pl.BlockSpec((full, 128), now)
+    sum_spec = pl.BlockSpec((rows, 128), before)
+    tile = (2, rows, 128)
+    return pl.pallas_call(
+        functools.partial(backward_kernel, count=count),
+        grid_spec=pltpu.PrefetchScalarGridSpec(
+            num_scalar_prefetch=1,
+            grid=(pairs + 1,),
+            in_specs=[
+                row_spec,
+                key_spec,
+                key_spec,
+                row_spec,
+                row_spec,
+                pl.BlockSpec((1, 2, rows), lambda pair, *_: (jnp.minimum(pair, pairs - 1), 0, 0)),
+                ANY,
+                ANY,
+            ],
+            out_specs=[row_spec, sum_spec, sum_spec, ANY, ANY],
+            scratch_shapes=[
+                pltpu.VMEM((128, rows), jnp.float32),
+                pltpu.VMEM((2,) + tile, jnp.bfloat16),
+                pltpu.VMEM((2, 2) + tile, jnp.bfloat16),
+                pltpu.VMEM((2,) + tile, jnp.bfloat16),
+                pltpu.VMEM((2,) + tile, jnp.bfloat16),
+                pltpu.VMEM((2,) + tile, jnp.bfloat16),
+                DMA((2,)),
+                DMA((2, 2)),
+                DMA((2,)),
+                DMA((2,)),
+            ]
+            + LateSum.scratch(count, shard, width) * 2,
+        ),
+        out_shape=[jax.ShapeDtypeStruct((rows, width), jnp.bfloat16)] * 3
+        + [jax.ShapeDtypeStruct((4, shard, width), jnp.bfloat16)] * 2,
+        compiler_params=pltpu.CompilerParams(
+            collective_id=2, has_side_effects=True, vmem_limit_bytes=VMEM_BYTES
+        ),
+        cost_estimate=pl.CostEstimate(
+            flops=40 * rows * full * width, bytes_accessed=40_000_000, transcendentals=0
+        ),
+        name="attend_backward",
+    )(limit, queries, keys, values, grad_rows, attended, lse, inner_part, outer_part)
 
 
 def on_device(
@@ -818,11 +1046,17 @@
     grad_output_w = product(mixed_low, d_branch, ((0,), (0,))).astype(low)
     grad_output_b = jnp.sum(d_branch.astype(jnp.float32), axis=0)
     d_mixed = product(d_branch, w_output, ((1,), (1,))).astype(low)
-    d_query, key_terms, value_terms = attend_backward(
-        queries, keys, values, limits, d_mixed, attended, lse
-    )
-    d_keys = lax.psum_scatter(key_terms, "ctx", scatter_dimension=0, tiled=True)
-    d_values = lax.psum_scatter(value_terms, "ctx", scatter_dimension=0, tiled=True)
+    d_query, d_keys, d_values, inner_w, outer_w = attend_backward(
+        queries,
+        keys,
+        values,
+        limits,
+        d_mixed,
+        attended,
+        lse,
+        grad_inner_w.reshape(count, shard, 4 * width),
+        grad_outer_w.reshape(count, 4, shard, width),
+    )
     grad_query_w = product(token_rows, d_query, ((0,), (0,))).astype(low)
     grad_query_b = jnp.sum(d_query.astype(jnp.float32), axis=0)
     grad_key_w = product(token_rows, d_keys, ((0,), (0,))).astype(low)
@@ -854,13 +1088,9 @@
             jnp.zeros((4, width), jnp.float32),
         )
     )
-    attention_w, inner_w, outer_w, small_sums = sum_gradients(
-        (
-            attention_w.reshape(4, count, shard, width),
-            grad_inner_w.reshape(count, shard, 4 * width),
-            grad_outer_w.reshape(count, 4, shard, width),
-        ),
-        (0, 1, 2),
+    attention_w, small_sums = sum_gradients(
+        (attention_w.reshape(4, count, shard, width),),
+        (0,),
         small_sums,
         shard,
         width,

time: 743 us -> 628 us (0.85)
  waiting for transfers between devices: 88.2 us -> 1.4 us
  matrix products: 125 us -> 105 us
  Pallas kernels: 454 us -> 437 us
    reduce_scatter x2 -> x0, waiting for transfers between devices: 86.3 us -> none  [the longest x1 56.7 us: on_device(): lax.psum_scatter(value_terms, 'ctx', scatter_dimension=0, tiled=True)]
    pallas_call x1, Pallas kernels: 116 us -> 67.5 us  [sum_gradients(): pl.pallas_call(functools.partial(sums_kernel, kinds=kinds, count=count),...]
    pallas_call x1, Pallas kernels: 132 us -> 156 us  [attend_backward(): pl.pallas_call(functools.partial(backward_kernel, count=count), grid_spec...]
    dot_general x18, matrix products: 125 us -> 105 us  [product(): lax.dot_general(left, right, (dims, ((), ())), preferred_element_type=jnp...]
    pallas_call x1, Pallas kernels: 136 us -> 144 us  [bring_in(): pl.pallas_call(functools.partial(arrival_kernel, count=count), in_specs=[...]
  transfers between devices with their start and end apart: 5 -> 3, of which waited for: 2 -> 0; matrix products, arithmetic and copies ran while one was open for 14% -> 12% of each run, Pallas kernels for 44% -> 45%
where the time goes in v3:
time: 628 us; the launch traced here: 619 us
  Pallas kernels  437 us (70%)
  matrix products  105 us (17%)
  local copies, waits for them, and re-layouts  29.5 us (5%)
  other arithmetic  22.3 us (4%)
  between operations  16.6 us (3%)
  starting transfers between devices  7.17 us (1%)
    pallas_call x1, Pallas kernels, attend_backward(): pl.pallas_call(functools.partial(backward_kernel, count=count), grid_spec...  156 us
    pallas_call x1, Pallas kernels, bring_in(): pl.pallas_call(functools.partial(arrival_kernel, count=count), in_specs=[...  144 us
    dot_general x18, matrix products, product(): lax.dot_general(left, right, (dims, ((), ())), preferred_element_type=jnp...  105 us
    pallas_call x1, Pallas kernels, attend_forward(): pl.pallas_call(functools.partial(forward_kernel, key_rows=FORWARD_KEYS),...  69.3 us
    pallas_call x1, Pallas kernels, sum_gradients(): pl.pallas_call(functools.partial(sums_kernel, kinds=kinds, count=count),...  67.5 us
  transfers between devices with their start and end apart: 3, of which 0 were waited for; matrix products, arithmetic and copies ran while one was open for 12% of the time, Pallas kernels for 45%

profile of v3, /device:TPU:29, one launch (start us, length us, event | category | flops | bytes accessed | tf_op | source)
XLA Modules:
  0.0 618.7 jit_solution(17616121790540122797)
XLA Ops:
  10.0 1.3 iota_reduce_fusion
  11.3 0.8 reshape.136
  12.0 5.0 gather_fusion
  18.2 1.1 pad_maximum_fusion.1.weights
  19.3 144.0 %bring_in.1 = (bf16[4,8,128,768]{3,2,1,0:T(8,128)(2,1)S(1)}, bf16[4,8,96,768]{3,2,1,0:T(8,128)(2,1)S(1)}, bf16[8,16,128]{2,1,0:T(8,128)(2,1)S(1)}) custom-call(bf16[8,128,768]{2,1,0:T(8,128)(2,1)S(1)} %copy_select_fusion.placed, bf16[4,96,768]{2,1,0:T(8,128)(2,1)S(1)} %pad_maximum_fusion.1.weights, bf16[16,128]{1,0:T(8,128)(2,1)S(1)} %pad.4.small), custom_call_target="tpu_custom_call" | custom-call | tf_op jit(solution)/shard_map/bring_in/pallas_call | solution.py:344
  163.3 2.7 copy-done.2
  166.1 1.9 fusion.27
  168.7 9.2 %convolution_convert_fusion.key_ref = bf16[4096,768]{1,0:T(8,128)(2,1)} fusion(bf16[4096,768]{1,0:T(8,128)(2,1)} %bitcast.116, bf16[768,768]{1,0:T(8,128)(2,1)} %bitcast.126), kind=kOutput, calls=%fused_computation.13 | convolution fusion | flops 4834983936 | bytes 13762560 | tf_op jit(solution)/shard_map/dot_general | solution.py:48
  177.9 10.2 %add_convert_fusion.value_ref = bf16[4096,768]{1,0:T(8,128)(2,1)} fusion(f32[768]{0:T(1024)S(1)} %add.139, bf16[4096,768]{1,0:T(8,128)(2,1)} %bitcast.117, bf16[768,768]{1,0:T(8,128)(2,1)S(1)} %bitcast.119), kind=kOutput, calls=%fused_computation.12 | convolution fusion | flops 4838129664 | bytes 13765632 | tf_op jit(solution)/shard_map/dot_general | solution.py:48
  188.1 1.5 constant_dynamic-slice_fusion.1
  194.6 3.8 add_convert_fusion.3.query_ref
  198.4 69.3 %attend_forward.1 = (f32[1024,768]{1,0:T(8,128)}, f32[6,2,1024]{2,1,0:T(2,128)}) custom-call(s32[1]{0:T(128)S(6)} %select_n.40.limit_ref, bf16[1024,768]{1,0:T(8,128)(2,1)} %add_convert_fusion.3.query_ref, bf16[4096,768]{1,0:T(8,128)(2,1)} %convolution_convert_fusion.key_ref, bf16[4096,768]{1,0:T(8,128)(2,1)} %add_convert_fusion.value_ref), custom_call_target="tpu_custom_call" | custom-call | flops 51539607552 | bytes 20000000 | tf_op jit(solution)/shard_map/attend_forward/pallas_call | solution.py:120
  267.8 3.7 fusion.28
  271.5 1.7 copy-done.4
  273.8 12.5 %multiply_convert_fusion = (bf16[1024,3072]{1,0:T(8,128)(2,1)}, f32[1024,3072]{1,0:T(8,128)}) fusion(f32[3072]{0:T(1024)S(1)} %add.150, bf16[768,3072]{1,0:T(8,128)(2,1)} %all-gather.3.cloned.1.call-done, f32[1024,768]{1,0:T(8,128)} %copy-done.4, f32[768]{0:T(1024)S(1)} %add.147, f32[768]{0:T(1024)S(1)} %mul.132, f32[1024]{0:T(1024)S(1)} %add_rsqrt_fusion.1, ...), kind=kOutput, calls=%fused_computation.10 | convolution fusion | flops 4854644736 | bytes 26765312 | tf_op jit(solution)/shard_map/dot_general | solution.py:48
  286.3 9.7 %fusion.29 = (f32[1024]{0:T(1024)S(1)}, f32[1024,768]{1,0:T(8,128)S(1)}) fusion(f32[768]{0:T(1024)S(1)} %add.154, bf16[1024,3072]{1,0:T(8,128)(2,1)} %get-tuple-element.138, bf16[3072,768]{1,0:T(8,128)(2,1)} %all-gather.5.cloned.1.call-done, f32[768]{0:T(1024)S(1)} %add.147, f32[768]{0:T(1024)S(1)} %mul.132, f32[1024]{0:T(1024)S(1)} %add_rsqrt_fusion.1, ...), kind=kOutput, calls=%fused_computation.107 | convolution fusion | flops 4837342208 | bytes 17323008 | tf_op jit(solution)/shard_map/dot_general | solution.py:48
  296.5 1.9 fusion.14
  298.5 2.9 convert_reduce_fusion.2
  301.4 7.1 %convolution_convert_fusion.1 = bf16[3072,768]{1,0:T(8,128)(2,1)} fusion(bf16[1024,3072]{1,0:T(8,128)(2,1)S(1)} %copy-done.40, f32[1024,768]{1,0:T(8,128)S(1)} %get-tuple-element.116), kind=kOutput, calls=%fused_computation.14 | convolution fusion | flops 4834983936 | bytes 14155776 | tf_op jit(solution)/shard_map/dot_general | solution.py:48
  308.5 12.4 %convert_reduce_fusion = (f32[3072]{0:T(1024)}, bf16[1024,3072]{1,0:T(8,128)(2,1)S(1)}) fusion(f32[1024,3072]{1,0:T(8,128)} %get-tuple-element.139, f32[3072]{0:T(1024)S(1)} %add.150, bf16[3072,768]{1,0:T(8,128)(2,1)S(1)} %bitcast.152, f32[1024,768]{1,0:T(8,128)S(1)} %get-tuple-element.116), kind=kOutput, calls=%fused_computation.9 | convolution fusion | flops 4873516032 | bytes 26763264 | tf_op jit(solution)/shard_map/dot_general | solution.py:48
  320.9 8.1 %convolution_convert_fusion.2 = bf16[768,3072]{1,0:T(8,128)(2,1)} fusion(bf16[1024,3072]{1,0:T(8,128)(2,1)S(1)} %get-tuple-element.144, f32[1024,768]{1,0:T(8,128)S(1)} %copy-done.5, f32[768]{0:T(1024)S(1)} %add.147, f32[768]{0:T(1024)S(1)} %mul.132, f32[1024]{0:T(1024)S(1)} %add_rsqrt_fusion.1, f32[1024]{0:T(1024)S(1)} %broadcast_multiply_fusion.5), kind=kOutput, calls=%fused_computation.15 | convolution fusion | flops 4838129664 | bytes 14170112 | tf_op jit(solution)/shard_map/dot_general | solution.py:48
  329.0 6.1 multiply_reduce_fusion
  335.1 1.1 convert_reduce_fusion.3
  336.4 2.7 convolution_convert_fusion.3.grad_ref
  339.1 156.3 %attend_backward.1 = (bf16[1024,768]{1,0:T(8,128)(2,1)}, bf16[1024,768]{1,0:T(8,128)(2,1)}, bf16[1024,768]{1,0:T(8,128)(2,1)}, bf16[4,96,768]{2,1,0:T(8,128)(2,1)}, bf16[4,96,768]{2,1,0:T(8,128)(2,1)}) custom-call(s32[1]{0:T(128)S(6)} %select_n.40.limit_ref, bf16[1024,768]{1,0:T(8,128)(2,1)} %add_convert_fusion.3.query_ref, ...), custom_call_target="tpu_custom_call" | custom-call | flops 128849018880 | bytes 40000000 | tf_op jit(solution)/shard_map/attend_backward/pallas_call | solution.py:917
  495.4 1.7 convert_reduce_fusion.5
  497.1 4.0 convolution_convert_fusion.7
  501.2 3.1 fusion.30
  504.7 3.0 fusion.31
  508.4 2.7 add_convert_fusion.1
  511.1 7.1 %all-to-all-start = ((bf16[8,128,768]{2,1,0:T(8,128)(2,1)}), bf16[8,128,768]{2,1,0:T(8,128)(2,1)S(1)}, u32[]{:S(2)}, u32[]{:S(2)}) async-start(bf16[8,128,768]{2,1,0:T(8,128)(2,1)} %bitcast.27), calls=%async_computation | async-start | bytes 3145728 | tf_op jit(solution)/shard_map/all_to_all | solution.py:1069
  518.2 1.3 concatenate.8.refs_1_
  519.5 3.4 convolution_convert_fusion.6
  522.9 1.5 convolution_convert_fusion.5
  524.8 1.0 copy-done.39
  525.8 1.5 convolution_convert_fusion.4
  527.3 2.4 pad_maximum_fusion.refs_0_
  529.7 67.5 %sum_gradients.1 = (bf16[4,96,768]{2,1,0:T(8,128)(2,1)}, f32[16,768]{1,0:T(8,128)}) custom-call(bf16[4,8,96,768]{3,2,1,0:T(8,128)(2,1)} %pad_maximum_fusion.refs_0_, f32[16,768]{1,0:T(8,128)} %concatenate.8.refs_1_), custom_call_target="tpu_custom_call" | custom-call | tf_op jit(solution)/shard_map/sum_gradients/pallas_call | solution.py:726
  597.2 0.7 slice.99
  598.0 0.7 slice.108
  598.7 1.2 convert_element_type.128
  599.9 1.2 convert_bitcast_fusion.1
  601.1 1.1 copy.42
  603.5 1.0 slice_bitcast_fusion
  604.5 1.1 bitcast_convert_fusion
  605.7 2.0 gather_fusion.1
  607.7 1.6 select_bitcast_fusion
  609.3 2.0 copy.41
  (144 shorter events, 12.2 us)
Async XLA Ops:
  7.2 4.9 copy-start
  7.2 266.6 %all-gather.3.cloned.1.call-start = ((), (), s32[]{:S(2)}) async-start(), calls=%async_computation.1 | async-start | bytes 5308416 | tf_op jit(solution)/shard_map/all_gather | solution.py:1006
  7.9 278.3 %all-gather.5.cloned.1.call-start = ((), (), s32[]{:S(2)}) async-start(), calls=%async_computation.2 | async-start | bytes 5308416 | tf_op jit(solution)/shard_map/all_gather | solution.py:1007
  17.1 0.7 copy-start.28
  17.1 0.7 copy-start.29
  17.1 0.7 copy-start.30
  17.1 0.7 copy-start.31
  17.1 0.7 copy-start.32
  17.1 0.7 copy-start.33
  17.1 0.7 copy-start.34
  17.2 0.7 copy-start.35
  17.2 0.9 copy-start.22
  17.2 1.0 copy-start.23
  163.3 2.7 copy-start.2
  166.1 2.3 copy-start.3
  168.0 9.9 %copy-start.10 = (bf16[1,8,96,768]{3,2,1,0:T(8,128)(2,1)}, bf16[1,8,96,768]{3,2,1,0:T(8,128)(2,1)S(1)}, u32[]{:S(2)}) copy-start(bf16[1,8,96,768]{3,2,1,0:T(8,128)(2,1)S(1)} %get-tuple-element.119) | copy-start | bytes 3538948
  188.1 1.6 copy-start.37
  188.1 4.1 copy-start.38
  189.6 78.1 %copy-start.14 = (bf16[1,8,128,768]{3,2,1,0:T(8,128)(2,1)}, bf16[1,8,128,768]{3,2,1,0:T(8,128)(2,1)S(1)}, u32[]{:S(2)}) copy-start(bf16[1,8,128,768]{3,2,1,0:T(8,128)(2,1)S(1)} %constant_dynamic-slice_fusion.1) | copy-start | bytes 4718596
  271.5 1.7 copy-start.4
  296.5 4.8 copy-start.40
  298.5 10.0 %slice-start.2 = ((s8[4718592]{0:T(1024)(128)(4,1)}), s8[4194304]{0:T(1024)(128)(4,1)S(1)}, s32[]{:S(2)}) async-start(s8[4718592]{0:T(1024)(128)(4,1)} %bitcast.151), calls=%async_computation.5 | async-start | bytes 8388608
  301.4 7.1 %slice-start.3 = ((s8[4718592]{0:T(1024)(128)(4,1)}), s8[524288]{0:T(1024)(128)(4,1)S(1)}, s32[]{:S(2)}) async-start(s8[4718592]{0:T(1024)(128)(4,1)} %bitcast.151), calls=%async_computation.6 | async-start | bytes 1048576
  301.4 27.6 %slice-start = ((s8[4718592]{0:T(1024)(128)(4,1)}), s8[4194304]{0:T(1024)(128)(4,1)S(1)}, s32[]{:S(2)}) async-start(s8[4718592]{0:T(1024)(128)(4,1)} %bitcast.149), calls=%async_computation.3 | async-start | bytes 8388608
  308.4 12.5 %copy-start.5 = (f32[1024,768]{1,0:T(8,128)S(1)}, f32[1024,768]{1,0:T(8,128)}, u32[]{:S(2)}) copy-start(f32[1024,768]{1,0:T(8,128)} %copy-done.4) | copy-start | bytes 9437188
  308.4 20.6 %slice-start.1 = ((s8[4718592]{0:T(1024)(128)(4,1)}), s8[524288]{0:T(1024)(128)(4,1)S(1)}, s32[]{:S(2)}) async-start(s8[4718592]{0:T(1024)(128)(4,1)} %bitcast.149), calls=%async_computation.4 | async-start | bytes 1048576
  335.1 1.3 copy-start.19
  336.2 2.8 copy-start.6
  339.1 158.0 %copy-start.15 = (bf16[1,8,128,768]{3,2,1,0:T(8,128)(2,1)S(1)}, bf16[1,8,128,768]{3,2,1,0:T(8,128)(2,1)}, u32[]{:S(2)}) copy-start(bf16[1,8,128,768]{3,2,1,0:T(8,128)(2,1)} %copy-done.14) | copy-start | bytes 4718596
  497.1 4.0 copy-start.13
  497.1 4.0 copy-start.18
  501.1 3.1 copy-start.9
  501.1 3.5 copy-start.27
  501.2 3.5 copy-start.24
  501.2 3.5 copy-start.25
  501.2 3.5 copy-start.17
  504.7 3.0 copy-start.7
  504.7 3.0 copy-start.11
  504.7 3.7 copy-start.12
  511.0 7.1 %copy-start.26 = (f32[1,768]{1,0:T(1,128)S(1)}, f32[1,768]{1,0:T(1,128)}, u32[]{:S(2)}) copy-start(f32[1,768]{1,0:T(1,128)} %stack.103) | copy-start | bytes 9220
  511.1 94.6 %all-to-all-start = ((bf16[8,128,768]{2,1,0:T(8,128)(2,1)}), bf16[8,128,768]{2,1,0:T(8,128)(2,1)S(1)}, u32[]{:S(2)}, u32[]{:S(2)}) async-start(bf16[8,128,768]{2,1,0:T(8,128)(2,1)} %bitcast.27), calls=%async_computation | async-start | bytes 3145728 | tf_op jit(solution)/shard_map/all_to_all | solution.py:1069
  519.5 3.4 copy-start.16
  522.9 1.9 copy-start.8
  522.9 2.8 copy-start.39
  525.8 1.5 copy-start.20
  599.9 4.7 copy-start.21
  603.5 4.2 copy-start.36
  605.7 5.7 copy-start.1
Sparse Core Ops, SparseCore 0:
  10.2 128.4 all-gather.2
  140.9 77.5 all-gather.4

commit v4 on v3

--- a/solution.py
+++ b/solution.py
@@ -68,77 +68,6 @@
         jnp.where(low_half, pair, other).astype(jnp.bfloat16),
         jnp.where(low_half, other, pair).astype(jnp.bfloat16),
     )
-
-
-def forward_kernel(limit_ref, query_ref, key_ref, value_ref, attended_ref, lse_ref, *, key_rows):
-    low_half = lane_is_low()
-    limit = limit_ref[0]
-    queries = split_query(query_ref[...].astype(jnp.float32), low_half)
-    query_rows = query_ref.shape[0]
-
-    def step(tile, state):
-        start = pl.multiple_of(tile * key_rows, key_rows)
-        usable = start + lax.broadcasted_iota(jnp.int32, (key_rows, 1), 0) < limit
-        key_tile = key_ref[pl.ds(start, key_rows), :].astype(jnp.float32)
-        keys = twice(jnp.where(usable, key_tile, key_ref[0:1, :].astype(jnp.float32)), low_half)
-        value_tile = value_ref[pl.ds(start, key_rows), :].astype(jnp.float32)
-        value_tile = jnp.where(usable, value_tile, 0.0)
-        count = jnp.where(usable, 1.0, 0.0)
-        values = (
-            jnp.where(low_half, value_tile, count).astype(jnp.bfloat16),
-            jnp.where(low_half, count, value_tile).astype(jnp.bfloat16),
-        )
-        fresh = []
-        for head in range(2):
-            top, total = state[head]
-            scores = product(queries[head], keys[head], ((1,), (1,)))
-            new_top = jnp.maximum(top, jnp.max(scores, axis=1, keepdims=True))
-            weights = jnp.exp2(scores - new_top).astype(jnp.bfloat16)
-            total = total * jnp.exp2(top - new_top) + product(weights, values[head], ((1,), (0,)))
-            fresh.append((new_top, total))
-        return tuple(fresh)
-
-    empty = (
-        jnp.full((query_rows, 1), NEG_BIG, jnp.float32),
-        jnp.zeros((query_rows, 128), jnp.float32),
-    )
-    (top_a, total_a), (top_b, total_b) = lax.fori_loop(
-        0, key_ref.shape[0] // key_rows, step, (empty, empty)
-    )
-    mass_a, mass_b = total_a[:, 64:65], total_b[:, 0:1]
-    attended_ref[...] = jnp.where(low_half, total_a / mass_a, total_b / mass_b)
-    lse = jnp.where(low_half, top_a + jnp.log2(mass_a), top_b + jnp.log2(mass_b)).T
-    lse_ref[0, 0:1, :] = lse[0:1, :]
-    lse_ref[0, 1:2, :] = lse[64:65, :]
-
-
-def attend_forward(queries, keys, values, limit):
-    rows, width = queries.shape
-    full = keys.shape[0]
-    pairs = width // 128
-    row_spec = pl.BlockSpec((rows, 128), lambda pair, *_: (0, pair))
-    return pl.pallas_call(
-        functools.partial(forward_kernel, key_rows=FORWARD_KEYS),
-        grid_spec=pltpu.PrefetchScalarGridSpec(
-            num_scalar_prefetch=1,
-            grid=(pairs,),
-            in_specs=[
-                row_spec,
-                pl.BlockSpec((full, 128), lambda pair, *_: (0, pair)),
-                pl.BlockSpec((full, 128), lambda pair, *_: (0, pair)),
-            ],
-            out_specs=[row_spec, pl.BlockSpec((1, 2, rows), lambda pair, *_: (pair, 0, 0))],
-        ),
-        out_shape=[
-            jax.ShapeDtypeStruct((rows, width), jnp.float32),
-            jax.ShapeDtypeStruct((pairs, 2, rows), jnp.float32),
-        ],
-        compiler_params=pltpu.CompilerParams(vmem_limit_bytes=VMEM_BYTES),
-        cost_estimate=pl.CostEstimate(
-            flops=16 * rows * full * width, bytes_accessed=20_000_000, transcendentals=0
-        ),
-        name="attend_forward",
-    )(limit, queries, keys, values)
 
 
 MESH = pl.DeviceIdType.MESH
@@ -212,7 +141,7 @@
 ):
     ctx, group, across, sibling = places()
     own_tok = pltpu.make_async_copy(placed.at[group], tok_stage, local_sem.at[0])
-    own_w = pltpu.make_async_copy(weights.at[ctx], w_stage, local_sem.at[1])
+    own_w = pltpu.make_async_copy(weights, w_stage, local_sem.at[1])
     own_small = pltpu.make_async_copy(small, small_stage, local_sem.at[2])
     own_tok.start()
     own_w.start()
@@ -254,7 +183,7 @@
     own_w.wait()
     own_small.wait()
     put_tok = pltpu.make_async_copy(tok_stage, tokens.at[ctx, group], local_sem.at[0])
-    put_w = pltpu.make_async_copy(w_stage, gathered.at[ctx, group], local_sem.at[1])
+    put_w = pltpu.make_async_copy(w_stage, gathered.at[:, group], local_sem.at[1])
     put_small = pltpu.make_async_copy(small_stage, small_all.at[group], local_sem.at[2])
     put_tok.start()
     put_w.start()
@@ -290,12 +219,10 @@
             {"ctx": sibling},
         )
 
-    put_w.wait()
-    across_copy(0, group).start()
-    sibling_copy(0, group).start()
     put_tok.wait()
     across_copy(1, group).start()
     sibling_copy(1, group).start()
+    put_w.wait()
     put_small.wait()
 
     def arrive(step, carry):
@@ -310,6 +237,9 @@
 
     lax.fori_loop(1, count, arrive, 0)
 
+    across_copy(1, group).wait_recv()
+    relay_copy(1, group).start()
+
     def passed(step, carry):
         origin = lax.rem(group - step + count, count)
         for kind in range(2):
@@ -317,7 +247,10 @@
             relay_copy(kind, origin).start()
         return carry
 
-    lax.fori_loop(0, count, passed, 0)
+    lax.fori_loop(1, count, passed, 0)
+    across_copy(1, group).wait_send()
+    sibling_copy(1, group).wait()
+    relay_copy(1, group).wait()
 
     def finish(step, carry):
         origin = lax.rem(group - step + count, count)
@@ -327,7 +260,7 @@
             relay_copy(kind, origin).wait()
         return carry
 
-    lax.fori_loop(0, count, finish, 0)
+    lax.fori_loop(1, count, finish, 0)
 
     def sent(step, carry):
         peer = lax.rem(group + step, count)
@@ -352,7 +285,7 @@
         ],
         scratch_shapes=[
             pltpu.VMEM((rows, width), jnp.bfloat16),
-            pltpu.VMEM(weights.shape[1:], jnp.bfloat16),
+            pltpu.VMEM((4,) + weights.shape[1:], jnp.bfloat16),
             pltpu.VMEM(small.shape, jnp.bfloat16),
             DMA((3,)),
         ]
@@ -735,6 +668,236 @@
         ),
         name="sum_gradients",
     )(*parts, vectors)
+
+
+class Gather:
+    SCRATCH = 11
+
+    def __init__(self, inner, outer, inner_all, outer_all, scratch, count):
+        self.own, self.all, self.count = (inner, outer), (inner_all, outer_all), count
+        self.stages, self.local = scratch[:2], scratch[2]
+        self.g_send, self.g_recv, self.x_send, self.x_recv = scratch[3:7]
+        self.s_send, self.s_recv, self.r_send, self.r_recv = scratch[7:11]
+        self.ctx, self.group, self.across, self.sibling = places()
+        self.width = outer.shape[-1]
+
+    @staticmethod
+    def scratch(count, rows, width):
+        return [
+            pltpu.VMEM((rows, 4 * width), jnp.bfloat16),
+            pltpu.VMEM((4, rows, width), jnp.bfloat16),
+            DMA((4,)),
+        ] + [DMA((2, count))] * 8
+
+    def columns(self, quarter):
+        return pl.ds(pl.multiple_of(quarter * self.width, self.width), self.width)
+
+    def mine(self, kind):
+        if kind == 0:
+            return self.own[0].at[:, self.columns(self.ctx)]
+        return self.own[1].at[self.ctx]
+
+    def place(self, kind, block, quarter):
+        if kind == 0:
+            return self.all[0].at[block, :, self.columns(quarter)]
+        return self.all[1].at[block, quarter]
+
+    def origin(self, step):
+        return lax.rem(self.group - step + self.count, self.count)
+
+    def group_copy(self, kind, step):
+        return remote(
+            self.mine(kind),
+            self.place(kind, self.group, self.ctx),
+            self.g_send.at[kind, step],
+            self.g_recv.at[kind, step],
+            {"fsdp": lax.rem(self.group + step, self.count)},
+        )
+
+    def pass_on(self, kind, step, quarter, send, recv, target):
+        place = self.place(kind, self.origin(step), quarter)
+        block = self.origin(step)
+        return remote(place, place, send.at[kind, block], recv.at[kind, block], {"ctx": target})
+
+    def across_copy(self, kind, step):
+        return self.pass_on(kind, step, self.ctx, self.x_send, self.x_recv, self.across)
+
+    def sibling_copy(self, kind, step):
+        return self.pass_on(kind, step, self.ctx, self.s_send, self.s_recv, self.sibling)
+
+    def relay_copy(self, kind, step):
+        return self.pass_on(kind, step, self.across, self.r_send, self.r_recv, self.sibling)
+
+    def load(self, kind):
+        return pltpu.make_async_copy(self.own[kind], self.stages[kind], self.local.at[kind])
+
+    def put(self, kind):
+        return pltpu.make_async_copy(
+            self.stages[kind], self.all[kind].at[self.group], self.local.at[2 + kind]
+        )
+
+    def over(self, first, last, body):
+        def one(step, carry):
+            for kind in range(2):
+                body(kind, step)
+            return carry
+
+        if first < last:
+            lax.fori_loop(first, last, one, 0)
+
+    def start(self):
+        for kind in range(2):
+            self.load(kind).start()
+        self.over(1, self.count, lambda kind, step: self.group_copy(kind, step).start())
+        for kind in range(2):
+            self.load(kind).wait()
+            self.put(kind).start()
+
+    def arrive(self, first, last):
+        def body(kind, step):
+            self.group_copy(kind, step).wait_recv()
+            self.across_copy(kind, step).start()
+            self.sibling_copy(kind, step).start()
+
+        self.over(first, last, body)
+
+    def relay(self, first, last):
+        def body(kind, step):
+            self.across_copy(kind, step).wait_recv()
+            self.relay_copy(kind, step).start()
+
+        self.over(first, last, body)
+
+    def finish(self):
+        def body(kind, step):
+            self.group_copy(kind, step).wait_send()
+            self.across_copy(kind, step).wait_send()
+            self.sibling_copy(kind, step).wait()
+            self.relay_copy(kind, step).wait()
+
+        self.over(1, self.count, body)
+        for kind in range(2):
+            self.put(kind).wait()
+
+
+def forward_kernel(
+    limit_ref,
+    query_ref,
+    key_ref,
+    value_ref,
+    inner_ref,
+    outer_ref,
+    attended_ref,
+    lse_ref,
+    inner_all,
+    outer_all,
+    *scratch,
+    key_rows,
+    count,
+    arrivals,
+):
+    pair = pl.program_id(0)
+    pairs = pl.num_programs(0) - 1
+    gather = Gather(inner_ref, outer_ref, inner_all, outer_all, scratch, count)
+    for when, (first, last, relay_first, relay_last) in enumerate(arrivals):
+
+        @pl.when(pair == when)
+        def _():
+            if when == 0:
+                greet(count)
+                gather.start()
+            gather.arrive(first, last)
+            gather.relay(relay_first, relay_last)
+            if when == len(arrivals) - 1:
+                gather.finish()
+
+    @pl.when(pair < pairs)
+    def _():
+        low_half = lane_is_low()
+        limit = limit_ref[0]
+        queries = split_query(query_ref[...].astype(jnp.float32), low_half)
+        query_rows = query_ref.shape[0]
+
+        def step(tile, state):
+            start = pl.multiple_of(tile * key_rows, key_rows)
+            usable = start + lax.broadcasted_iota(jnp.int32, (key_rows, 1), 0) < limit
+            key_tile = key_ref[pl.ds(start, key_rows), :].astype(jnp.float32)
+            keys = twice(jnp.where(usable, key_tile, key_ref[0:1, :].astype(jnp.float32)), low_half)
+            value_tile = value_ref[pl.ds(start, key_rows), :].astype(jnp.float32)
+            value_tile = jnp.where(usable, value_tile, 0.0)
+            count = jnp.where(usable, 1.0, 0.0)
+            values = (
+                jnp.where(low_half, value_tile, count).astype(jnp.bfloat16),
+                jnp.where(low_half, count, value_tile).astype(jnp.bfloat16),
+            )
+            fresh = []
+            for head in range(2):
+                top, total = state[head]
+                scores = product(queries[head], keys[head], ((1,), (1,)))
+                new_top = jnp.maximum(top, jnp.max(scores, axis=1, keepdims=True))
+                weights = jnp.exp2(scores - new_top).astype(jnp.bfloat16)
+                total = total * jnp.exp2(top - new_top) + product(weights, values[head], ((1,), (0,)))
+                fresh.append((new_top, total))
+            return tuple(fresh)
+
+        empty = (
+            jnp.full((query_rows, 1), NEG_BIG, jnp.float32),
+            jnp.zeros((query_rows, 128), jnp.float32),
+        )
+        (top_a, total_a), (top_b, total_b) = lax.fori_loop(
+            0, key_ref.shape[0] // key_rows, step, (empty, empty)
+        )
+        mass_a, mass_b = total_a[:, 64:65], total_b[:, 0:1]
+        attended_ref[...] = jnp.where(low_half, total_a / mass_a, total_b / mass_b)
+        lse = jnp.where(low_half, top_a + jnp.log2(mass_a), top_b + jnp.log2(mass_b)).T
+        lse_ref[0, 0:1, :] = lse[0:1, :]
+        lse_ref[0, 1:2, :] = lse[64:65, :]
+
+
+def attend_forward(queries, keys, values, limit, inner, outer, count):
+    rows, width = queries.shape
+    full = keys.shape[0]
+    pairs = width // 128
+    shard = inner.shape[0]
+    sevenths = (0, 0, 1, 3, 5) + (7,) * (pairs - 3)
+    marks = [1 + (count - 1) * n // 7 for n in sevenths]
+    marks = marks[: pairs + 2]
+    late = [1, 1, 1] + marks[2 : pairs]
+    late = late[: pairs + 1] + [count]
+    arrivals = [
+        (marks[i], marks[i + 1], late[i], late[i + 1]) for i in range(pairs + 1)
+    ]
+    now = lambda pair, *_: (0, jnp.minimum(pair, pairs - 1))
+    row_spec = pl.BlockSpec((rows, 128), now)
+    key_spec = pl.BlockSpec((full, 128), now)
+    return pl.pallas_call(
+        functools.partial(forward_kernel, key_rows=FORWARD_KEYS, count=count, arrivals=arrivals),
+        grid_spec=pltpu.PrefetchScalarGridSpec(
+            num_scalar_prefetch=1,
+            grid=(pairs + 1,),
+            in_specs=[row_spec, key_spec, key_spec, ANY, ANY],
+            out_specs=[
+                row_spec,
+                pl.BlockSpec((1, 2, rows), lambda pair, *_: (jnp.minimum(pair, pairs - 1), 0, 0)),
+                ANY,
+                ANY,
+            ],
+            scratch_shapes=Gather.scratch(count, shard, width),
+        ),
+        out_shape=[
+            jax.ShapeDtypeStruct((rows, width), jnp.float32),
+            jax.ShapeDtypeStruct((pairs, 2, rows), jnp.float32),
+            jax.ShapeDtypeStruct((count, shard, 4 * width), jnp.bfloat16),
+            jax.ShapeDtypeStruct((count, 4, shard, width), jnp.bfloat16),
+        ],
+        compiler_params=pltpu.CompilerParams(
+            collective_id=3, has_side_effects=True, vmem_limit_bytes=VMEM_BYTES
+        ),
+        cost_estimate=pl.CostEstimate(
+            flops=16 * rows * full * width, bytes_accessed=20_000_000, transcendentals=0
+        ),
+        name="attend_forward",
+    )(limit, queries, keys, values, inner, outer)
 
 
 def backward_kernel(
@@ -1003,8 +1166,6 @@
     vectors = jnp.pad(vectors, ((0, 4), (0, 128 - shard)))
     weights = jnp.stack((query_weight, key_weight, value_weight, output_weight))
     tokens, weights, vectors = bring_in(placed, weights, vectors)
-    w_inner = lax.all_gather(inner_weight, "fsdp", axis=0, tiled=True)
-    w_outer = lax.all_gather(outer_weight, "fsdp", axis=0, tiled=True)
     w_query, w_key, w_value, w_output = (weights[i].reshape(width, width) for i in range(4))
     vectors = vectors[:, :12, :shard].astype(jnp.float32)
     b_query, b_value, b_output, gain_one, shift_one, b_outer, gain_two, shift_two = (
@@ -1019,7 +1180,17 @@
     queries = (product(token_rows, w_query, ((1,), (0,))) + b_query).astype(low)
     keys = product(all_rows, w_key, ((1,), (0,))).astype(low)
     values = (product(all_rows, w_value, ((1,), (0,))) + b_value).astype(low)
-    attended, lse = attend_forward(queries, keys, values, limits)
+    attended, lse, w_inner, w_outer = attend_forward(
+        queries,
+        keys,
+        values,
+        limits,
+        inner_weight,
+        outer_weight.reshape(4, shard, width),
+        count,
+    )
+    w_inner = w_inner.reshape(width, 4 * width)
+    w_outer = w_outer.reshape(4 * width, width)
     mixed_low = attended.astype(low)
     branch = product(mixed_low, w_output, ((1,), (0,))) + b_output
     normed, unit_one, scale_one = norm_forward(

time: 628 us -> 589 us (0.938)
  Pallas kernels: 437 us -> 413 us
  between operations: 16.6 us -> 2.96 us
  local copies, waits for them, and re-layouts: 29.5 us -> 35.8 us
    pallas_call x1, Pallas kernels: 144 us -> 94.8 us  [bring_in(): pl.pallas_call(functools.partial(arrival_kernel, count=count), in_specs=[...]
    pallas_call x1, Pallas kernels: 69.3 us -> 94.8 us  [attend_forward(): pl.pallas_call(functools.partial(forward_kernel, key_rows=FORWARD_KEYS, c...]
    pallas_call x1, Pallas kernels: 67.5 us -> 60.5 us  [sum_gradients(): pl.pallas_call(functools.partial(sums_kernel, kinds=kinds, count=count),...]
    pallas_call x1, Pallas kernels: 156 us -> 163 us  [attend_backward(): pl.pallas_call(functools.partial(backward_kernel, count=count), grid_spec...]
    unnamed x91 -> x117, local copies, waits for them, and re-layouts: 9.29 us -> 13.2 us
  transfers between devices with their start and end apart: 3 -> 1, of which waited for: 0 -> 0; matrix products, arithmetic and copies ran while one was open for 12% -> 5% of each run, Pallas kernels for 45% -> 10%
where the time goes in v4:
time: 589 us; the launch traced here: 583 us
  Pallas kernels  413 us (70%)
  matrix products  100 us (17%)
  local copies, waits for them, and re-layouts  35.8 us (6%)
  other arithmetic  24.3 us (4%)
  starting transfers between devices  6.75 us (1%)
    pallas_call x1, Pallas kernels, attend_backward(): pl.pallas_call(functools.partial(backward_kernel, count=count), grid_spec...  163 us
    dot_general x18, matrix products, product(): lax.dot_general(left, right, (dims, ((), ())), preferred_element_type=jnp...  100 us
    pallas_call x1, Pallas kernels, attend_forward(): pl.pallas_call(functools.partial(forward_kernel, key_rows=FORWARD_KEYS, c...  94.8 us
    pallas_call x1, Pallas kernels, bring_in(): pl.pallas_call(functools.partial(arrival_kernel, count=count), in_specs=[...  94.8 us
    pallas_call x1, Pallas kernels, sum_gradients(): pl.pallas_call(functools.partial(sums_kernel, kinds=kinds, count=count),...  60.5 us
    unnamed x117, local copies, waits for them, and re-layouts  13.2 us
  transfers between devices with their start and end apart: 1, of which 0 were waited for; matrix products, arithmetic and copies ran while one was open for 5% of the time, Pallas kernels for 10%

profile of v4, /device:TPU:29, one launch (start us, length us, event | category | flops | bytes accessed | tf_op | source)
XLA Modules:
  0.0 583.3 jit_solution(7743730295295837488)
XLA Ops:
  0.7 1.4 dynamic-slice.4
  4.0 0.8 reshape.145
  4.8 5.0 gather_fusion
  10.9 1.1 pad_maximum_fusion.1.weights
  12.0 94.8 %bring_in.1 = (bf16[4,8,128,768]{3,2,1,0:T(8,128)(2,1)S(1)}, bf16[4,8,96,768]{3,2,1,0:T(8,128)(2,1)S(1)}, bf16[8,16,128]{2,1,0:T(8,128)(2,1)S(1)}) custom-call(bf16[8,128,768]{2,1,0:T(8,128)(2,1)S(1)} %copy_select_fusion.placed, bf16[4,96,768]{2,1,0:T(8,128)(2,1)S(1)} %pad_maximum_fusion.1.weights, bf16[16,128]{1,0:T(8,128)(2,1)S(1)} %pad.4.small), custom_call_target="tpu_custom_call" | custom-call | tf_op jit(solution)/shard_map/bring_in/pallas_call | solution.py:277
  106.8 2.2 copy-done.2
  109.0 2.7 copy-done.3
  111.8 4.2 fusion.27
  117.6 1.7 constant_dynamic-slice_fusion.1
  119.3 10.5 %convolution_convert_fusion.key_ref = bf16[4096,768]{1,0:T(8,128)(2,1)} fusion(bf16[4096,768]{1,0:T(8,128)(2,1)} %bitcast.119, bf16[768,768]{1,0:T(8,128)(2,1)S(1)} %bitcast.131), kind=kOutput, calls=%fused_computation.13 | convolution fusion | flops 4834983936 | bytes 13762560 | tf_op jit(solution)/shard_map/dot_general | solution.py:48
  129.9 7.1 %add_convert_fusion.value_ref = bf16[4096,768]{1,0:T(8,128)(2,1)} fusion(f32[768]{0:T(1024)S(1)} %add.139, bf16[4096,768]{1,0:T(8,128)(2,1)S(1)} %bitcast.122, bf16[768,768]{1,0:T(8,128)(2,1)S(1)} %bitcast.124), kind=kOutput, calls=%fused_computation.12 | convolution fusion | flops 4838129664 | bytes 13765632 | tf_op jit(solution)/shard_map/dot_general | solution.py:48
  137.0 2.5 add_convert_fusion.3.query_ref
  139.5 94.8 %attend_forward.1 = (f32[1024,768]{1,0:T(8,128)}, f32[6,2,1024]{2,1,0:T(2,128)}, bf16[8,96,3072]{2,1,0:T(8,128)(2,1)}, bf16[8,4,96,768]{3,2,1,0:T(8,128)(2,1)}) custom-call(s32[1]{0:T(128)S(6)} %select_n.40.limit_ref, bf16[1024,768]{1,0:T(8,128)(2,1)} %add_convert_fusion.3.query_ref, bf16[4096,768]{1,0:T(8,128)(2,1)} %convolution_convert_fusion.key_ref, ...), custom_call_target="tpu_custom_call" | custom-call | flops 51539607552 | bytes 20000000 | tf_op jit(solution)/shard_map/attend_forward/pallas_call | solution.py:873
  234.3 3.4 fusion.28
  237.8 1.7 copy-done.8
  240.3 11.9 %multiply_convert_fusion = (bf16[1024,3072]{1,0:T(8,128)(2,1)S(1)}, f32[1024,3072]{1,0:T(8,128)}) fusion(f32[3072]{0:T(1024)S(1)} %add.150, bf16[768,3072]{1,0:T(8,128)(2,1)} %bitcast.155, f32[1024,768]{1,0:T(8,128)} %copy-done.8, f32[768]{0:T(1024)S(1)} %add.147, f32[768]{0:T(1024)S(1)} %mul.132, f32[1024]{0:T(1024)S(1)} %add_rsqrt_fusion.1, ...), kind=kOutput, calls=%fused_computation.10 | convolution fusion | flops 4854644736 | bytes 26765312 | tf_op jit(solution)/shard_map/dot_general | solution.py:48
  252.2 10.0 %fusion.29 = (f32[1024]{0:T(1024)S(1)}, f32[1024,768]{1,0:T(8,128)S(1)}) fusion(f32[768]{0:T(1024)S(1)} %add.154, bf16[1024,3072]{1,0:T(8,128)(2,1)S(1)} %get-tuple-element.142, bf16[3072,768]{1,0:T(8,128)(2,1)} %bitcast.159, f32[768]{0:T(1024)S(1)} %add.147, f32[768]{0:T(1024)S(1)} %mul.132, f32[1024]{0:T(1024)S(1)} %add_rsqrt_fusion.1, ...), kind=kOutput, calls=%fused_computation.107 | convolution fusion | flops 4837342208 | bytes 17323008 | tf_op jit(solution)/shard_map/dot_general | solution.py:48
  262.3 1.6 copy-done.4
  264.8 4.1 fusion.14
  268.9 2.9 convert_reduce_fusion.2
  271.8 7.1 %convolution_convert_fusion.1 = bf16[3072,768]{1,0:T(8,128)(2,1)} fusion(bf16[1024,3072]{1,0:T(8,128)(2,1)S(1)} %copy-done.51, f32[1024,768]{1,0:T(8,128)S(1)} %get-tuple-element.120), kind=kOutput, calls=%fused_computation.14 | convolution fusion | flops 4834983936 | bytes 14155776 | tf_op jit(solution)/shard_map/dot_general | solution.py:48
  278.9 12.5 %convert_reduce_fusion = (f32[3072]{0:T(1024)}, bf16[1024,3072]{1,0:T(8,128)(2,1)S(1)}) fusion(f32[1024,3072]{1,0:T(8,128)} %get-tuple-element.143, f32[3072]{0:T(1024)S(1)} %add.150, bf16[3072,768]{1,0:T(8,128)(2,1)S(1)} %bitcast.162, f32[1024,768]{1,0:T(8,128)S(1)} %get-tuple-element.120), kind=kOutput, calls=%fused_computation.9 | convolution fusion | flops 4873516032 | bytes 26763264 | tf_op jit(solution)/shard_map/dot_general | solution.py:48
  291.4 8.3 %convolution_convert_fusion.2 = bf16[768,3072]{1,0:T(8,128)(2,1)} fusion(bf16[1024,3072]{1,0:T(8,128)(2,1)S(1)} %get-tuple-element.148, f32[1024,768]{1,0:T(8,128)S(1)} %copy-done.10, f32[768]{0:T(1024)S(1)} %add.147, f32[768]{0:T(1024)S(1)} %mul.132, f32[1024]{0:T(1024)S(1)} %add_rsqrt_fusion.1, f32[1024]{0:T(1024)S(1)} %broadcast_multiply_fusion.5), kind=kOutput, calls=%fused_computation.15 | convolution fusion | flops 4838129664 | bytes 14170112 | tf_op jit(solution)/shard_map/dot_general | solution.py:48
  299.7 6.5 %multiply_reduce_fusion = (f32[768]{0:T(1024)}, f32[1024]{0:T(1024)S(1)}, f32[1024]{0:T(1024)S(1)}, f32[768]{0:T(1024)}, f32[1024,768]{1,0:T(8,128)S(1)}) fusion(f32[1024,768]{1,0:T(8,128)S(1)} %copy-done.10, f32[1024]{0:T(1024)S(1)} %add_rsqrt_fusion.1, f32[1024]{0:T(1024)S(1)} %broadcast_multiply_fusion.5, f32[768]{0:T(1024)S(1)} %mul.132, ...), kind=kOutput, calls=%fused_computation.29 | convolution fusion | flops 4839698432 | bytes 20472832 | tf_op jit(solution)/shard_map/dot_general | solution.py:48
  306.2 1.7 convert_reduce_fusion.3
  307.9 2.6 convolution_convert_fusion.3.grad_ref
  310.5 163.0 %attend_backward.1 = (bf16[1024,768]{1,0:T(8,128)(2,1)}, bf16[1024,768]{1,0:T(8,128)(2,1)}, bf16[1024,768]{1,0:T(8,128)(2,1)}, bf16[4,96,768]{2,1,0:T(8,128)(2,1)}, bf16[4,96,768]{2,1,0:T(8,128)(2,1)}) custom-call(s32[1]{0:T(128)S(6)} %select_n.40.limit_ref, bf16[1024,768]{1,0:T(8,128)(2,1)} %add_convert_fusion.3.query_ref, ...), custom_call_target="tpu_custom_call" | custom-call | flops 128849018880 | bytes 40000000 | tf_op jit(solution)/shard_map/attend_backward/pallas_call | solution.py:1080
  473.6 3.0 fusion.30
  476.6 1.4 fusion.31
  479.3 2.7 add_convert_fusion.1
  482.0 6.7 %all-to-all-start = ((bf16[8,128,768]{2,1,0:T(8,128)(2,1)}), bf16[8,128,768]{2,1,0:T(8,128)(2,1)S(1)}, u32[]{:S(2)}, u32[]{:S(2)}) async-start(bf16[8,128,768]{2,1,0:T(8,128)(2,1)} %bitcast.30), calls=%async_computation | async-start | bytes 3145728 | tf_op jit(solution)/shard_map/all_to_all | solution.py:1240
  488.7 1.8 convert_reduce_fusion.5
  491.1 2.5 convolution_convert_fusion.7
  493.5 2.5 convolution_convert_fusion.6
  496.0 0.8 copy-done.47
  496.9 2.5 convolution_convert_fusion.4
  499.8 1.3 concatenate.8.refs_1_
  501.1 3.5 convolution_convert_fusion.5
  504.6 2.4 pad_maximum_fusion.refs_0_
  507.1 60.5 %sum_gradients.1 = (bf16[4,96,768]{2,1,0:T(8,128)(2,1)}, f32[16,768]{1,0:T(8,128)}) custom-call(bf16[4,8,96,768]{3,2,1,0:T(8,128)(2,1)} %pad_maximum_fusion.refs_0_, f32[16,768]{1,0:T(8,128)} %concatenate.8.refs_1_), custom_call_target="tpu_custom_call" | custom-call | tf_op jit(solution)/shard_map/sum_gradients/pallas_call | solution.py:659
  569.1 1.2 convert_element_type.128
  570.3 1.2 convert_bitcast_fusion.1
  571.4 1.1 copy.42
  574.5 1.0 slice_bitcast_fusion
  575.5 2.2 bitcast_convert_fusion
  577.7 1.8 gather_fusion.1
  579.4 1.6 select_bitcast_fusion
  581.1 2.0 copy.41
  (165 shorter events, 10.8 us)
Async XLA Ops:
  0.7 4.1 copy-start
  106.8 2.2 copy-start.2
  109.0 2.7 copy-start.3
  111.8 4.4 copy-start.45
  116.0 13.8 %copy-start.15 = (bf16[1,8,96,768]{3,2,1,0:T(8,128)(2,1)}, bf16[1,8,96,768]{3,2,1,0:T(8,128)(2,1)S(1)}, u32[]{:S(2)}) copy-start(bf16[1,8,96,768]{3,2,1,0:T(8,128)(2,1)S(1)} %get-tuple-element.124) | copy-start | bytes 3538948
  117.6 1.7 copy-start.20
  117.6 12.3 %slice-start = ((s8[6291456]{0:T(1024)(128)(4,1)}), s8[4194304]{0:T(1024)(128)(4,1)S(1)}, s32[]{:S(2)}) async-start(s8[6291456]{0:T(1024)(128)(4,1)} %bitcast.120), calls=%async_computation.1 | async-start | bytes 8388608
  119.3 115.0 %copy-start.18 = (bf16[1,8,128,768]{3,2,1,0:T(8,128)(2,1)}, bf16[1,8,128,768]{3,2,1,0:T(8,128)(2,1)S(1)}, u32[]{:S(2)}) copy-start(bf16[1,8,128,768]{3,2,1,0:T(8,128)(2,1)S(1)} %constant_dynamic-slice_fusion.1) | copy-start | bytes 4718596
  119.3 10.6 %slice-start.1 = ((s8[6291456]{0:T(1024)(128)(4,1)}), s8[2097152]{0:T(1024)(128)(4,1)S(1)}, s32[]{:S(2)}) async-start(s8[6291456]{0:T(1024)(128)(4,1)} %bitcast.120), calls=%async_computation.2 | async-start | bytes 4194304
  129.9 7.1 %copy-start.22 = (bf16[1,8,96,768]{3,2,1,0:T(8,128)(2,1)S(1)}, bf16[1,8,96,768]{3,2,1,0:T(8,128)(2,1)}, u32[]{:S(2)}) copy-start(bf16[1,8,96,768]{3,2,1,0:T(8,128)(2,1)} %get-tuple-element.126) | copy-start | bytes 3538948
  139.5 94.8 %copy-start.24 = (bf16[1,8,96,768]{3,2,1,0:T(8,128)(2,1)S(1)}, bf16[1,8,96,768]{3,2,1,0:T(8,128)(2,1)}, u32[]{:S(2)}) copy-start(bf16[1,8,96,768]{3,2,1,0:T(8,128)(2,1)} %get-tuple-element.123) | copy-start | bytes 3538948
  237.7 1.7 copy-start.8
  240.3 11.9 %copy-start.9 = (f32[1024,768]{1,0:T(8,128)S(1)}, f32[1024,768]{1,0:T(8,128)}, u32[]{:S(2)}) copy-start(f32[1024,768]{1,0:T(8,128)} %copy-done.8) | copy-start | bytes 9437188
  252.2 10.1 %copy-start.50 = (bf16[1024,3072]{1,0:T(8,128)(2,1)}, bf16[1024,3072]{1,0:T(8,128)(2,1)S(1)}, u32[]{:S(2)}) copy-start(bf16[1024,3072]{1,0:T(8,128)(2,1)S(1)} %get-tuple-element.142) | copy-start | bytes 18874372
  262.3 2.5 copy-start.6
  264.8 4.1 copy-start.5
  264.8 7.0 %copy-start.51 = (bf16[1024,3072]{1,0:T(8,128)(2,1)S(1)}, bf16[1024,3072]{1,0:T(8,128)(2,1)}, u32[]{:S(2)}) copy-start(bf16[1024,3072]{1,0:T(8,128)(2,1)} %copy-done.50) | copy-start | bytes 18874372
  268.9 10.0 %slice-start.4 = ((s8[4718592]{0:T(1024)(128)(4,1)}), s8[4194304]{0:T(1024)(128)(4,1)S(1)}, s32[]{:S(2)}) async-start(s8[4718592]{0:T(1024)(128)(4,1)} %bitcast.160), calls=%async_computation.5 | async-start | bytes 8388608
  271.8 7.1 %slice-start.5 = ((s8[4718592]{0:T(1024)(128)(4,1)}), s8[524288]{0:T(1024)(128)(4,1)S(1)}, s32[]{:S(2)}) async-start(s8[4718592]{0:T(1024)(128)(4,1)} %bitcast.160), calls=%async_computation.6 | async-start | bytes 1048576
  271.8 27.9 %slice-start.2 = ((s8[4718592]{0:T(1024)(128)(4,1)}), s8[4194304]{0:T(1024)(128)(4,1)S(1)}, s32[]{:S(2)}) async-start(s8[4718592]{0:T(1024)(128)(4,1)} %bitcast.156), calls=%async_computation.3 | async-start | bytes 8388608
  278.9 12.5 %copy-start.10 = (f32[1024,768]{1,0:T(8,128)S(1)}, f32[1024,768]{1,0:T(8,128)}, u32[]{:S(2)}) copy-start(f32[1024,768]{1,0:T(8,128)} %copy-done.8) | copy-start | bytes 9437188
  278.9 20.8 %slice-start.3 = ((s8[4718592]{0:T(1024)(128)(4,1)}), s8[524288]{0:T(1024)(128)(4,1)S(1)}, s32[]{:S(2)}) async-start(s8[4718592]{0:T(1024)(128)(4,1)} %bitcast.156), calls=%async_computation.4 | async-start | bytes 1048576
  306.2 1.7 copy-start.25
  307.9 2.6 copy-start.11
  310.5 163.1 %copy-start.23 = (bf16[1,8,96,768]{3,2,1,0:T(8,128)(2,1)S(1)}, bf16[1,8,96,768]{3,2,1,0:T(8,128)(2,1)}, u32[]{:S(2)}) copy-start(bf16[1,8,96,768]{3,2,1,0:T(8,128)(2,1)} %get-tuple-element.126) | copy-start | bytes 3538948
  473.6 3.0 copy-start.21
  473.6 3.0 copy-start.48
  476.6 1.9 copy-start.12
  476.6 2.3 copy-start.14
  476.6 2.7 copy-start.16
  482.0 95.7 %all-to-all-start = ((bf16[8,128,768]{2,1,0:T(8,128)(2,1)}), bf16[8,128,768]{2,1,0:T(8,128)(2,1)S(1)}, u32[]{:S(2)}, u32[]{:S(2)}) async-start(bf16[8,128,768]{2,1,0:T(8,128)(2,1)} %bitcast.30), calls=%async_computation | async-start | bytes 3145728 | tf_op jit(solution)/shard_map/all_to_all | solution.py:1240
  488.7 2.1 copy-start.17
  488.7 2.3 copy-start.19
  491.1 2.5 copy-start.49
  493.5 2.5 copy-start.13
  493.5 3.3 copy-start.47
  496.8 2.6 copy-start.7
  496.8 2.9 copy-start.33
  496.8 2.9 copy-start.36
  496.8 2.9 copy-start.35
  496.8 2.9 copy-start.34
  496.8 2.9 copy-start.31
  496.9 3.0 copy-start.32
  501.1 3.5 copy-start.26
  501.1 3.5 copy-start.27
  501.1 3.5 copy-start.28
  567.6 5.6 copy-start.46
  577.7 5.4 copy-start.1
  (11 other events, 9.4 us)

commit v5 on v4

--- a/solution.py
+++ b/solution.py
@@ -9,7 +9,7 @@
 
 SCALE = 64 ** (-0.5)
 LOG2E = 1.4426950408889634
-FORWARD_KEYS = 2048
+LAST_SLOT = 12
 VMEM_BYTES = 60 * 2**20
 
 NORM_EPSILON = 1e-12
@@ -111,6 +111,177 @@
             barrier, inc=1, device_id={"ctx": lax.rem(ctx + other, 4)}, device_id_type=MESH
         )
     pl.semaphore_wait(barrier, count - 1 + 3)
+
+
+class Gather:
+    SCRATCH = 11
+
+    def __init__(self, kinds, sems, count):
+        self.kinds, self.count = kinds, count
+        self.right_send, self.left_send, self.line_recv = sems[:3]
+        self.y_send, self.y_recv, self.x_send, self.x_recv = sems[3:7]
+        self.s_send, self.s_recv, self.r_send, self.r_recv = sems[7:11]
+        self.ctx, self.group, self.across, self.sibling = places()
+        self.line, self.side, self.length = self.group // 2, lax.rem(self.group, 2), count // 2
+
+    @staticmethod
+    def scratch(kinds, count):
+        return [DMA((kinds, count))] * Gather.SCRATCH
+
+    def copy(self, kind, block, quarter, send, recv, where, own=False):
+        mine, place = self.kinds[kind]
+        target = place(block, quarter)
+        source = mine(quarter) if own else target
+        return remote(source, target, send.at[kind, block], recv.at[kind, block], where)
+
+    def right(self, kind, block, own=False):
+        there = {"fsdp": lax.rem(self.group + 2, self.count)}
+        return self.copy(kind, block, self.ctx, self.right_send, self.line_recv, there, own)
+
+    def left(self, kind, block, own=False):
+        there = {"fsdp": lax.rem(self.group - 2 + self.count, self.count)}
+        return self.copy(kind, block, self.ctx, self.left_send, self.line_recv, there, own)
+
+    def pair(self, kind, block, own=False):
+        there = {"fsdp": self.group + 1 - 2 * self.side}
+        return self.copy(kind, block, self.ctx, self.y_send, self.y_recv, there, own)
+
+    def cross(self, kind, block):
+        return self.copy(kind, block, self.ctx, self.x_send, self.x_recv, {"ctx": self.across})
+
+    def share(self, kind, block):
+        return self.copy(kind, block, self.ctx, self.s_send, self.s_recv, {"ctx": self.sibling})
+
+    def relay(self, kind, block):
+        return self.copy(kind, block, self.across, self.r_send, self.r_recv, {"ctx": self.sibling})
+
+    def at(self, line, side):
+        return 2 * line + side
+
+    def every(self, body):
+        for kind in range(len(self.kinds)):
+            body(kind)
+
+    def before(self, distance, body):
+        @pl.when(self.line - distance >= 0)
+        def _():
+            body(self.line - distance)
+
+    def after(self, distance, body):
+        @pl.when(self.line + distance < self.length)
+        def _():
+            body(self.line + distance)
+
+    def start(self):
+        block = self.group
+
+        def body(kind):
+            self.after(1, lambda _: self.right(kind, block, True).start())
+            self.before(1, lambda _: self.left(kind, block, True).start())
+            self.pair(kind, block, True).start()
+
+        self.every(body)
+
+    def along(self, distance):
+        def from_left(line):
+            block = self.at(line, self.side)
+
+            def body(kind):
+                self.right(kind, block).wait_recv()
+                self.after(1, lambda _: self.right(kind, block).start())
+                self.pair(kind, block).start()
+                self.cross(kind, block).start()
+                self.share(kind, block).start()
+
+            self.every(body)
+
+        def from_right(line):
+            block = self.at(line, self.side)
+
+            def body(kind):
+                self.left(kind, block).wait_recv()
+                self.before(1, lambda _: self.left(kind, block).start())
+                self.pair(kind, block).start()
+                self.cross(kind, block).start()
+                self.share(kind, block).start()
+
+            self.every(body)
+
+        self.before(distance, from_left)
+        self.after(distance, from_right)
+
+    def both(self, distance, side, body):
+        if isinstance(distance, int) and distance == 0:
+            body(self.at(self.line, side))
+        else:
+            self.before(distance, lambda line: body(self.at(line, side)))
+            self.after(distance, lambda line: body(self.at(line, side)))
+
+    def beside(self, distance):
+        def one(block):
+            def body(kind):
+                self.pair(kind, block).wait_recv()
+                self.cross(kind, block).start()
+                self.share(kind, block).start()
+
+            self.every(body)
+
+        self.both(distance, 1 - self.side, one)
+
+    def crossed(self, distance, side):
+        def one(block):
+            def body(kind):
+                self.cross(kind, block).wait_recv()
+                self.relay(kind, block).start()
+
+            self.every(body)
+
+        self.both(distance, self.side if side == 0 else 1 - self.side, one)
+
+    def finish(self):
+        def passed(block):
+            def body(kind):
+                self.cross(kind, block).wait_send()
+                self.share(kind, block).wait()
+                self.relay(kind, block).wait()
+
+            self.every(body)
+
+        def own(kind):
+            self.after(1, lambda _: self.right(kind, self.group).wait_send())
+            self.before(1, lambda _: self.left(kind, self.group).wait_send())
+            self.pair(kind, self.group).wait_send()
+
+        self.every(own)
+
+        def one(distance, carry):
+            def lefts(line):
+                block = self.at(line, self.side)
+
+                def body(kind):
+                    self.after(1, lambda _: self.right(kind, block).wait_send())
+                    self.pair(kind, block).wait_send()
+
+                self.every(body)
+                passed(block)
+
+            def rights(line):
+                block = self.at(line, self.side)
+
+                def body(kind):
+                    self.before(1, lambda _: self.left(kind, block).wait_send())
+                    self.pair(kind, block).wait_send()
+
+                self.every(body)
+                passed(block)
+
+            self.before(distance, lefts)
+            self.after(distance, rights)
+            self.both(distance, 1 - self.side, passed)
+            return carry
+
+        lax.fori_loop(1, self.length, one, 0)
+        passed(self.at(self.line, 1 - self.side))
 
 
 def arrival_kernel(
@@ -126,8 +297,6 @@
     local_sem,
     tok_send,
     tok_recv,
-    w_send,
-    w_recv,
     small_send,
     small_recv,
     x_send,
@@ -136,10 +305,11 @@
     s_recv,
     r_send,
     r_recv,
-    *,
+    *sems,
     count,
 ):
     ctx, group, across, sibling = places()
+    gather = Gather(((lambda q: weights.at[q], lambda b, q: gathered.at[q, b]),), sems, count)
     own_tok = pltpu.make_async_copy(placed.at[group], tok_stage, local_sem.at[0])
     own_w = pltpu.make_async_copy(weights, w_stage, local_sem.at[1])
     own_small = pltpu.make_async_copy(small, small_stage, local_sem.at[2])
@@ -157,27 +327,31 @@
             {"fsdp": peer},
         )
 
-    def w_copy(peer, step):
-        return remote(
-            weights.at[ctx],
-            gathered.at[ctx, group],
-            w_send.at[step],
-            w_recv.at[step],
-            {"fsdp": peer},
-        )
-
     def small_copy(peer, step):
         return remote(
             small, small_all.at[group], small_send.at[step], small_recv.at[step], {"fsdp": peer}
         )
 
+    def pass_on(block, quarter, send, recv, target):
+        place = tokens.at[quarter, block]
+        return remote(place, place, send.at[block], recv.at[block], {"ctx": target})
+
+    def across_copy(block):
+        return pass_on(block, ctx, x_send, x_recv, across)
+
+    def sibling_copy(block):
+        return pass_on(block, ctx, s_send, s_recv, sibling)
+
+    def relay_copy(block):
+        return pass_on(block, across, r_send, r_recv, sibling)
+
     def send(step, carry):
         peer = lax.rem(group + step, count)
-        w_copy(peer, step).start()
         tok_copy(peer, step).start()
         small_copy(peer, step).start()
         return carry
 
+    gather.start()
     lax.fori_loop(1, count, send, 0)
     own_tok.wait()
     own_w.wait()
@@ -188,83 +362,62 @@
     put_tok.start()
     put_w.start()
     put_small.start()
-
-    def across_copy(kind, block):
-        where = gathered if kind == 0 else tokens
-        return remote(
-            where.at[ctx, block],
-            where.at[ctx, block],
-            x_send.at[kind, block],
-            x_recv.at[kind, block],
-            {"ctx": across},
-        )
-
-    def sibling_copy(kind, block):
-        where = gathered if kind == 0 else tokens
-        return remote(
-            where.at[ctx, block],
-            where.at[ctx, block],
-            s_send.at[kind, block],
-            s_recv.at[kind, block],
-            {"ctx": sibling},
-        )
-
-    def relay_copy(kind, block):
-        where = gathered if kind == 0 else tokens
-        return remote(
-            where.at[across, block],
-            where.at[across, block],
-            r_send.at[kind, block],
-            r_recv.at[kind, block],
-            {"ctx": sibling},
-        )
-
     put_tok.wait()
-    across_copy(1, group).start()
-    sibling_copy(1, group).start()
+    across_copy(group).start()
+    sibling_copy(group).start()
     put_w.wait()
     put_small.wait()
 
     def arrive(step, carry):
         origin = lax.rem(group - step + count, count)
-        w_copy(origin, step).wait_recv()
-        across_copy(0, origin).start()
-        sibling_copy(0, origin).start()
         tok_copy(origin, step).wait_recv()
-        across_copy(1, origin).start()
-        sibling_copy(1, origin).start()
+        across_copy(origin).start()
+        sibling_copy(origin).start()
         return carry
 
-    lax.fori_loop(1, count, arrive, 0)
-
-    across_copy(1, group).wait_recv()
-    relay_copy(1, group).start()
+    length = count // 2
+    gather.along(1)
+    gather.beside(0)
+    lax.fori_loop(1, 3, arrive, 0)
+
+    def advance(distance, carry):
+        gather.along(distance)
+        gather.beside(distance - 1)
+        lax.fori_loop(2 * distance - 1, 2 * distance + 1, arrive, 0)
+        return carry
+
+    lax.fori_loop(2, length, advance, 0)
+    gather.beside(length - 1)
+    lax.fori_loop(2 * length - 1, count, arrive, 0)
+
+    def crossed(distance, carry):
+        gather.crossed(distance, 0)
+        gather.crossed(distance, 1)
+        return carry
+
+    gather.crossed(0, 1)
+    lax.fori_loop(1, length, crossed, 0)
 
     def passed(step, carry):
         origin = lax.rem(group - step + count, count)
-        for kind in range(2):
-            across_copy(kind, origin).wait_recv()
-            relay_copy(kind, origin).start()
+        across_copy(origin).wait_recv()
+        relay_copy(origin).start()
         return carry
 
-    lax.fori_loop(1, count, passed, 0)
-    across_copy(1, group).wait_send()
-    sibling_copy(1, group).wait()
-    relay_copy(1, group).wait()
+    lax.fori_loop(0, count, passed, 0)
+    gather.finish()
 
     def finish(step, carry):
         origin = lax.rem(group - step + count, count)
-        for kind in range(2):
-            across_copy(kind, origin).wait_send()
-            sibling_copy(kind, origin).wait()
-            relay_copy(kind, origin).wait()
+        across_copy(origin).wait_send()
+        sibling_copy(origin).wait()
+        relay_copy(origin).wait()
         return carry
 
-    lax.fori_loop(1, count, finish, 0)
+    lax.fori_loop(0, count, finish, 0)
 
     def sent(step, carry):
         peer = lax.rem(group + step, count)
-        w_copy(peer, step).wait_send()
         tok_copy(peer, step).wait_send()
         small_copy(peer, step).wait()
         return carry
@@ -289,8 +442,8 @@
             pltpu.VMEM(small.shape, jnp.bfloat16),
             DMA((3,)),
         ]
-        + [DMA((count,))] * 6
-        + [DMA((2, count))] * 6,
+        + [DMA((count,))] * 10
+        + Gather.scratch(1, count),
         compiler_params=pltpu.CompilerParams(
             collective_id=0, has_side_effects=True, vmem_limit_bytes=8 * 2**20
         ),
@@ -670,114 +823,26 @@
     )(*parts, vectors)
 
 
-class Gather:
-    SCRATCH = 11
-
-    def __init__(self, inner, outer, inner_all, outer_all, scratch, count):
-        self.own, self.all, self.count = (inner, outer), (inner_all, outer_all), count
-        self.stages, self.local = scratch[:2], scratch[2]
-        self.g_send, self.g_recv, self.x_send, self.x_recv = scratch[3:7]
-        self.s_send, self.s_recv, self.r_send, self.r_recv = scratch[7:11]
-        self.ctx, self.group, self.across, self.sibling = places()
-        self.width = outer.shape[-1]
-
-    @staticmethod
-    def scratch(count, rows, width):
-        return [
-            pltpu.VMEM((rows, 4 * width), jnp.bfloat16),
-            pltpu.VMEM((4, rows, width), jnp.bfloat16),
-            DMA((4,)),
-        ] + [DMA((2, count))] * 8
-
-    def columns(self, quarter):
-        return pl.ds(pl.multiple_of(quarter * self.width, self.width), self.width)
-
-    def mine(self, kind):
-        if kind == 0:
-            return self.own[0].at[:, self.columns(self.ctx)]
-        return self.own[1].at[self.ctx]
-
-    def place(self, kind, block, quarter):
-        if kind == 0:
-            return self.all[0].at[block, :, self.columns(quarter)]
-        return self.all[1].at[block, quarter]
-
-    def origin(self, step):
-        return lax.rem(self.group - step + self.count, self.count)
-
-    def group_copy(self, kind, step):
-        return remote(
-            self.mine(kind),
-            self.place(kind, self.group, self.ctx),
-            self.g_send.at[kind, step],
-            self.g_recv.at[kind, step],
-            {"fsdp": lax.rem(self.group + step, self.count)},
-        )
-
-    def pass_on(self, kind, step, quarter, send, recv, target):
-        place = self.place(kind, self.origin(step), quarter)
-        block = self.origin(step)
-        return remote(place, place, send.at[kind, block], recv.at[kind, block], {"ctx": target})
-
-    def across_copy(self, kind, step):
-        return self.pass_on(kind, step, self.ctx, self.x_send, self.x_recv, self.across)
-
-    def sibling_copy(self, kind, step):
-        return self.pass_on(kind, step, self.ctx, self.s_send, self.s_recv, self.sibling)
-
-    def relay_copy(self, kind, step):
-        return self.pass_on(kind, step, self.across, self.r_send, self.r_recv, self.sibling)
-
-    def load(self, kind):
-        return pltpu.make_async_copy(self.own[kind], self.stages[kind], self.local.at[kind])
-
-    def put(self, kind):
-        return pltpu.make_async_copy(
-            self.stages[kind], self.all[kind].at[self.group], self.local.at[2 + kind]
-        )
-
-    def over(self, first, last, body):
-        def one(step, carry):
-            for kind in range(2):
-                body(kind, step)
-            return carry
-
-        if first < last:
-            lax.fori_loop(first, last, one, 0)
-
-    def start(self):
-        for kind in range(2):
-            self.load(kind).start()
-        self.over(1, self.count, lambda kind, step: self.group_copy(kind, step).start())
-        for kind in range(2):
-            self.load(kind).wait()
-            self.put(kind).start()
-
-    def arrive(self, first, last):
-        def body(kind, step):
-            self.group_copy(kind, step).wait_recv()
-            self.across_copy(kind, step).start()
-            self.sibling_copy(kind, step).start()
-
-        self.over(first, last, body)
-
-    def relay(self, first, last):
-        def body(kind, step):
-            self.across_copy(kind, step).wait_recv()
-            self.relay_copy(kind, step).start()
-
-        self.over(first, last, body)
-
-    def finish(self):
-        def body(kind, step):
-            self.group_copy(kind, step).wait_send()
-            self.across_copy(kind, step).wait_send()
-            self.sibling_copy(kind, step).wait()
-            self.relay_copy(kind, step).wait()
-
-        self.over(1, self.count, body)
-        for kind in range(2):
-            self.put(kind).wait()
+def gather_plan(length):
+    stretch = max(length - 2, 1)
+    slots = [[] for _ in range(LAST_SLOT + 1)]
+
+    def put(name, at, over, first):
+        for distance in range(1, length):
+            slot = min(at + (distance - 1) * over // stretch, LAST_SLOT)
+            events = slots[slot]
+            if events and events[-1][0] == name:
+                events[-1] = (name, events[-1][1], distance + 1)
+            else:
+                events.append((name, distance, distance + 1))
+        if first:
+            slots[first].append((name, 0, 1))
+
+    put("along", 2, 4, 0)
+    put("beside", 5, 3, 2)
+    put("line", 6, 4, 0)
+    put("pair", 8, 4, 6)
+    return slots
 
 
 def forward_kernel(
@@ -794,22 +859,64 @@
     *scratch,
     key_rows,
     count,
-    arrivals,
 ):
     pair = pl.program_id(0)
     pairs = pl.num_programs(0) - 1
-    gather = Gather(inner_ref, outer_ref, inner_all, outer_all, scratch, count)
-    for when, (first, last, relay_first, relay_last) in enumerate(arrivals):
-
-        @pl.when(pair == when)
-        def _():
-            if when == 0:
-                greet(count)
-                gather.start()
-            gather.arrive(first, last)
-            gather.relay(relay_first, relay_last)
-            if when == len(arrivals) - 1:
-                gather.finish()
+    inner_stage, outer_stage, local, *sems = scratch
+    width = outer_ref.shape[-1]
+
+    def columns(quarter):
+        return pl.ds(pl.multiple_of(quarter * width, width), width)
+
+    kinds = (
+        (lambda q: inner_ref.at[:, columns(q)], lambda b, q: inner_all.at[b, :, columns(q)]),
+        (lambda q: outer_ref.at[q], lambda b, q: outer_all.at[b, q]),
+    )
+    gather = Gather(kinds, sems, count)
+    loads = (
+        pltpu.make_async_copy(inner_ref, inner_stage, local.at[0]),
+        pltpu.make_async_copy(outer_ref, outer_stage, local.at[1]),
+    )
+    puts = (
+        pltpu.make_async_copy(inner_stage, inner_all.at[gather.group], local.at[2]),
+        pltpu.make_async_copy(outer_stage, outer_all.at[gather.group], local.at[3]),
+    )
+    plan = gather_plan(count // 2)
+
+    def communicate(events):
+        for name, first, last in events:
+            act = {
+                "along": gather.along,
+                "beside": gather.beside,
+                "line": lambda distance: gather.crossed(distance, 0),
+                "pair": lambda distance: gather.crossed(distance, 1),
+            }[name]
+            if last - first == 1:
+                act(first)
+            else:
+
+                def one(distance, carry, act=act):
+                    act(distance)
+                    return carry
+
+                lax.fori_loop(first, last, one, 0)
+
+    @pl.when(pair == 0)
+    def _():
+        greet(count)
+        for load in loads:
+            load.start()
+        gather.start()
+        for load, put in zip(loads, puts):
+            load.wait()
+            put.start()
+
+    @pl.when(pair == pairs)
+    def _():
+        communicate(plan[LAST_SLOT])
+        gather.finish()
+        for put in puts:
+            put.wait()
 
     @pl.when(pair < pairs)
     def _():
@@ -819,6 +926,13 @@
         query_rows = query_ref.shape[0]
 
         def step(tile, state):
+            for slot in range(1, LAST_SLOT):
+                if plan[slot]:
+
+                    @pl.when(2 * pair + tile == slot)
+                    def _(slot=slot):
+                        communicate(plan[slot])
+
             start = pl.multiple_of(tile * key_rows, key_rows)
             usable = start + lax.broadcasted_iota(jnp.int32, (key_rows, 1), 0) < limit
             key_tile = key_ref[pl.ds(start, key_rows), :].astype(jnp.float32)
@@ -859,19 +973,11 @@
     full = keys.shape[0]
     pairs = width // 128
     shard = inner.shape[0]
-    sevenths = (0, 0, 1, 3, 5) + (7,) * (pairs - 3)
-    marks = [1 + (count - 1) * n // 7 for n in sevenths]
-    marks = marks[: pairs + 2]
-    late = [1, 1, 1] + marks[2 : pairs]
-    late = late[: pairs + 1] + [count]
-    arrivals = [
-        (marks[i], marks[i + 1], late[i], late[i + 1]) for i in range(pairs + 1)
-    ]
     now = lambda pair, *_: (0, jnp.minimum(pair, pairs - 1))
     row_spec = pl.BlockSpec((rows, 128), now)
     key_spec = pl.BlockSpec((full, 128), now)
     return pl.pallas_call(
-        functools.partial(forward_kernel, key_rows=FORWARD_KEYS, count=count, arrivals=arrivals),
+        functools.partial(forward_kernel, key_rows=full // 2, count=count),
         grid_spec=pltpu.PrefetchScalarGridSpec(
             num_scalar_prefetch=1,
             grid=(pairs + 1,),
@@ -882,7 +988,12 @@
                 ANY,
                 ANY,
             ],
-            scratch_shapes=Gather.scratch(count, shard, width),
+            scratch_shapes=[
+                pltpu.VMEM((shard, 4 * width), jnp.bfloat16),
+                pltpu.VMEM((4, shard, width), jnp.bfloat16),
+                DMA((4,)),
+            ]
+            + Gather.scratch(2, count),
         ),
         out_shape=[
             jax.ShapeDtypeStruct((rows, width), jnp.float32),

time: 589 us -> 556 us (0.944)
  Pallas kernels: 413 us -> 381 us
    pallas_call x1, Pallas kernels: 94.8 us -> 74.5 us  [bring_in(): pl.pallas_call(functools.partial(arrival_kernel, count=count), in_specs=[...]
    pallas_call x1, Pallas kernels: 94.8 us -> 87 us  [attend_forward(): pl.pallas_call(functools.partial(forward_kernel, key_rows=full // 2, coun...]
  transfers between devices with their start and end apart: 1 -> 1, of which waited for: 0 -> 0; matrix products, arithmetic and copies ran while one was open for 5% -> 5% of each run, Pallas kernels for 10% -> 11%
where the time goes in v5:
time: 556 us; the launch traced here: 551 us
  Pallas kernels  381 us (69%)
  matrix products  100 us (18%)
  local copies, waits for them, and re-layouts  35.8 us (6%)
  other arithmetic  24.3 us (4%)
  starting transfers between devices  5.94 us (1%)
    pallas_call x1, Pallas kernels, attend_backward(): pl.pallas_call(functools.partial(backward_kernel, count=count), grid_spec...  159 us
    dot_general x18, matrix products, product(): lax.dot_general(left, right, (dims, ((), ())), preferred_element_type=jnp...  100 us
    pallas_call x1, Pallas kernels, attend_forward(): pl.pallas_call(functools.partial(forward_kernel, key_rows=full // 2, coun...  87 us
    pallas_call x1, Pallas kernels, bring_in(): pl.pallas_call(functools.partial(arrival_kernel, count=count), in_specs=[...  74.5 us
    pallas_call x1, Pallas kernels, sum_gradients(): pl.pallas_call(functools.partial(sums_kernel, kinds=kinds, count=count),...  60.5 us
    unnamed x117, local copies, waits for them, and re-layouts  13.2 us
  transfers between devices with their start and end apart: 1, of which 0 were waited for; matrix products, arithmetic and copies ran while one was open for 5% of the time, Pallas kernels for 11%

profile of v5, /device:TPU:29, one launch (start us, length us, event | category | flops | bytes accessed | tf_op | source)
XLA Modules:
  0.0 550.6 jit_solution(15147933410544059781)
XLA Ops:
  0.7 1.4 dynamic-slice.4
  4.0 0.8 reshape.145
  4.8 5.0 gather_fusion
  10.9 1.1 pad_maximum_fusion.1.weights
  12.0 74.5 %bring_in.1 = (bf16[4,8,128,768]{3,2,1,0:T(8,128)(2,1)S(1)}, bf16[4,8,96,768]{3,2,1,0:T(8,128)(2,1)S(1)}, bf16[8,16,128]{2,1,0:T(8,128)(2,1)S(1)}) custom-call(bf16[8,128,768]{2,1,0:T(8,128)(2,1)S(1)} %copy_select_fusion.placed, bf16[4,96,768]{2,1,0:T(8,128)(2,1)S(1)} %pad_maximum_fusion.1.weights, bf16[16,128]{1,0:T(8,128)(2,1)S(1)} %pad.4.small), custom_call_target="tpu_custom_call" | custom-call | tf_op jit(solution)/shard_map/bring_in/pallas_call | solution.py:430
  86.5 2.2 copy-done.2
  88.8 2.7 copy-done.3
  91.6 4.2 fusion.27
  97.4 1.7 constant_dynamic-slice_fusion.1
  99.1 10.5 %convolution_convert_fusion.key_ref = bf16[4096,768]{1,0:T(8,128)(2,1)} fusion(bf16[4096,768]{1,0:T(8,128)(2,1)} %bitcast.119, bf16[768,768]{1,0:T(8,128)(2,1)S(1)} %bitcast.131), kind=kOutput, calls=%fused_computation.13 | convolution fusion | flops 4834983936 | bytes 13762560 | tf_op jit(solution)/shard_map/dot_general | solution.py:48
  109.7 7.1 %add_convert_fusion.value_ref = bf16[4096,768]{1,0:T(8,128)(2,1)} fusion(f32[768]{0:T(1024)S(1)} %add.139, bf16[4096,768]{1,0:T(8,128)(2,1)S(1)} %bitcast.122, bf16[768,768]{1,0:T(8,128)(2,1)S(1)} %bitcast.124), kind=kOutput, calls=%fused_computation.12 | convolution fusion | flops 4838129664 | bytes 13765632 | tf_op jit(solution)/shard_map/dot_general | solution.py:48
  116.8 2.5 add_convert_fusion.3.query_ref
  119.3 87.0 %attend_forward.1 = (f32[1024,768]{1,0:T(8,128)}, f32[6,2,1024]{2,1,0:T(2,128)}, bf16[8,96,3072]{2,1,0:T(8,128)(2,1)}, bf16[8,4,96,768]{3,2,1,0:T(8,128)(2,1)}) custom-call(s32[1]{0:T(128)S(6)} %select_n.40.limit_ref, bf16[1024,768]{1,0:T(8,128)(2,1)} %add_convert_fusion.3.query_ref, bf16[4096,768]{1,0:T(8,128)(2,1)} %convolution_convert_fusion.key_ref, ...), custom_call_target="tpu_custom_call" | custom-call | flops 51539607552 | bytes 20000000 | tf_op jit(solution)/shard_map/attend_forward/pallas_call | solution.py:979
  206.3 3.4 fusion.28
  209.8 1.7 copy-done.8
  212.3 12.0 %multiply_convert_fusion = (bf16[1024,3072]{1,0:T(8,128)(2,1)S(1)}, f32[1024,3072]{1,0:T(8,128)}) fusion(f32[3072]{0:T(1024)S(1)} %add.150, bf16[768,3072]{1,0:T(8,128)(2,1)} %bitcast.155, f32[1024,768]{1,0:T(8,128)} %copy-done.8, f32[768]{0:T(1024)S(1)} %add.147, f32[768]{0:T(1024)S(1)} %mul.132, f32[1024]{0:T(1024)S(1)} %add_rsqrt_fusion.1, ...), kind=kOutput, calls=%fused_computation.10 | convolution fusion | flops 4854644736 | bytes 26765312 | tf_op jit(solution)/shard_map/dot_general | solution.py:48
  224.4 10.0 %fusion.29 = (f32[1024]{0:T(1024)S(1)}, f32[1024,768]{1,0:T(8,128)S(1)}) fusion(f32[768]{0:T(1024)S(1)} %add.154, bf16[1024,3072]{1,0:T(8,128)(2,1)S(1)} %get-tuple-element.142, bf16[3072,768]{1,0:T(8,128)(2,1)} %bitcast.159, f32[768]{0:T(1024)S(1)} %add.147, f32[768]{0:T(1024)S(1)} %mul.132, f32[1024]{0:T(1024)S(1)} %add_rsqrt_fusion.1, ...), kind=kOutput, calls=%fused_computation.107 | convolution fusion | flops 4837342208 | bytes 17323008 | tf_op jit(solution)/shard_map/dot_general | solution.py:48
  234.5 1.6 copy-done.4
  237.0 4.1 fusion.14
  241.1 2.9 convert_reduce_fusion.2
  244.0 7.1 %convolution_convert_fusion.1 = bf16[3072,768]{1,0:T(8,128)(2,1)} fusion(bf16[1024,3072]{1,0:T(8,128)(2,1)S(1)} %copy-done.51, f32[1024,768]{1,0:T(8,128)S(1)} %get-tuple-element.120), kind=kOutput, calls=%fused_computation.14 | convolution fusion | flops 4834983936 | bytes 14155776 | tf_op jit(solution)/shard_map/dot_general | solution.py:48
  251.1 12.5 %convert_reduce_fusion = (f32[3072]{0:T(1024)}, bf16[1024,3072]{1,0:T(8,128)(2,1)S(1)}) fusion(f32[1024,3072]{1,0:T(8,128)} %get-tuple-element.143, f32[3072]{0:T(1024)S(1)} %add.150, bf16[3072,768]{1,0:T(8,128)(2,1)S(1)} %bitcast.162, f32[1024,768]{1,0:T(8,128)S(1)} %get-tuple-element.120), kind=kOutput, calls=%fused_computation.9 | convolution fusion | flops 4873516032 | bytes 26763264 | tf_op jit(solution)/shard_map/dot_general | solution.py:48
  263.5 8.1 %convolution_convert_fusion.2 = bf16[768,3072]{1,0:T(8,128)(2,1)} fusion(bf16[1024,3072]{1,0:T(8,128)(2,1)S(1)} %get-tuple-element.148, f32[1024,768]{1,0:T(8,128)S(1)} %copy-done.10, f32[768]{0:T(1024)S(1)} %add.147, f32[768]{0:T(1024)S(1)} %mul.132, f32[1024]{0:T(1024)S(1)} %add_rsqrt_fusion.1, f32[1024]{0:T(1024)S(1)} %broadcast_multiply_fusion.5), kind=kOutput, calls=%fused_computation.15 | convolution fusion | flops 4838129664 | bytes 14170112 | tf_op jit(solution)/shard_map/dot_general | solution.py:48
  271.7 6.5 %multiply_reduce_fusion = (f32[768]{0:T(1024)}, f32[1024]{0:T(1024)S(1)}, f32[1024]{0:T(1024)S(1)}, f32[768]{0:T(1024)}, f32[1024,768]{1,0:T(8,128)S(1)}) fusion(f32[1024,768]{1,0:T(8,128)S(1)} %copy-done.10, f32[1024]{0:T(1024)S(1)} %add_rsqrt_fusion.1, f32[1024]{0:T(1024)S(1)} %broadcast_multiply_fusion.5, f32[768]{0:T(1024)S(1)} %mul.132, ...), kind=kOutput, calls=%fused_computation.29 | convolution fusion | flops 4839698432 | bytes 20472832 | tf_op jit(solution)/shard_map/dot_general | solution.py:48
  278.2 1.7 convert_reduce_fusion.3
  279.9 2.6 convolution_convert_fusion.3.grad_ref
  282.5 159.2 %attend_backward.1 = (bf16[1024,768]{1,0:T(8,128)(2,1)}, bf16[1024,768]{1,0:T(8,128)(2,1)}, bf16[1024,768]{1,0:T(8,128)(2,1)}, bf16[4,96,768]{2,1,0:T(8,128)(2,1)}, bf16[4,96,768]{2,1,0:T(8,128)(2,1)}) custom-call(s32[1]{0:T(128)S(6)} %select_n.40.limit_ref, bf16[1024,768]{1,0:T(8,128)(2,1)} %add_convert_fusion.3.query_ref, ...), custom_call_target="tpu_custom_call" | custom-call | flops 128849018880 | bytes 40000000 | tf_op jit(solution)/shard_map/attend_backward/pallas_call | solution.py:1191
  441.7 3.0 fusion.30
  444.7 1.4 fusion.31
  447.4 2.7 add_convert_fusion.1
  450.0 5.9 %all-to-all-start = ((bf16[8,128,768]{2,1,0:T(8,128)(2,1)}), bf16[8,128,768]{2,1,0:T(8,128)(2,1)S(1)}, u32[]{:S(2)}, u32[]{:S(2)}) async-start(bf16[8,128,768]{2,1,0:T(8,128)(2,1)} %bitcast.30), calls=%async_computation | async-start | bytes 3145728 | tf_op jit(solution)/shard_map/all_to_all | solution.py:1351
  456.0 1.8 convert_reduce_fusion.5
  458.3 2.5 convolution_convert_fusion.7
  460.8 2.5 convolution_convert_fusion.6
  463.3 0.8 copy-done.47
  464.1 2.5 convolution_convert_fusion.4
  467.1 1.3 concatenate.8.refs_1_
  468.4 3.5 convolution_convert_fusion.5
  471.9 2.4 pad_maximum_fusion.refs_0_
  474.3 60.5 %sum_gradients.1 = (bf16[4,96,768]{2,1,0:T(8,128)(2,1)}, f32[16,768]{1,0:T(8,128)}) custom-call(bf16[4,8,96,768]{3,2,1,0:T(8,128)(2,1)} %pad_maximum_fusion.refs_0_, f32[16,768]{1,0:T(8,128)} %concatenate.8.refs_1_), custom_call_target="tpu_custom_call" | custom-call | tf_op jit(solution)/shard_map/sum_gradients/pallas_call | solution.py:812
  536.4 1.2 convert_element_type.128
  537.6 1.2 convert_bitcast_fusion.1
  538.7 1.1 copy.42
  541.8 1.0 slice_bitcast_fusion
  542.8 2.2 bitcast_convert_fusion
  545.0 1.8 gather_fusion.1
  546.7 1.6 select_bitcast_fusion
  548.4 2.0 copy.41
  (165 shorter events, 10.8 us)
Async XLA Ops:
  0.7 4.1 copy-start
  86.5 2.2 copy-start.2
  88.8 2.7 copy-start.3
  91.6 4.4 copy-start.45
  95.8 13.8 %copy-start.15 = (bf16[1,8,96,768]{3,2,1,0:T(8,128)(2,1)}, bf16[1,8,96,768]{3,2,1,0:T(8,128)(2,1)S(1)}, u32[]{:S(2)}) copy-start(bf16[1,8,96,768]{3,2,1,0:T(8,128)(2,1)S(1)} %get-tuple-element.124) | copy-start | bytes 3538948
  97.4 1.7 copy-start.20
  97.4 12.3 %slice-start = ((s8[6291456]{0:T(1024)(128)(4,1)}), s8[4194304]{0:T(1024)(128)(4,1)S(1)}, s32[]{:S(2)}) async-start(s8[6291456]{0:T(1024)(128)(4,1)} %bitcast.120), calls=%async_computation.1 | async-start | bytes 8388608
  99.1 107.2 %copy-start.18 = (bf16[1,8,128,768]{3,2,1,0:T(8,128)(2,1)}, bf16[1,8,128,768]{3,2,1,0:T(8,128)(2,1)S(1)}, u32[]{:S(2)}) copy-start(bf16[1,8,128,768]{3,2,1,0:T(8,128)(2,1)S(1)} %constant_dynamic-slice_fusion.1) | copy-start | bytes 4718596
  99.1 10.6 %slice-start.1 = ((s8[6291456]{0:T(1024)(128)(4,1)}), s8[2097152]{0:T(1024)(128)(4,1)S(1)}, s32[]{:S(2)}) async-start(s8[6291456]{0:T(1024)(128)(4,1)} %bitcast.120), calls=%async_computation.2 | async-start | bytes 4194304
  109.7 7.1 %copy-start.22 = (bf16[1,8,96,768]{3,2,1,0:T(8,128)(2,1)S(1)}, bf16[1,8,96,768]{3,2,1,0:T(8,128)(2,1)}, u32[]{:S(2)}) copy-start(bf16[1,8,96,768]{3,2,1,0:T(8,128)(2,1)} %get-tuple-element.126) | copy-start | bytes 3538948
  119.3 87.0 %copy-start.24 = (bf16[1,8,96,768]{3,2,1,0:T(8,128)(2,1)S(1)}, bf16[1,8,96,768]{3,2,1,0:T(8,128)(2,1)}, u32[]{:S(2)}) copy-start(bf16[1,8,96,768]{3,2,1,0:T(8,128)(2,1)} %get-tuple-element.123) | copy-start | bytes 3538948
  209.7 1.7 copy-start.8
  212.3 12.1 %copy-start.9 = (f32[1024,768]{1,0:T(8,128)S(1)}, f32[1024,768]{1,0:T(8,128)}, u32[]{:S(2)}) copy-start(f32[1024,768]{1,0:T(8,128)} %copy-done.8) | copy-start | bytes 9437188
  224.4 10.1 %copy-start.50 = (bf16[1024,3072]{1,0:T(8,128)(2,1)}, bf16[1024,3072]{1,0:T(8,128)(2,1)S(1)}, u32[]{:S(2)}) copy-start(bf16[1024,3072]{1,0:T(8,128)(2,1)S(1)} %get-tuple-element.142) | copy-start | bytes 18874372
  234.4 2.5 copy-start.6
  237.0 4.1 copy-start.5
  237.0 7.0 %copy-start.51 = (bf16[1024,3072]{1,0:T(8,128)(2,1)S(1)}, bf16[1024,3072]{1,0:T(8,128)(2,1)}, u32[]{:S(2)}) copy-start(bf16[1024,3072]{1,0:T(8,128)(2,1)} %copy-done.50) | copy-start | bytes 18874372
  241.1 10.0 %slice-start.4 = ((s8[4718592]{0:T(1024)(128)(4,1)}), s8[4194304]{0:T(1024)(128)(4,1)S(1)}, s32[]{:S(2)}) async-start(s8[4718592]{0:T(1024)(128)(4,1)} %bitcast.160), calls=%async_computation.5 | async-start | bytes 8388608
  244.0 7.1 %slice-start.5 = ((s8[4718592]{0:T(1024)(128)(4,1)}), s8[524288]{0:T(1024)(128)(4,1)S(1)}, s32[]{:S(2)}) async-start(s8[4718592]{0:T(1024)(128)(4,1)} %bitcast.160), calls=%async_computation.6 | async-start | bytes 1048576
  244.0 27.7 %slice-start.2 = ((s8[4718592]{0:T(1024)(128)(4,1)}), s8[4194304]{0:T(1024)(128)(4,1)S(1)}, s32[]{:S(2)}) async-start(s8[4718592]{0:T(1024)(128)(4,1)} %bitcast.156), calls=%async_computation.3 | async-start | bytes 8388608
  251.1 12.5 %copy-start.10 = (f32[1024,768]{1,0:T(8,128)S(1)}, f32[1024,768]{1,0:T(8,128)}, u32[]{:S(2)}) copy-start(f32[1024,768]{1,0:T(8,128)} %copy-done.8) | copy-start | bytes 9437188
  251.1 20.6 %slice-start.3 = ((s8[4718592]{0:T(1024)(128)(4,1)}), s8[524288]{0:T(1024)(128)(4,1)S(1)}, s32[]{:S(2)}) async-start(s8[4718592]{0:T(1024)(128)(4,1)} %bitcast.156), calls=%async_computation.4 | async-start | bytes 1048576
  278.2 1.7 copy-start.25
  279.9 2.6 copy-start.11
  282.5 159.2 %copy-start.23 = (bf16[1,8,96,768]{3,2,1,0:T(8,128)(2,1)S(1)}, bf16[1,8,96,768]{3,2,1,0:T(8,128)(2,1)}, u32[]{:S(2)}) copy-start(bf16[1,8,96,768]{3,2,1,0:T(8,128)(2,1)} %get-tuple-element.126) | copy-start | bytes 3538948
  441.6 3.0 copy-start.21
  441.7 3.0 copy-start.48
  444.7 1.9 copy-start.12
  444.7 2.3 copy-start.14
  444.7 2.7 copy-start.16
  450.0 94.9 %all-to-all-start = ((bf16[8,128,768]{2,1,0:T(8,128)(2,1)}), bf16[8,128,768]{2,1,0:T(8,128)(2,1)S(1)}, u32[]{:S(2)}, u32[]{:S(2)}) async-start(bf16[8,128,768]{2,1,0:T(8,128)(2,1)} %bitcast.30), calls=%async_computation | async-start | bytes 3145728 | tf_op jit(solution)/shard_map/all_to_all | solution.py:1351
  456.0 2.1 copy-start.17
  456.0 2.3 copy-start.19
  458.3 2.5 copy-start.49
  460.8 2.5 copy-start.13
  460.8 3.3 copy-start.47
  464.1 2.6 copy-start.7
  464.1 2.9 copy-start.33
  464.1 2.9 copy-start.36
  464.1 2.9 copy-start.35
  464.1 2.9 copy-start.34
  464.1 2.9 copy-start.31
  464.1 3.0 copy-start.32
  468.4 3.5 copy-start.26
  468.4 3.5 copy-start.27
  468.4 3.5 copy-start.28
  534.9 5.6 %copy-start.46 = (s32[8]{0:T(128)S(1)}, s32[8]{0:T(128)}, u32[]{:S(2)}) copy-start(s32[8]{0:T(128)} %param.23) | copy-start | bytes 100
  545.0 5.4 copy-start.1
  (11 other events, 9.4 us)

commit v6 on v5

--- a/solution.py
+++ b/solution.py
@@ -73,6 +73,19 @@
 MESH = pl.DeviceIdType.MESH
 DMA = pltpu.SemaphoreType.DMA
 ANY = pl.BlockSpec(memory_space=pl.ANY)
+SUM_PLAN = {
+    3: ((0, "after_core"),),
+    4: ((1, "after_core"), (2, "after_core")),
+    8: ((0, "after_pair"),),
+    12: ((1, "after_pair"),),
+    13: ((2, "after_pair"),),
+    15: ((0, "after_line"),),
+    18: ((0, "after_across"),),
+    19: ((1, "after_line"),),
+    20: ((2, "after_line"),),
+    22: ((1, "after_across"),),
+    23: ((2, "after_across"),),
+}
 STAGES = ("start", "after_core", "after_across", "after_group", "finish")
 
 
@@ -454,8 +467,8 @@
 class Sum:
     SCRATCH = 16
 
-    def __init__(self, kind, ref, out, scratch, count):
-        self.kind, self.ref, self.out, self.count = kind, ref, out, count
+    def __init__(self, ref, out, scratch, count):
+        self.ref, self.out, self.count = ref, out, count
         self.near, self.far, self.got_near, self.got_far = scratch[:4]
         self.got_across, self.got_group, self.done = scratch[4:7]
         self.load, self.c_send, self.c_recv, self.x_send, self.x_recv = scratch[7:12]
@@ -474,12 +487,8 @@
         )
 
     def quarter(self, index):
-        if self.kind == 0:
-            return self.ref.at[index]
-        if self.kind == 1:
-            start = pl.multiple_of(index * self.width, self.width)
-            return self.ref.at[:, :, pl.ds(start, self.width)]
-        return self.ref.at[:, index]
+        start = pl.multiple_of(lax.rem(index, 2) * self.width, self.width)
+        return self.ref.at[:, index // 2, :, pl.ds(start, self.width)]
 
     def loads(self):
         return (
@@ -674,54 +683,64 @@
 
 
 class LateSum:
-    SCRATCH = 16
-
-    def __init__(self, kind, ref, out, scratch, count):
-        self.kind, self.ref, self.out, self.count = kind, ref, out, count
-        self.near, self.got, self.got_group, self.half, self.got_across, self.done = scratch[:6]
-        self.load, self.c_send, self.c_recv, self.g_send, self.g_recv = scratch[6:11]
-        self.x_send, self.x_recv, self.o_send, self.o_recv, self.put = scratch[11:16]
+    SCRATCH = 19
+
+    def __init__(self, view, out, scratch, count):
+        self.view, self.out, self.count = view, out, count
+        self.near, self.got, self.got_pair, self.got_line = scratch[:4]
+        self.half, self.got_across, self.done = scratch[4:7]
+        self.load, self.c_send, self.c_recv, self.p_send, self.p_recv = scratch[7:12]
+        self.l_send, self.l_recv, self.x_send, self.x_recv = scratch[12:16]
+        self.o_send, self.o_recv, self.put = scratch[16:19]
         self.ctx, self.group, self.across, self.sibling = places()
         self.core = lax.rem(self.ctx, 2)
-        self.width = self.near.shape[-1]
+        self.line, self.side, self.length = self.group // 2, lax.rem(self.group, 2), count // 2
+        self.halves = self.half.shape[0]
 
     @staticmethod
-    def scratch(count, rows, width):
+    def scratch(count, halves, rows, width):
+        def block(*lead):
+            return pltpu.VMEM(lead + (halves, rows, width), jnp.bfloat16)
+
         return (
-            [pltpu.VMEM((count, 2, rows, width), jnp.bfloat16)] * 3
-            + [pltpu.VMEM((2, rows, width), jnp.bfloat16)] * 3
-            + [DMA((2,))] * 3
-            + [DMA((count,))] * 2
-            + [DMA((2,))] * 5
-        )
-
-    def quarter(self, index):
-        if self.kind == 1:
-            start = pl.multiple_of(index * self.width, self.width)
-            return self.ref.at[:, :, pl.ds(start, self.width)]
-        return self.ref.at[:, index]
+            [block(count), block(count), block(count // 2), block(count // 2)]
+            + [block(), block(), block()]
+            + [DMA((halves,))] * 3
+            + [DMA((count // 2,))] * 4
+            + [DMA((1,))] * 2
+            + [DMA((halves,))] * 3
+        )
 
     def load_copy(self, half):
         return pltpu.make_async_copy(
-            self.quarter(2 * half + self.core), self.near.at[:, half], self.load.at[half]
+            self.view(2 * half + self.core), self.near.at[:, half], self.load.at[half]
         )
 
     def core_copy(self, half):
         return remote(
-            self.quarter(2 * half + 1 - self.core),
+            self.view(2 * half + 1 - self.core),
             self.got.at[:, half],
             self.c_send.at[half],
             self.c_recv.at[half],
             {"ctx": self.sibling},
         )
 
-    def group_copy(self, step):
-        peer = lax.rem(self.group + step, self.count)
+    def pair_copy(self, line):
+        return remote(
+            self.near.at[2 * line + 1 - self.side],
+            self.got_pair.at[line],
+            self.p_send.at[line],
+            self.p_recv.at[line],
+            {"fsdp": self.group + 1 - 2 * self.side},
+        )
+
+    def line_copy(self, step):
+        peer = 2 * lax.rem(self.line + step, self.length) + self.side
         return remote(
             self.near.at[peer],
-            self.got_group.at[step],
-            self.g_send.at[step],
-            self.g_recv.at[step],
+            self.got_line.at[step],
+            self.l_send.at[step],
+            self.l_recv.at[step],
             {"fsdp": peer},
         )
 
@@ -744,36 +763,54 @@
             self.done.at[half], self.out.at[2 * half + self.core], self.put.at[half]
         )
 
+    def add(self, block, other):
+        both = self.near[block].astype(jnp.float32) + other.astype(jnp.float32)
+        self.near[block] = both.astype(jnp.bfloat16)
+
     def start(self):
-        for half in range(2):
+        for half in range(self.halves):
             self.load_copy(half).start()
             self.core_copy(half).start()
 
     def after_core(self):
-        for half in range(2):
+        for half in range(self.halves):
             self.load_copy(half).wait()
             self.core_copy(half).wait()
 
+        def theirs(step, carry):
+            line = lax.rem(self.line + step, self.length)
+            block = 2 * line + 1 - self.side
+            self.add(block, self.got[block])
+            self.pair_copy(line).start()
+            return carry
+
+        lax.fori_loop(0, self.length, theirs, 0)
+
+        def mine(line, carry):
+            block = 2 * line + self.side
+            self.add(block, self.got[block])
+            return carry
+
+        lax.fori_loop(0, self.length, mine, 0)
+
+    def after_pair(self):
         def one(step, carry):
-            block = lax.rem(self.group + step, self.count)
-            both = self.near[block].astype(jnp.float32) + self.got[block].astype(jnp.float32)
-            self.near[block] = both.astype(jnp.bfloat16)
+            line = lax.rem(self.line + step, self.length)
+            self.pair_copy(line).wait()
+            self.add(2 * line + self.side, self.got_pair[line])
+            self.line_copy(step).start()
             return carry
 
-        lax.fori_loop(0, self.count, one, 0)
-
-        def send(step, carry):
-            self.group_copy(step).start()
-            return carry
-
-        lax.fori_loop(1, self.count, send, 0)
-
-    def after_group(self):
+        lax.fori_loop(1, self.length, one, 0)
+        self.pair_copy(self.line).wait()
+        self.add(self.group, self.got_pair[self.line])
+
+    def after_line(self):
         def one(step, total):
-            self.group_copy(step).wait()
-            return total + self.got_group[step].astype(jnp.float32)
-
-        total = lax.fori_loop(1, self.count, one, self.near[self.group].astype(jnp.float32))
+            self.line_copy(step).wait()
+            return total + self.got_line[step].astype(jnp.float32)
+
+        total = lax.fori_loop(1, self.length, one, self.near[self.group].astype(jnp.float32))
         self.half[...] = total.astype(jnp.bfloat16)
         self.x_copy().start()
 
@@ -781,39 +818,40 @@
         self.x_copy().wait()
         both = self.half[...].astype(jnp.float32) + self.got_across[...].astype(jnp.float32)
         self.done[...] = both.astype(jnp.bfloat16)
-        for half in range(2):
+        for half in range(self.halves):
             self.own_out(half).start()
             self.out_copy(half).start()
 
     def finish(self):
-        for half in range(2):
+        for half in range(self.halves):
             self.own_out(half).wait()
             self.out_copy(half).wait()
 
 
-def sums_kernel(*refs, kinds, count):
-    parts = len(kinds)
+def sums_kernel(*refs, parts, count):
     ins, outs, rest = refs[: parts + 1], refs[parts + 1 : 2 * parts + 2], refs[2 * parts + 2 :]
     jobs = [VectorSum(ins[parts], outs[parts], rest[: VectorSum.SCRATCH], count)]
     rest = rest[VectorSum.SCRATCH :]
-    for index, kind in enumerate(kinds):
+    for index in range(parts):
         own = rest[index * Sum.SCRATCH : (index + 1) * Sum.SCRATCH]
-        jobs.append(Sum(kind, ins[index], outs[index], own, count))
+        jobs.append(Sum(ins[index], outs[index], own, count))
     greet(count)
     for stage in STAGES:
         for job in jobs:
             getattr(job, stage)()
 
 
-def sum_gradients(parts, kinds, vectors, rows, width, count):
+def sum_gradients(parts, vectors):
+    count, _, rows, width = parts[0].shape
+    width = width // 2
     scratch = VectorSum.scratch(count, *vectors.shape)
-    for _ in kinds:
+    for _ in parts:
         scratch += Sum.scratch(count, rows, width)
     return pl.pallas_call(
-        functools.partial(sums_kernel, kinds=kinds, count=count),
-        in_specs=[ANY] * (len(kinds) + 1),
-        out_specs=[ANY] * (len(kinds) + 1),
-        out_shape=[jax.ShapeDtypeStruct((4, rows, width), jnp.bfloat16)] * len(kinds)
+        functools.partial(sums_kernel, parts=len(parts), count=count),
+        in_specs=[ANY] * (len(parts) + 1),
+        out_specs=[ANY] * (len(parts) + 1),
+        out_shape=[jax.ShapeDtypeStruct((4, rows, width), jnp.bfloat16)] * len(parts)
         + [jax.ShapeDtypeStruct(vectors.shape, jnp.float32)],
         scratch_shapes=scratch,
         compiler_params=pltpu.CompilerParams(
@@ -1021,11 +1059,13 @@
     lse_ref,
     inner_ref,
     outer_ref,
+    output_ref,
     d_query_ref,
     d_key_ref,
     d_value_ref,
     inner_out,
     outer_out,
+    output_out,
     query_sum,
     part,
     got_core,
@@ -1044,9 +1084,16 @@
     slot = lax.rem(pair, 2)
     ctx, _, across, sibling = places()
     key_rows = query_ref.shape[0]
+    def columns(ref, parts):
+        size = ref.shape[2] // parts
+        return lambda index: ref.at[:, :, pl.ds(pl.multiple_of(index * size, size), size)]
+
+    views = (columns(inner_ref, 4), lambda index: outer_ref.at[:, index], columns(output_ref, 2))
     jobs = [
-        LateSum(1, inner_ref, inner_out, rest[: LateSum.SCRATCH], count),
-        LateSum(2, outer_ref, outer_out, rest[LateSum.SCRATCH :], count),
+        LateSum(
+            view, out, rest[index * LateSum.SCRATCH : (index + 1) * LateSum.SCRATCH], count
+        )
+        for index, (view, out) in enumerate(zip(views, (inner_out, outer_out, output_out)))
     ]
 
     def core_copy(which):
@@ -1075,11 +1122,6 @@
         greet(count)
         for job in jobs:
             job.start()
-
-    @pl.when(pair == 1)
-    def _():
-        for job in jobs:
-            job.after_core()
 
     @pl.when(pair < pairs)
     def _():
@@ -1109,6 +1151,13 @@
         query_sum[...] = jnp.zeros_like(query_sum)
 
         def step(tile, carry):
+            for at, stages in SUM_PLAN.items():
+
+                @pl.when(4 * pair + tile == at)
+                def _(stages=stages):
+                    for index, stage in stages:
+                        getattr(jobs[index], stage)()
+
             odd = lax.rem(tile, 2)
             quarter = lax.rem(sibling + odd * (ctx - sibling) + 2 * (1 - tile // 2), 4)
             start = pl.multiple_of(quarter * key_rows, key_rows)
@@ -1168,20 +1217,16 @@
 
     @pl.when(pair == pairs)
     def _():
-        for job in jobs:
-            job.after_group()
         settle()
         for job in jobs:
-            job.after_across()
-        for job in jobs:
             job.finish()
 
 
-def attend_backward(queries, keys, values, limit, grad_rows, attended, lse, inner_part, outer_part):
+def attend_backward(queries, keys, values, limit, grad_rows, attended, lse, parts):
     rows, width = queries.shape
     full = keys.shape[0]
     pairs = width // 128
-    count, shard = inner_part.shape[:2]
+    count, shard = parts[0].shape[:2]
     now = lambda pair, *_: (0, jnp.minimum(pair, pairs - 1))
     before = lambda pair, *_: (0, jnp.maximum(pair - 1, 0))
     row_spec = pl.BlockSpec((rows, 128), now)
@@ -1202,8 +1247,9 @@
                 pl.BlockSpec((1, 2, rows), lambda pair, *_: (jnp.minimum(pair, pairs - 1), 0, 0)),
                 ANY,
                 ANY,
+                ANY,
             ],
-            out_specs=[row_spec, sum_spec, sum_spec, ANY, ANY],
+            out_specs=[row_spec, sum_spec, sum_spec, ANY, ANY, ANY],
             scratch_shapes=[
                 pltpu.VMEM((128, rows), jnp.float32),
                 pltpu.VMEM((2,) + tile, jnp.bfloat16),
@@ -1216,10 +1262,12 @@
                 DMA((2,)),
                 DMA((2,)),
             ]
-            + LateSum.scratch(count, shard, width) * 2,
+            + LateSum.scratch(count, 2, shard, width) * 2
+            + LateSum.scratch(count, 1, shard, width // 2),
         ),
         out_shape=[jax.ShapeDtypeStruct((rows, width), jnp.bfloat16)] * 3
-        + [jax.ShapeDtypeStruct((4, shard, width), jnp.bfloat16)] * 2,
+        + [jax.ShapeDtypeStruct((4, shard, width), jnp.bfloat16)] * 2
+        + [jax.ShapeDtypeStruct((2, shard, width // 2), jnp.bfloat16)],
         compiler_params=pltpu.CompilerParams(
             collective_id=2, has_side_effects=True, vmem_limit_bytes=VMEM_BYTES
         ),
@@ -1227,7 +1275,7 @@
             flops=40 * rows * full * width, bytes_accessed=40_000_000, transcendentals=0
         ),
         name="attend_backward",
-    )(limit, queries, keys, values, grad_rows, attended, lse, inner_part, outer_part)
+    )(limit, queries, keys, values, grad_rows, attended, lse, *parts)
 
 
 def on_device(
@@ -1256,7 +1304,7 @@
     group = lax.axis_index("fsdp")
     shard = query_bias.shape[0]
     low = jnp.bfloat16
-    placed = jnp.swapaxes(jnp.take(hidden_in, seq_order, axis=1), 0, 1)
+    placed = jnp.swapaxes(hidden_in.at[:, seq_order].get(mode="promise_in_bounds"), 0, 1)
     vectors = jnp.concatenate(
         (
             jnp.stack(
@@ -1328,7 +1376,7 @@
     grad_output_w = product(mixed_low, d_branch, ((0,), (0,))).astype(low)
     grad_output_b = jnp.sum(d_branch.astype(jnp.float32), axis=0)
     d_mixed = product(d_branch, w_output, ((1,), (1,))).astype(low)
-    d_query, d_keys, d_values, inner_w, outer_w = attend_backward(
+    d_query, d_keys, d_values, inner_w, outer_w, output_w = attend_backward(
         queries,
         keys,
         values,
@@ -1336,8 +1384,11 @@
         d_mixed,
         attended,
         lse,
-        grad_inner_w.reshape(count, shard, 4 * width),
-        grad_outer_w.reshape(count, 4, shard, width),
+        (
+            grad_inner_w.reshape(count, shard, 4 * width),
+            grad_outer_w.reshape(count, 4, shard, width),
+            grad_output_w.reshape(count, shard, width),
+        ),
     )
     grad_query_w = product(token_rows, d_query, ((0,), (0,))).astype(low)
     grad_query_b = jnp.sum(d_query.astype(jnp.float32), axis=0)
@@ -1350,8 +1401,7 @@
     back_rows = d_placed.astype(low).reshape(count, local_len // count, width)
     returned = lax.all_to_all(back_rows, "fsdp", split_axis=0, concat_axis=0, tiled=True)
     inverse = jnp.argmax(seq_order[:, None] == jnp.arange(count), axis=0)
-    grad_in = jnp.take(jnp.swapaxes(returned, 0, 1), inverse, axis=1)
-    attention_w = jnp.stack((grad_query_w, grad_key_w, grad_value_w, grad_output_w))
+    grad_in = jnp.swapaxes(returned, 0, 1).at[:, inverse].get(mode="promise_in_bounds")
     small_sums = jnp.concatenate(
         (
             jnp.stack(
@@ -1370,15 +1420,20 @@
             jnp.zeros((4, width), jnp.float32),
         )
     )
-    attention_w, small_sums = sum_gradients(
-        (attention_w.reshape(4, count, shard, width),),
-        (0,),
+    *attention_w, small_sums = sum_gradients(
+        [
+            part.reshape(count, 2, shard // 2, width)
+            for part in (grad_query_w, grad_key_w, grad_value_w)
+        ],
         small_sums,
-        shard,
-        width,
-        count,
-    )
-    attention_w = attention_w.astype(jnp.float32)
+    )
+    attention_w = [
+        jnp.swapaxes(part.reshape(2, 2, shard // 2, width // 2), 1, 2)
+        .reshape(shard, width)
+        .astype(jnp.float32)
+        for part in attention_w
+    ]
+    output_w = jnp.swapaxes(output_w, 0, 1).reshape(shard, width).astype(jnp.float32)
     inner_w = jnp.swapaxes(inner_w, 0, 1).reshape(shard, 4 * width).astype(jnp.float32)
     outer_w = outer_w.reshape(4 * shard, width).astype(jnp.float32)
     small = lax.dynamic_slice_in_dim(small_sums[:8], group * shard, shard, axis=1)
@@ -1393,7 +1448,7 @@
         attention_w[1],
         attention_w[2],
         small[1],
-        attention_w[3],
+        output_w,
         small[2],
         small[3],
         small[4],

time: 556 us -> 540 us (0.971)
  Pallas kernels: 381 us -> 361 us
    pallas_call x1, Pallas kernels: 159 us -> 146 us  [attend_backward(): pl.pallas_call(functools.partial(backward_kernel, count=count), grid_spec...]
    pallas_call x1, Pallas kernels: 60.5 us -> 54.2 us  [sum_gradients(): pl.pallas_call(functools.partial(sums_kernel, parts=len(parts), count=cou...]
    unnamed x117 -> x120, local copies, waits for them, and re-layouts: 13.2 us -> 16.2 us
  transfers between devices with their start and end apart: 1 -> 1, of which waited for: 0 -> 0; matrix products, arithmetic and copies ran while one was open for 5% -> 5% of each run, Pallas kernels for 11% -> 10%
where the time goes in v6:
time: 540 us; the launch traced here: 532 us
  Pallas kernels  361 us (67%)
  matrix products  101 us (19%)
  local copies, waits for them, and re-layouts  38.7 us (7%)
  other arithmetic  21.1 us (4%)
  starting transfers between devices  6.94 us (1%)
    pallas_call x1, Pallas kernels, attend_backward(): pl.pallas_call(functools.partial(backward_kernel, count=count), grid_spec...  146 us
    dot_general x18, matrix products, product(): lax.dot_general(left, right, (dims, ((), ())), preferred_element_type=jnp...  101 us
    pallas_call x1, Pallas kernels, attend_forward(): pl.pallas_call(functools.partial(forward_kernel, key_rows=full // 2, coun...  87 us
    pallas_call x1, Pallas kernels, bring_in(): pl.pallas_call(functools.partial(arrival_kernel, count=count), in_specs=[...  74.5 us
    pallas_call x1, Pallas kernels, sum_gradients(): pl.pallas_call(functools.partial(sums_kernel, parts=len(parts), count=cou...  54.2 us
    unnamed x120, local copies, waits for them, and re-layouts  16.2 us
  transfers between devices with their start and end apart: 1, of which 0 were waited for; matrix products, arithmetic and copies ran while one was open for 5% of the time, Pallas kernels for 10%

profile of v6, /device:TPU:29, one launch (start us, length us, event | category | flops | bytes accessed | tf_op | source)
XLA Modules:
  0.0 531.9 jit_solution(517784914962237222)
XLA Ops:
  0.7 1.4 dynamic-slice.4
  3.4 5.0 gather_fusion
  9.5 1.1 pad_maximum_fusion.weights
  10.6 74.5 %bring_in.1 = (bf16[4,8,128,768]{3,2,1,0:T(8,128)(2,1)S(1)}, bf16[4,8,96,768]{3,2,1,0:T(8,128)(2,1)S(1)}, bf16[8,16,128]{2,1,0:T(8,128)(2,1)S(1)}) custom-call(bf16[8,128,768]{2,1,0:T(8,128)(2,1)S(1)} %copy.46.placed, bf16[4,96,768]{2,1,0:T(8,128)(2,1)S(1)} %pad_maximum_fusion.weights, bf16[16,128]{1,0:T(8,128)(2,1)S(1)} %pad.4.small), custom_call_target="tpu_custom_call" | custom-call | tf_op jit(solution)/shard_map/bring_in/pallas_call | solution.py:443
  85.1 2.2 copy-done.2
  87.3 2.7 copy-done.3
  90.2 4.2 fusion.27
  94.6 0.7 dynamic-slice.5
  96.0 1.7 constant_dynamic-slice_fusion.1
  97.7 10.5 %convolution_convert_fusion.key_ref = bf16[4096,768]{1,0:T(8,128)(2,1)} fusion(bf16[4096,768]{1,0:T(8,128)(2,1)} %bitcast.132, bf16[768,768]{1,0:T(8,128)(2,1)S(1)} %bitcast.146), kind=kOutput, calls=%fused_computation.13 | convolution fusion | flops 4834983936 | bytes 13762560 | tf_op jit(solution)/shard_map/dot_general | solution.py:48
  108.3 7.1 %add_convert_fusion.value_ref = bf16[4096,768]{1,0:T(8,128)(2,1)} fusion(f32[768]{0:T(1024)S(1)} %add.143, bf16[4096,768]{1,0:T(8,128)(2,1)S(1)} %bitcast.135, bf16[768,768]{1,0:T(8,128)(2,1)S(1)} %bitcast.139), kind=kOutput, calls=%fused_computation.12 | convolution fusion | flops 4838129664 | bytes 13765632 | tf_op jit(solution)/shard_map/dot_general | solution.py:48
  115.4 2.5 add_convert_fusion.3.query_ref
  117.9 87.0 %attend_forward.1 = (f32[1024,768]{1,0:T(8,128)}, f32[6,2,1024]{2,1,0:T(2,128)}, bf16[8,96,3072]{2,1,0:T(8,128)(2,1)}, bf16[8,4,96,768]{3,2,1,0:T(8,128)(2,1)}) custom-call(s32[1]{0:T(128)S(6)} %select_n.40.limit_ref, bf16[1024,768]{1,0:T(8,128)(2,1)} %add_convert_fusion.3.query_ref, bf16[4096,768]{1,0:T(8,128)(2,1)} %convolution_convert_fusion.key_ref, ...), custom_call_target="tpu_custom_call" | custom-call | flops 51539607552 | bytes 20000000 | tf_op jit(solution)/shard_map/attend_forward/pallas_call | solution.py:1017
  204.9 3.4 fusion.28
  208.3 1.7 copy-done.8
  210.9 12.1 %multiply_convert_fusion = (bf16[1024,3072]{1,0:T(8,128)(2,1)S(1)}, f32[1024,3072]{1,0:T(8,128)}) fusion(f32[3072]{0:T(1024)S(1)} %add.154, bf16[768,3072]{1,0:T(8,128)(2,1)} %bitcast.179, f32[1024,768]{1,0:T(8,128)} %copy-done.8, f32[768]{0:T(1024)S(1)} %add.151, f32[768]{0:T(1024)S(1)} %mul.132, f32[1024]{0:T(1024)S(1)} %add_rsqrt_fusion.1, ...), kind=kOutput, calls=%fused_computation.10 | convolution fusion | flops 4854644736 | bytes 26765312 | tf_op jit(solution)/shard_map/dot_general | solution.py:48
  223.0 10.0 %fusion.29 = (f32[1024]{0:T(1024)S(1)}, f32[1024,768]{1,0:T(8,128)S(1)}) fusion(f32[768]{0:T(1024)S(1)} %add.158, bf16[1024,3072]{1,0:T(8,128)(2,1)S(1)} %get-tuple-element.143, bf16[3072,768]{1,0:T(8,128)(2,1)} %bitcast.183, f32[768]{0:T(1024)S(1)} %add.151, f32[768]{0:T(1024)S(1)} %mul.132, f32[1024]{0:T(1024)S(1)} %add_rsqrt_fusion.1, ...), kind=kOutput, calls=%fused_computation.102 | convolution fusion | flops 4837342208 | bytes 17323008 | tf_op jit(solution)/shard_map/dot_general | solution.py:48
  233.1 1.6 copy-done.4
  235.6 4.1 fusion.14
  239.7 2.9 convert_reduce_fusion.2
  242.6 7.1 %convolution_convert_fusion.1 = bf16[3072,768]{1,0:T(8,128)(2,1)} fusion(bf16[1024,3072]{1,0:T(8,128)(2,1)S(1)} %copy-done.51, f32[1024,768]{1,0:T(8,128)S(1)} %get-tuple-element.125), kind=kOutput, calls=%fused_computation.14 | convolution fusion | flops 4834983936 | bytes 14155776 | tf_op jit(solution)/shard_map/dot_general | solution.py:48
  249.7 12.6 %convert_reduce_fusion = (f32[3072]{0:T(1024)}, bf16[1024,3072]{1,0:T(8,128)(2,1)S(1)}) fusion(f32[1024,3072]{1,0:T(8,128)} %get-tuple-element.144, f32[3072]{0:T(1024)S(1)} %add.154, bf16[3072,768]{1,0:T(8,128)(2,1)S(1)} %bitcast.186, f32[1024,768]{1,0:T(8,128)S(1)} %get-tuple-element.125), kind=kOutput, calls=%fused_computation.9 | convolution fusion | flops 4873516032 | bytes 26763264 | tf_op jit(solution)/shard_map/dot_general | solution.py:48
  262.3 6.5 %multiply_reduce_fusion = (f32[768]{0:T(1024)}, f32[1024]{0:T(1024)S(1)}, f32[1024]{0:T(1024)S(1)}, f32[768]{0:T(1024)}, f32[1024,768]{1,0:T(8,128)S(1)}) fusion(f32[1024,768]{1,0:T(8,128)S(1)} %copy-done.10, f32[1024]{0:T(1024)S(1)} %add_rsqrt_fusion.1, f32[1024]{0:T(1024)S(1)} %broadcast_multiply_fusion.5, f32[768]{0:T(1024)S(1)} %mul.132, ...), kind=kOutput, calls=%fused_computation.28 | convolution fusion | flops 4839698432 | bytes 20472832 | tf_op jit(solution)/shard_map/dot_general | solution.py:48
  268.8 7.9 %convolution_convert_fusion.2 = bf16[768,3072]{1,0:T(8,128)(2,1)} fusion(bf16[1024,3072]{1,0:T(8,128)(2,1)S(1)} %get-tuple-element.149, f32[1024,768]{1,0:T(8,128)S(1)} %copy-done.10, f32[768]{0:T(1024)S(1)} %add.151, f32[768]{0:T(1024)S(1)} %mul.132, f32[1024]{0:T(1024)S(1)} %add_rsqrt_fusion.1, f32[1024]{0:T(1024)S(1)} %broadcast_multiply_fusion.5), kind=kOutput, calls=%fused_computation.15 | convolution fusion | flops 4838129664 | bytes 14170112 | tf_op jit(solution)/shard_map/dot_general | solution.py:48
  276.8 1.7 convert_reduce_fusion.3
  278.7 2.5 convolution_convert_fusion.7
  281.2 2.6 convolution_convert_fusion.3.grad_ref
  283.8 145.6 %attend_backward.1 = (bf16[1024,768]{1,0:T(8,128)(2,1)}, bf16[1024,768]{1,0:T(8,128)(2,1)}, bf16[1024,768]{1,0:T(8,128)(2,1)}, bf16[4,96,768]{2,1,0:T(8,128)(2,1...) custom-call(s32[1]{0:T(128)S(6)} %select_n.40.limit_ref, bf16[1024,768]{1,0:T(8,128)(2,1)} %add_convert_fusion.3.query_ref, ...), custom_call_target="tpu_custom_call" | custom-call | flops 128849018880 | bytes 40000000 | tf_op jit(solution)/shard_map/attend_backward/pallas_call | solution.py:1236
  429.4 3.0 fusion.30
  432.5 1.4 fusion.31
  435.1 2.7 add_convert_fusion.1
  437.8 6.9 %all-to-all-start = ((bf16[8,128,768]{2,1,0:T(8,128)(2,1)}), bf16[8,128,768]{2,1,0:T(8,128)(2,1)S(1)}, u32[]{:S(2)}, u32[]{:S(2)}) async-start(bf16[8,128,768]{2,1,0:T(8,128)(2,1)} %bitcast.138), calls=%async_computation | async-start | bytes 3145728 | tf_op jit(solution)/shard_map/all_to_all | solution.py:1402
  444.8 1.8 convert_reduce_fusion.5
  446.6 1.7 convert_reduce_fusion.4
  448.6 2.5 convolution_convert_fusion.4
  451.1 2.5 convolution_convert_fusion.5
  453.8 1.3 concatenate.7.refs_3_
  455.1 3.9 convolution_convert_fusion.6
  458.9 54.2 %sum_gradients.1 = (bf16[4,48,384]{2,1,0:T(8,128)(2,1)}, bf16[4,48,384]{2,1,0:T(8,128)(2,1)}, bf16[4,48,384]{2,1,0:T(8,128)(2,1)}, f32[16,768]{1,0:T(8,128)}) custom-call(bf16[8,2,48,768]{3,2,1,0:T(8,128)(2,1)} %bitcast.154, bf16[8,2,48,768]{3,2,1,0:T(8,128)(2,1)} %bitcast.153, bf16[8,2,48,768]{3,2,1,0:T(8,128)(2,1)} %bitcast.152, f32[16,768]{1,0:T(8,128)} %concatenate.7.refs_3_), custom_call_target="tpu_custom_call" | custom-call | tf_op jit(solution)/shard_map/sum_gradients/pallas_call | solution.py:850
  513.2 0.8 slice.86
  514.0 0.7 slice.92
  514.7 0.9 convert_bitcast_fusion.4
  516.5 0.9 convert_bitcast_fusion.3
  519.3 1.2 convert_bitcast_fusion.1
  520.5 1.1 copy.54
  524.3 2.2 bitcast_convert_fusion
  526.4 1.8 gather_fusion.1
  528.2 3.4 copy.52
  (170 shorter events, 11.1 us)
Async XLA Ops:
  0.7 2.7 copy-start
  85.1 2.2 copy-start.2
  87.3 2.7 copy-start.3
  90.2 4.4 copy-start.45
  94.4 13.8 %copy-start.15 = (bf16[1,8,96,768]{3,2,1,0:T(8,128)(2,1)}, bf16[1,8,96,768]{3,2,1,0:T(8,128)(2,1)S(1)}, u32[]{:S(2)}) copy-start(bf16[1,8,96,768]{3,2,1,0:T(8,128)(2,1)S(1)} %get-tuple-element.129) | copy-start | bytes 3538948
  96.0 1.7 copy-start.20
  96.0 12.3 %slice-start = ((s8[6291456]{0:T(1024)(128)(4,1)}), s8[4194304]{0:T(1024)(128)(4,1)S(1)}, s32[]{:S(2)}) async-start(s8[6291456]{0:T(1024)(128)(4,1)} %bitcast.133), calls=%async_computation.1 | async-start | bytes 8388608
  97.7 107.3 %copy-start.18 = (bf16[1,8,128,768]{3,2,1,0:T(8,128)(2,1)}, bf16[1,8,128,768]{3,2,1,0:T(8,128)(2,1)S(1)}, u32[]{:S(2)}) copy-start(bf16[1,8,128,768]{3,2,1,0:T(8,128)(2,1)S(1)} %constant_dynamic-slice_fusion.1) | copy-start | bytes 4718596
  97.7 10.6 %slice-start.1 = ((s8[6291456]{0:T(1024)(128)(4,1)}), s8[2097152]{0:T(1024)(128)(4,1)S(1)}, s32[]{:S(2)}) async-start(s8[6291456]{0:T(1024)(128)(4,1)} %bitcast.133), calls=%async_computation.2 | async-start | bytes 4194304
  108.3 7.1 %copy-start.22 = (bf16[1,8,96,768]{3,2,1,0:T(8,128)(2,1)S(1)}, bf16[1,8,96,768]{3,2,1,0:T(8,128)(2,1)}, u32[]{:S(2)}) copy-start(bf16[1,8,96,768]{3,2,1,0:T(8,128)(2,1)} %get-tuple-element.131) | copy-start | bytes 3538948
  117.9 87.0 %copy-start.24 = (bf16[1,8,96,768]{3,2,1,0:T(8,128)(2,1)S(1)}, bf16[1,8,96,768]{3,2,1,0:T(8,128)(2,1)}, u32[]{:S(2)}) copy-start(bf16[1,8,96,768]{3,2,1,0:T(8,128)(2,1)} %get-tuple-element.128) | copy-start | bytes 3538948
  208.3 1.7 copy-start.8
  210.9 12.1 %copy-start.9 = (f32[1024,768]{1,0:T(8,128)S(1)}, f32[1024,768]{1,0:T(8,128)}, u32[]{:S(2)}) copy-start(f32[1024,768]{1,0:T(8,128)} %copy-done.8) | copy-start | bytes 9437188
  223.0 10.1 %copy-start.50 = (bf16[1024,3072]{1,0:T(8,128)(2,1)}, bf16[1024,3072]{1,0:T(8,128)(2,1)S(1)}, u32[]{:S(2)}) copy-start(bf16[1024,3072]{1,0:T(8,128)(2,1)S(1)} %get-tuple-element.143) | copy-start | bytes 18874372
  233.0 1.6 copy-start.4
  233.0 2.5 copy-start.6
  235.6 4.1 copy-start.5
  235.6 7.0 %copy-start.51 = (bf16[1024,3072]{1,0:T(8,128)(2,1)S(1)}, bf16[1024,3072]{1,0:T(8,128)(2,1)}, u32[]{:S(2)}) copy-start(bf16[1024,3072]{1,0:T(8,128)(2,1)} %copy-done.50) | copy-start | bytes 18874372
  239.7 10.0 %slice-start.4 = ((s8[4718592]{0:T(1024)(128)(4,1)}), s8[4194304]{0:T(1024)(128)(4,1)S(1)}, s32[]{:S(2)}) async-start(s8[4718592]{0:T(1024)(128)(4,1)} %bitcast.184), calls=%async_computation.5 | async-start | bytes 8388608
  242.6 7.1 %slice-start.5 = ((s8[4718592]{0:T(1024)(128)(4,1)}), s8[524288]{0:T(1024)(128)(4,1)S(1)}, s32[]{:S(2)}) async-start(s8[4718592]{0:T(1024)(128)(4,1)} %bitcast.184), calls=%async_computation.6 | async-start | bytes 1048576
  242.6 19.7 %slice-start.2 = ((s8[4718592]{0:T(1024)(128)(4,1)}), s8[4194304]{0:T(1024)(128)(4,1)S(1)}, s32[]{:S(2)}) async-start(s8[4718592]{0:T(1024)(128)(4,1)} %bitcast.180), calls=%async_computation.3 | async-start | bytes 8388608
  249.7 12.6 %copy-start.10 = (f32[1024,768]{1,0:T(8,128)S(1)}, f32[1024,768]{1,0:T(8,128)}, u32[]{:S(2)}) copy-start(f32[1024,768]{1,0:T(8,128)} %copy-done.8) | copy-start | bytes 9437188
  249.7 12.6 %slice-start.3 = ((s8[4718592]{0:T(1024)(128)(4,1)}), s8[524288]{0:T(1024)(128)(4,1)S(1)}, s32[]{:S(2)}) async-start(s8[4718592]{0:T(1024)(128)(4,1)} %bitcast.180), calls=%async_computation.4 | async-start | bytes 1048576
  276.8 1.9 copy-start.47
  278.5 2.7 copy-start.11
  278.7 2.5 copy-start.25
  283.8 145.6 %copy-start.23 = (bf16[1,8,96,768]{3,2,1,0:T(8,128)(2,1)S(1)}, bf16[1,8,96,768]{3,2,1,0:T(8,128)(2,1)}, u32[]{:S(2)}) copy-start(bf16[1,8,96,768]{3,2,1,0:T(8,128)(2,1)} %get-tuple-element.131) | copy-start | bytes 3538948
  429.4 3.0 copy-start.21
  429.4 3.0 copy-start.48
  432.4 1.9 copy-start.12
  432.5 2.3 copy-start.13
  432.5 2.7 copy-start.16
  437.8 10.5 %copy-start.7 = (bf16[1024,1,768]{2,0,1:T(8,128)(2,1)S(1)}, bf16[1024,1,768]{2,0,1:T(8,128)(2,1)}, u32[]{:S(2)}) copy-start(bf16[1024,1,768]{2,0,1:T(8,128)(2,1)} %param.37) | copy-start | bytes 4718596
  437.8 88.6 %all-to-all-start = ((bf16[8,128,768]{2,1,0:T(8,128)(2,1)}), bf16[8,128,768]{2,1,0:T(8,128)(2,1)S(1)}, u32[]{:S(2)}, u32[]{:S(2)}) async-start(bf16[8,128,768]{2,1,0:T(8,128)(2,1)} %bitcast.138), calls=%async_computation | async-start | bytes 3145728 | tf_op jit(solution)/shard_map/all_to_all | solution.py:1402
  444.8 3.8 copy-start.14
  444.8 3.8 copy-start.19
  448.6 2.5 copy-start.49
  451.1 2.5 copy-start.32
  451.1 2.6 copy-start.35
  451.1 2.6 copy-start.34
  451.1 2.6 copy-start.33
  451.1 2.6 copy-start.30
  451.1 2.6 copy-start.31
  451.1 3.9 copy-start.17
  513.2 5.2 copy-start.29
  517.6 4.0 copy-start.28
  518.4 4.6 copy-start.46
  526.4 5.2 copy-start.1
  (11 other events, 8.5 us)

commit v7 on v6

--- a/solution.py
+++ b/solution.py
@@ -129,8 +129,8 @@
 class Gather:
     SCRATCH = 11
 
-    def __init__(self, kinds, sems, count):
-        self.kinds, self.count = kinds, count
+    def __init__(self, kinds, sems, count, over_x=True):
+        self.kinds, self.count, self.over_x = kinds, count, over_x
         self.right_send, self.left_send, self.line_recv = sems[:3]
         self.y_send, self.y_recv, self.x_send, self.x_recv = sems[3:7]
         self.s_send, self.s_recv, self.r_send, self.r_recv = sems[7:11]
@@ -168,6 +168,11 @@
     def relay(self, kind, block):
         return self.copy(kind, block, self.across, self.r_send, self.r_recv, {"ctx": self.sibling})
 
+    def hand_over(self, kind, block):
+        if self.over_x:
+            self.cross(kind, block).start()
+        self.share(kind, block).start()
+
     def at(self, line, side):
         return 2 * line + side
 
@@ -203,8 +208,7 @@
                 self.right(kind, block).wait_recv()
                 self.after(1, lambda _: self.right(kind, block).start())
                 self.pair(kind, block).start()
-                self.cross(kind, block).start()
-                self.share(kind, block).start()
+                self.hand_over(kind, block)
 
             self.every(body)
 
@@ -215,8 +219,7 @@
                 self.left(kind, block).wait_recv()
                 self.before(1, lambda _: self.left(kind, block).start())
                 self.pair(kind, block).start()
-                self.cross(kind, block).start()
-                self.share(kind, block).start()
+                self.hand_over(kind, block)
 
             self.every(body)
 
@@ -234,8 +237,7 @@
         def one(block):
             def body(kind):
                 self.pair(kind, block).wait_recv()
-                self.cross(kind, block).start()
-                self.share(kind, block).start()
+                self.hand_over(kind, block)
 
             self.every(body)
 
@@ -254,9 +256,10 @@
     def finish(self):
         def passed(block):
             def body(kind):
-                self.cross(kind, block).wait_send()
                 self.share(kind, block).wait()
-                self.relay(kind, block).wait()
+                if self.over_x:
+                    self.cross(kind, block).wait_send()
+                    self.relay(kind, block).wait()
 
             self.every(body)
 
@@ -322,7 +325,9 @@
     count,
 ):
     ctx, group, across, sibling = places()
-    gather = Gather(((lambda q: weights.at[q], lambda b, q: gathered.at[q, b]),), sems, count)
+    half = pl.ds(2 * lax.rem(ctx, 2), 2)
+    kind = (lambda q: weights.at[half], lambda b, q: gathered.at[half, b])
+    gather = Gather((kind,), sems, count, over_x=False)
     own_tok = pltpu.make_async_copy(placed.at[group], tok_stage, local_sem.at[0])
     own_w = pltpu.make_async_copy(weights, w_stage, local_sem.at[1])
     own_small = pltpu.make_async_copy(small, small_stage, local_sem.at[2])
@@ -402,14 +407,6 @@
     lax.fori_loop(2, length, advance, 0)
     gather.beside(length - 1)
     lax.fori_loop(2 * length - 1, count, arrive, 0)
-
-    def crossed(distance, carry):
-        gather.crossed(distance, 0)
-        gather.crossed(distance, 1)
-        return carry
-
-    gather.crossed(0, 1)
-    lax.fori_loop(1, length, crossed, 0)
 
     def passed(step, carry):
         origin = lax.rem(group - step + count, count)
@@ -877,9 +874,9 @@
             slots[first].append((name, 0, 1))
 
     put("along", 2, 4, 0)
-    put("beside", 5, 3, 2)
-    put("line", 6, 4, 0)
-    put("pair", 8, 4, 6)
+    put("beside", 5, 4, 2)
+    put("line", 7, 4, 0)
+    put("pair", 9, 3, 7)
     return slots
 
 

time: 540 us -> 532 us (0.985)
  Pallas kernels: 361 us -> 354 us
    pallas_call x1, Pallas kernels: 87 us -> 81.1 us  [attend_forward(): pl.pallas_call(functools.partial(forward_kernel, key_rows=full // 2, coun...]
where the time goes in v7:
time: 532 us; the launch traced here: 524 us
  Pallas kernels  354 us (67%)
  matrix products  101 us (19%)
  local copies, waits for them, and re-layouts  38.7 us (7%)
  other arithmetic  21.1 us (4%)
  starting transfers between devices  6.15 us (1%)
    pallas_call x1, Pallas kernels, attend_backward(): pl.pallas_call(functools.partial(backward_kernel, count=count), grid_spec...  145 us
    dot_general x18, matrix products, product(): lax.dot_general(left, right, (dims, ((), ())), preferred_element_type=jnp...  101 us
    pallas_call x1, Pallas kernels, attend_forward(): pl.pallas_call(functools.partial(forward_kernel, key_rows=full // 2, coun...  81.1 us
    pallas_call x1, Pallas kernels, bring_in(): pl.pallas_call(functools.partial(arrival_kernel, count=count), in_specs=[...  74.2 us
    pallas_call x1, Pallas kernels, sum_gradients(): pl.pallas_call(functools.partial(sums_kernel, parts=len(parts), count=cou...  54.1 us
    unnamed x120, local copies, waits for them, and re-layouts  16.2 us
  transfers between devices with their start and end apart: 1, of which 0 were waited for; matrix products, arithmetic and copies ran while one was open for 5% of the time, Pallas kernels for 10%

profile of v7, /device:TPU:29, one launch (start us, length us, event | category | flops | bytes accessed | tf_op | source)
XLA Modules:
  0.0 523.8 jit_solution(18353042451575315237)
XLA Ops:
  0.7 1.4 dynamic-slice.4
  3.4 5.0 gather_fusion
  9.5 1.1 pad_maximum_fusion.weights
  10.6 74.2 %bring_in.1 = (bf16[4,8,128,768]{3,2,1,0:T(8,128)(2,1)S(1)}, bf16[4,8,96,768]{3,2,1,0:T(8,128)(2,1)S(1)}, bf16[8,16,128]{2,1,0:T(8,128)(2,1)S(1)}) custom-call(bf16[8,128,768]{2,1,0:T(8,128)(2,1)S(1)} %copy.46.placed, bf16[4,96,768]{2,1,0:T(8,128)(2,1)S(1)} %pad_maximum_fusion.weights, bf16[16,128]{1,0:T(8,128)(2,1)S(1)} %pad.4.small), custom_call_target="tpu_custom_call" | custom-call | tf_op jit(solution)/shard_map/bring_in/pallas_call | solution.py:440
  84.8 2.2 copy-done.2
  87.0 2.7 copy-done.3
  89.8 4.2 fusion.27
  94.2 0.7 dynamic-slice.5
  95.6 1.7 constant_dynamic-slice_fusion.1
  97.3 10.5 %convolution_convert_fusion.key_ref = bf16[4096,768]{1,0:T(8,128)(2,1)} fusion(bf16[4096,768]{1,0:T(8,128)(2,1)} %bitcast.132, bf16[768,768]{1,0:T(8,128)(2,1)S(1)} %bitcast.146), kind=kOutput, calls=%fused_computation.13 | convolution fusion | flops 4834983936 | bytes 13762560 | tf_op jit(solution)/shard_map/dot_general | solution.py:48
  107.9 7.1 %add_convert_fusion.value_ref = bf16[4096,768]{1,0:T(8,128)(2,1)} fusion(f32[768]{0:T(1024)S(1)} %add.143, bf16[4096,768]{1,0:T(8,128)(2,1)S(1)} %bitcast.135, bf16[768,768]{1,0:T(8,128)(2,1)S(1)} %bitcast.139), kind=kOutput, calls=%fused_computation.12 | convolution fusion | flops 4838129664 | bytes 13765632 | tf_op jit(solution)/shard_map/dot_general | solution.py:48
  115.0 2.5 add_convert_fusion.3.query_ref
  117.5 81.1 %attend_forward.1 = (f32[1024,768]{1,0:T(8,128)}, f32[6,2,1024]{2,1,0:T(2,128)}, bf16[8,96,3072]{2,1,0:T(8,128)(2,1)}, bf16[8,4,96,768]{3,2,1,0:T(8,128)(2,1)}) custom-call(s32[1]{0:T(128)S(6)} %select_n.40.limit_ref, bf16[1024,768]{1,0:T(8,128)(2,1)} %add_convert_fusion.3.query_ref, bf16[4096,768]{1,0:T(8,128)(2,1)} %convolution_convert_fusion.key_ref, ...), custom_call_target="tpu_custom_call" | custom-call | flops 51539607552 | bytes 20000000 | tf_op jit(solution)/shard_map/attend_forward/pallas_call | solution.py:1014
  198.7 3.4 fusion.28
  202.1 1.7 copy-done.8
  204.6 12.0 %multiply_convert_fusion = (bf16[1024,3072]{1,0:T(8,128)(2,1)S(1)}, f32[1024,3072]{1,0:T(8,128)}) fusion(f32[3072]{0:T(1024)S(1)} %add.154, bf16[768,3072]{1,0:T(8,128)(2,1)} %bitcast.179, f32[1024,768]{1,0:T(8,128)} %copy-done.8, f32[768]{0:T(1024)S(1)} %add.151, f32[768]{0:T(1024)S(1)} %mul.132, f32[1024]{0:T(1024)S(1)} %add_rsqrt_fusion.1, ...), kind=kOutput, calls=%fused_computation.10 | convolution fusion | flops 4854644736 | bytes 26765312 | tf_op jit(solution)/shard_map/dot_general | solution.py:48
  216.7 10.0 %fusion.29 = (f32[1024]{0:T(1024)S(1)}, f32[1024,768]{1,0:T(8,128)S(1)}) fusion(f32[768]{0:T(1024)S(1)} %add.158, bf16[1024,3072]{1,0:T(8,128)(2,1)S(1)} %get-tuple-element.143, bf16[3072,768]{1,0:T(8,128)(2,1)} %bitcast.183, f32[768]{0:T(1024)S(1)} %add.151, f32[768]{0:T(1024)S(1)} %mul.132, f32[1024]{0:T(1024)S(1)} %add_rsqrt_fusion.1, ...), kind=kOutput, calls=%fused_computation.102 | convolution fusion | flops 4837342208 | bytes 17323008 | tf_op jit(solution)/shard_map/dot_general | solution.py:48
  226.8 1.6 copy-done.4
  229.3 4.1 fusion.14
  233.4 2.9 convert_reduce_fusion.2
  236.3 7.1 %convolution_convert_fusion.1 = bf16[3072,768]{1,0:T(8,128)(2,1)} fusion(bf16[1024,3072]{1,0:T(8,128)(2,1)S(1)} %copy-done.51, f32[1024,768]{1,0:T(8,128)S(1)} %get-tuple-element.125), kind=kOutput, calls=%fused_computation.14 | convolution fusion | flops 4834983936 | bytes 14155776 | tf_op jit(solution)/shard_map/dot_general | solution.py:48
  243.4 12.6 %convert_reduce_fusion = (f32[3072]{0:T(1024)}, bf16[1024,3072]{1,0:T(8,128)(2,1)S(1)}) fusion(f32[1024,3072]{1,0:T(8,128)} %get-tuple-element.144, f32[3072]{0:T(1024)S(1)} %add.154, bf16[3072,768]{1,0:T(8,128)(2,1)S(1)} %bitcast.186, f32[1024,768]{1,0:T(8,128)S(1)} %get-tuple-element.125), kind=kOutput, calls=%fused_computation.9 | convolution fusion | flops 4873516032 | bytes 26763264 | tf_op jit(solution)/shard_map/dot_general | solution.py:48
  256.0 6.5 %multiply_reduce_fusion = (f32[768]{0:T(1024)}, f32[1024]{0:T(1024)S(1)}, f32[1024]{0:T(1024)S(1)}, f32[768]{0:T(1024)}, f32[1024,768]{1,0:T(8,128)S(1)}) fusion(f32[1024,768]{1,0:T(8,128)S(1)} %copy-done.10, f32[1024]{0:T(1024)S(1)} %add_rsqrt_fusion.1, f32[1024]{0:T(1024)S(1)} %broadcast_multiply_fusion.5, f32[768]{0:T(1024)S(1)} %mul.132, ...), kind=kOutput, calls=%fused_computation.28 | convolution fusion | flops 4839698432 | bytes 20472832 | tf_op jit(solution)/shard_map/dot_general | solution.py:48
  262.5 7.9 %convolution_convert_fusion.2 = bf16[768,3072]{1,0:T(8,128)(2,1)} fusion(bf16[1024,3072]{1,0:T(8,128)(2,1)S(1)} %get-tuple-element.149, f32[1024,768]{1,0:T(8,128)S(1)} %copy-done.10, f32[768]{0:T(1024)S(1)} %add.151, f32[768]{0:T(1024)S(1)} %mul.132, f32[1024]{0:T(1024)S(1)} %add_rsqrt_fusion.1, f32[1024]{0:T(1024)S(1)} %broadcast_multiply_fusion.5), kind=kOutput, calls=%fused_computation.15 | convolution fusion | flops 4838129664 | bytes 14170112 | tf_op jit(solution)/shard_map/dot_general | solution.py:48
  270.5 1.7 convert_reduce_fusion.3
  272.4 2.5 convolution_convert_fusion.7
  274.9 2.6 convolution_convert_fusion.3.grad_ref
  277.5 144.8 %attend_backward.1 = (bf16[1024,768]{1,0:T(8,128)(2,1)}, bf16[1024,768]{1,0:T(8,128)(2,1)}, bf16[1024,768]{1,0:T(8,128)(2,1)}, bf16[4,96,768]{2,1,0:T(8,128)(2,1...) custom-call(s32[1]{0:T(128)S(6)} %select_n.40.limit_ref, bf16[1024,768]{1,0:T(8,128)(2,1)} %add_convert_fusion.3.query_ref, ...), custom_call_target="tpu_custom_call" | custom-call | flops 128849018880 | bytes 40000000 | tf_op jit(solution)/shard_map/attend_backward/pallas_call | solution.py:1233
  422.3 3.0 fusion.30
  425.4 1.4 fusion.31
  428.0 2.7 add_convert_fusion.1
  430.7 6.2 %all-to-all-start = ((bf16[8,128,768]{2,1,0:T(8,128)(2,1)}), bf16[8,128,768]{2,1,0:T(8,128)(2,1)S(1)}, u32[]{:S(2)}, u32[]{:S(2)}) async-start(bf16[8,128,768]{2,1,0:T(8,128)(2,1)} %bitcast.138), calls=%async_computation | async-start | bytes 3145728 | tf_op jit(solution)/shard_map/all_to_all | solution.py:1399
  436.9 1.8 convert_reduce_fusion.5
  438.7 1.7 convert_reduce_fusion.4
  440.7 2.5 convolution_convert_fusion.4
  443.3 2.5 convolution_convert_fusion.5
  445.9 1.3 concatenate.7.refs_3_
  447.2 3.9 convolution_convert_fusion.6
  451.0 54.1 %sum_gradients.1 = (bf16[4,48,384]{2,1,0:T(8,128)(2,1)}, bf16[4,48,384]{2,1,0:T(8,128)(2,1)}, bf16[4,48,384]{2,1,0:T(8,128)(2,1)}, f32[16,768]{1,0:T(8,128)}) custom-call(bf16[8,2,48,768]{3,2,1,0:T(8,128)(2,1)} %bitcast.154, bf16[8,2,48,768]{3,2,1,0:T(8,128)(2,1)} %bitcast.153, bf16[8,2,48,768]{3,2,1,0:T(8,128)(2,1)} %bitcast.152, f32[16,768]{1,0:T(8,128)} %concatenate.7.refs_3_), custom_call_target="tpu_custom_call" | custom-call | tf_op jit(solution)/shard_map/sum_gradients/pallas_call | solution.py:847
  505.1 0.8 slice.86
  505.9 0.7 slice.92
  506.6 0.9 convert_bitcast_fusion.4
  508.5 0.9 convert_bitcast_fusion.3
  511.2 1.2 convert_bitcast_fusion.1
  512.4 1.1 copy.54
  516.2 2.2 bitcast_convert_fusion
  518.4 1.8 gather_fusion.1
  520.2 3.4 copy.52
  (170 shorter events, 11.1 us)
Async XLA Ops:
  0.7 2.7 copy-start
  84.8 2.2 copy-start.2
  87.0 2.7 copy-start.3
  89.8 4.4 copy-start.45
  94.0 13.8 %copy-start.15 = (bf16[1,8,96,768]{3,2,1,0:T(8,128)(2,1)}, bf16[1,8,96,768]{3,2,1,0:T(8,128)(2,1)S(1)}, u32[]{:S(2)}) copy-start(bf16[1,8,96,768]{3,2,1,0:T(8,128)(2,1)S(1)} %get-tuple-element.129) | copy-start | bytes 3538948
  95.6 1.7 copy-start.20
  95.6 12.3 %slice-start = ((s8[6291456]{0:T(1024)(128)(4,1)}), s8[4194304]{0:T(1024)(128)(4,1)S(1)}, s32[]{:S(2)}) async-start(s8[6291456]{0:T(1024)(128)(4,1)} %bitcast.133), calls=%async_computation.1 | async-start | bytes 8388608
  97.3 101.4 %copy-start.18 = (bf16[1,8,128,768]{3,2,1,0:T(8,128)(2,1)}, bf16[1,8,128,768]{3,2,1,0:T(8,128)(2,1)S(1)}, u32[]{:S(2)}) copy-start(bf16[1,8,128,768]{3,2,1,0:T(8,128)(2,1)S(1)} %constant_dynamic-slice_fusion.1) | copy-start | bytes 4718596
  97.3 10.6 %slice-start.1 = ((s8[6291456]{0:T(1024)(128)(4,1)}), s8[2097152]{0:T(1024)(128)(4,1)S(1)}, s32[]{:S(2)}) async-start(s8[6291456]{0:T(1024)(128)(4,1)} %bitcast.133), calls=%async_computation.2 | async-start | bytes 4194304
  107.9 7.1 %copy-start.22 = (bf16[1,8,96,768]{3,2,1,0:T(8,128)(2,1)S(1)}, bf16[1,8,96,768]{3,2,1,0:T(8,128)(2,1)}, u32[]{:S(2)}) copy-start(bf16[1,8,96,768]{3,2,1,0:T(8,128)(2,1)} %get-tuple-element.131) | copy-start | bytes 3538948
  117.5 81.1 %copy-start.24 = (bf16[1,8,96,768]{3,2,1,0:T(8,128)(2,1)S(1)}, bf16[1,8,96,768]{3,2,1,0:T(8,128)(2,1)}, u32[]{:S(2)}) copy-start(bf16[1,8,96,768]{3,2,1,0:T(8,128)(2,1)} %get-tuple-element.128) | copy-start | bytes 3538948
  202.1 1.7 copy-start.8
  204.6 12.1 %copy-start.9 = (f32[1024,768]{1,0:T(8,128)S(1)}, f32[1024,768]{1,0:T(8,128)}, u32[]{:S(2)}) copy-start(f32[1024,768]{1,0:T(8,128)} %copy-done.8) | copy-start | bytes 9437188
  216.7 10.1 %copy-start.50 = (bf16[1024,3072]{1,0:T(8,128)(2,1)}, bf16[1024,3072]{1,0:T(8,128)(2,1)S(1)}, u32[]{:S(2)}) copy-start(bf16[1024,3072]{1,0:T(8,128)(2,1)S(1)} %get-tuple-element.143) | copy-start | bytes 18874372
  226.8 1.6 copy-start.4
  226.8 2.5 copy-start.6
  229.3 4.1 copy-start.5
  229.3 7.0 %copy-start.51 = (bf16[1024,3072]{1,0:T(8,128)(2,1)S(1)}, bf16[1024,3072]{1,0:T(8,128)(2,1)}, u32[]{:S(2)}) copy-start(bf16[1024,3072]{1,0:T(8,128)(2,1)} %copy-done.50) | copy-start | bytes 18874372
  233.4 10.0 %slice-start.4 = ((s8[4718592]{0:T(1024)(128)(4,1)}), s8[4194304]{0:T(1024)(128)(4,1)S(1)}, s32[]{:S(2)}) async-start(s8[4718592]{0:T(1024)(128)(4,1)} %bitcast.184), calls=%async_computation.5 | async-start | bytes 8388608
  236.3 7.1 %slice-start.5 = ((s8[4718592]{0:T(1024)(128)(4,1)}), s8[524288]{0:T(1024)(128)(4,1)S(1)}, s32[]{:S(2)}) async-start(s8[4718592]{0:T(1024)(128)(4,1)} %bitcast.184), calls=%async_computation.6 | async-start | bytes 1048576
  236.3 19.7 %slice-start.2 = ((s8[4718592]{0:T(1024)(128)(4,1)}), s8[4194304]{0:T(1024)(128)(4,1)S(1)}, s32[]{:S(2)}) async-start(s8[4718592]{0:T(1024)(128)(4,1)} %bitcast.180), calls=%async_computation.3 | async-start | bytes 8388608
  243.4 12.6 %copy-start.10 = (f32[1024,768]{1,0:T(8,128)S(1)}, f32[1024,768]{1,0:T(8,128)}, u32[]{:S(2)}) copy-start(f32[1024,768]{1,0:T(8,128)} %copy-done.8) | copy-start | bytes 9437188
  243.4 12.6 %slice-start.3 = ((s8[4718592]{0:T(1024)(128)(4,1)}), s8[524288]{0:T(1024)(128)(4,1)S(1)}, s32[]{:S(2)}) async-start(s8[4718592]{0:T(1024)(128)(4,1)} %bitcast.180), calls=%async_computation.4 | async-start | bytes 1048576
  270.5 1.9 copy-start.47
  272.2 2.7 copy-start.11
  272.4 2.5 copy-start.25
  277.5 144.8 %copy-start.23 = (bf16[1,8,96,768]{3,2,1,0:T(8,128)(2,1)S(1)}, bf16[1,8,96,768]{3,2,1,0:T(8,128)(2,1)}, u32[]{:S(2)}) copy-start(bf16[1,8,96,768]{3,2,1,0:T(8,128)(2,1)} %get-tuple-element.131) | copy-start | bytes 3538948
  422.3 3.0 copy-start.21
  422.3 3.0 copy-start.48
  425.3 1.9 copy-start.12
  425.3 2.3 copy-start.13
  425.4 2.7 copy-start.16
  430.7 9.7 %copy-start.7 = (bf16[1024,1,768]{2,0,1:T(8,128)(2,1)S(1)}, bf16[1024,1,768]{2,0,1:T(8,128)(2,1)}, u32[]{:S(2)}) copy-start(bf16[1024,1,768]{2,0,1:T(8,128)(2,1)} %param.37) | copy-start | bytes 4718596
  430.7 87.6 %all-to-all-start = ((bf16[8,128,768]{2,1,0:T(8,128)(2,1)}), bf16[8,128,768]{2,1,0:T(8,128)(2,1)S(1)}, u32[]{:S(2)}, u32[]{:S(2)}) async-start(bf16[8,128,768]{2,1,0:T(8,128)(2,1)} %bitcast.138), calls=%async_computation | async-start | bytes 3145728 | tf_op jit(solution)/shard_map/all_to_all | solution.py:1399
  436.9 3.8 copy-start.14
  436.9 3.8 copy-start.19
  440.7 2.5 copy-start.49
  443.2 2.5 copy-start.32
  443.2 2.6 copy-start.35
  443.2 2.6 copy-start.34
  443.2 2.6 copy-start.33
  443.2 2.6 copy-start.30
  443.2 2.6 copy-start.31
  443.2 3.9 copy-start.17
  505.1 5.2 copy-start.29
  509.6 4.0 copy-start.28
  510.3 4.6 copy-start.46
  518.3 5.2 copy-start.1
  (11 other events, 8.5 us)

commit v8 on v7

--- a/solution.py
+++ b/solution.py
@@ -1301,7 +1301,7 @@
     group = lax.axis_index("fsdp")
     shard = query_bias.shape[0]
     low = jnp.bfloat16
-    placed = jnp.swapaxes(hidden_in.at[:, seq_order].get(mode="promise_in_bounds"), 0, 1)
+    placed = jnp.swapaxes(hidden_in, 0, 1).at[seq_order].get(mode="promise_in_bounds")
     vectors = jnp.concatenate(
         (
             jnp.stack(
@@ -1398,7 +1398,7 @@
     back_rows = d_placed.astype(low).reshape(count, local_len // count, width)
     returned = lax.all_to_all(back_rows, "fsdp", split_axis=0, concat_axis=0, tiled=True)
     inverse = jnp.argmax(seq_order[:, None] == jnp.arange(count), axis=0)
-    grad_in = jnp.swapaxes(returned, 0, 1).at[:, inverse].get(mode="promise_in_bounds")
+    grad_in = jnp.swapaxes(returned.at[inverse].get(mode="promise_in_bounds"), 0, 1)
     small_sums = jnp.concatenate(
         (
             jnp.stack(

time: 532 us -> 526 us (0.989)
  local copies, waits for them, and re-layouts: 38.7 us -> 32.7 us
    gather x3 -> x2, local copies, waits for them, and re-layouts: 7.11 us -> 1.3 us  [the longest x1 0.65 us: on_device(): jnp.swapaxes(hidden_in, 0, 1).at[seq_order].get(mode='promise_in_bounds')]
    unnamed x120 -> x121, local copies, waits for them, and re-layouts: 16.2 us -> 11.9 us
where the time goes in v8:
time: 526 us; the launch traced here: 517 us
  Pallas kernels  354 us (67%)
  matrix products  103 us (20%)
  local copies, waits for them, and re-layouts  32.7 us (6%)
  other arithmetic  18.5 us (4%)
  starting transfers between devices  6.13 us (1%)
    pallas_call x1, Pallas kernels, attend_backward(): pl.pallas_call(functools.partial(backward_kernel, count=count), grid_spec...  145 us
    dot_general x18, matrix products, product(): lax.dot_general(left, right, (dims, ((), ())), preferred_element_type=jnp...  103 us
    pallas_call x1, Pallas kernels, attend_forward(): pl.pallas_call(functools.partial(forward_kernel, key_rows=full // 2, coun...  80.9 us
    pallas_call x1, Pallas kernels, bring_in(): pl.pallas_call(functools.partial(arrival_kernel, count=count), in_specs=[...  74.2 us
    pallas_call x1, Pallas kernels, sum_gradients(): pl.pallas_call(functools.partial(sums_kernel, parts=len(parts), count=cou...  54.2 us
    unnamed x121, local copies, waits for them, and re-layouts  11.9 us
  transfers between devices with their start and end apart: 1, of which 0 were waited for; matrix products, arithmetic and copies ran while one was open for 5% of the time, Pallas kernels for 10%

profile of v8, /device:TPU:29, one launch (start us, length us, event | category | flops | bytes accessed | tf_op | source)
XLA Modules:
  0.0 517.1 jit_solution(12220689512002322214)
XLA Ops:
  0.7 1.2 dynamic-slice.4
  3.3 1.8 copy.59
  6.0 1.1 pad_maximum_fusion.weights
  7.1 74.2 %bring_in.1 = (bf16[4,8,128,768]{3,2,1,0:T(8,128)(2,1)S(1)}, bf16[4,8,96,768]{3,2,1,0:T(8,128)(2,1)S(1)}, bf16[8,16,128]{2,1,0:T(8,128)(2,1)S(1)}) custom-call(bf16[8,128,768]{2,1,0:T(8,128)(2,1)S(1)} %gather_fusion, bf16[4,96,768]{2,1,0:T(8,128)(2,1)S(1)} %pad_maximum_fusion.weights, bf16[16,128]{1,0:T(8,128)(2,1)S(1)} %pad.4.small), custom_call_target="tpu_custom_call" | custom-call | tf_op jit(solution)/shard_map/bring_in/pallas_call | solution.py:440
  81.3 2.2 copy-done
  83.5 2.7 copy-done.1
  87.5 3.8 fusion.27
  91.3 1.7 add.143
  93.0 1.4 add.146
  94.4 1.2 dynamic-slice.5
  96.3 1.7 constant_dynamic-slice_fusion.1
  98.0 10.3 %convolution_convert_fusion.key_ref = bf16[4096,768]{1,0:T(8,128)(2,1)} fusion(bf16[4096,768]{1,0:T(8,128)(2,1)} %bitcast.134, bf16[768,768]{1,0:T(8,128)(2,1)S(1)} %bitcast.148), kind=kOutput, calls=%fused_computation.13 | convolution fusion | flops 4834983936 | bytes 13762560 | tf_op jit(solution)/shard_map/dot_general | solution.py:48
  108.3 7.1 %add_convert_fusion.value_ref = bf16[4096,768]{1,0:T(8,128)(2,1)} fusion(f32[768]{0:T(1024)S(1)} %copy-done.36, bf16[4096,768]{1,0:T(8,128)(2,1)S(1)} %bitcast.137, bf16[768,768]{1,0:T(8,128)(2,1)S(1)} %bitcast.141), kind=kOutput, calls=%fused_computation.12 | convolution fusion | flops 4838129664 | bytes 13765632 | tf_op jit(solution)/shard_map/dot_general | solution.py:48
  115.4 2.5 add_convert_fusion.3.query_ref
  117.9 80.9 %attend_forward.1 = (f32[1024,768]{1,0:T(8,128)}, f32[6,2,1024]{2,1,0:T(2,128)}, bf16[8,96,3072]{2,1,0:T(8,128)(2,1)}, bf16[8,4,96,768]{3,2,1,0:T(8,128)(2,1)}) custom-call(s32[1]{0:T(128)S(6)} %select_n.40.limit_ref, bf16[1024,768]{1,0:T(8,128)(2,1)} %add_convert_fusion.3.query_ref, bf16[4096,768]{1,0:T(8,128)(2,1)} %convolution_convert_fusion.key_ref, ...), custom_call_target="tpu_custom_call" | custom-call | flops 51539607552 | bytes 20000000 | tf_op jit(solution)/shard_map/attend_forward/pallas_call | solution.py:1014
  198.9 4.2 fusion.28
  204.1 12.0 %multiply_convert_fusion = (bf16[1024,3072]{1,0:T(8,128)(2,1)S(1)}, f32[1024,3072]{1,0:T(8,128)}) fusion(f32[3072]{0:T(1024)S(1)} %add.154, bf16[768,3072]{1,0:T(8,128)(2,1)} %bitcast.181, f32[1024,768]{1,0:T(8,128)S(1)} %get-tuple-element.142, f32[768]{0:T(1024)S(1)} %add.151, f32[768]{0:T(1024)S(1)} %mul.132, f32[1024]{0:T(1024)S(1)} %add_rsqrt_fusion.1, ...), kind=kOutput, calls=%fused_computation.10 | convolution fusion | flops 4854644736 | bytes 26765312 | tf_op jit(solution)/shard_map/dot_general | solution.py:48
  216.1 11.0 %fusion.29 = (f32[1024]{0:T(1024)S(1)}, f32[1024,768]{1,0:T(8,128)S(1)}) fusion(f32[768]{0:T(1024)S(1)} %add.158, bf16[1024,3072]{1,0:T(8,128)(2,1)S(1)} %get-tuple-element.143, bf16[3072,768]{1,0:T(8,128)(2,1)} %bitcast.185, f32[768]{0:T(1024)S(1)} %add.151, f32[768]{0:T(1024)S(1)} %mul.132, f32[1024]{0:T(1024)S(1)} %add_rsqrt_fusion.1, ...), kind=kOutput, calls=%fused_computation.103 | convolution fusion | flops 4837342208 | bytes 17323008 | tf_op jit(solution)/shard_map/dot_general | solution.py:48
  227.9 3.6 fusion.14
  231.5 2.9 convert_reduce_fusion.2
  234.4 7.1 %convolution_convert_fusion.1 = bf16[3072,768]{1,0:T(8,128)(2,1)} fusion(bf16[1024,3072]{1,0:T(8,128)(2,1)S(1)} %copy-done.51, f32[1024,768]{1,0:T(8,128)S(1)} %get-tuple-element.125), kind=kOutput, calls=%fused_computation.14 | convolution fusion | flops 4834983936 | bytes 14155776 | tf_op jit(solution)/shard_map/dot_general | solution.py:48
  241.5 12.6 %convert_reduce_fusion = (f32[3072]{0:T(1024)}, bf16[1024,3072]{1,0:T(8,128)(2,1)S(1)}) fusion(f32[1024,3072]{1,0:T(8,128)} %get-tuple-element.144, f32[3072]{0:T(1024)S(1)} %add.154, bf16[3072,768]{1,0:T(8,128)(2,1)S(1)} %bitcast.188, f32[1024,768]{1,0:T(8,128)S(1)} %get-tuple-element.125), kind=kOutput, calls=%fused_computation.9 | convolution fusion | flops 4873516032 | bytes 26763264 | tf_op jit(solution)/shard_map/dot_general | solution.py:48
  254.1 6.5 %multiply_reduce_fusion = (f32[768]{0:T(1024)}, f32[1024]{0:T(1024)S(1)}, f32[1024]{0:T(1024)S(1)}, f32[768]{0:T(1024)}, f32[1024,768]{1,0:T(8,128)S(1)}) fusion(f32[1024,768]{1,0:T(8,128)S(1)} %copy-done.5, f32[1024]{0:T(1024)S(1)} %add_rsqrt_fusion.1, f32[1024]{0:T(1024)S(1)} %broadcast_multiply_fusion.5, f32[768]{0:T(1024)S(1)} %mul.132, ...), kind=kOutput, calls=%fused_computation.28 | convolution fusion | flops 4839698432 | bytes 20472832 | tf_op jit(solution)/shard_map/dot_general | solution.py:48
  260.7 7.9 %convolution_convert_fusion.2 = bf16[768,3072]{1,0:T(8,128)(2,1)} fusion(bf16[1024,3072]{1,0:T(8,128)(2,1)S(1)} %get-tuple-element.149, f32[1024,768]{1,0:T(8,128)S(1)} %copy-done.5, f32[768]{0:T(1024)S(1)} %add.151, f32[768]{0:T(1024)S(1)} %mul.132, f32[1024]{0:T(1024)S(1)} %add_rsqrt_fusion.1, f32[1024]{0:T(1024)S(1)} %broadcast_multiply_fusion.5), kind=kOutput, calls=%fused_computation.15 | convolution fusion | flops 4838129664 | bytes 14170112 | tf_op jit(solution)/shard_map/dot_general | solution.py:48
  268.6 1.7 convert_reduce_fusion.3
  270.5 2.5 convolution_convert_fusion.7
  273.0 2.6 convolution_convert_fusion.3.grad_ref
  275.6 144.8 %attend_backward.1 = (bf16[1024,768]{1,0:T(8,128)(2,1)}, bf16[1024,768]{1,0:T(8,128)(2,1)}, bf16[1024,768]{1,0:T(8,128)(2,1)}, bf16[4,96,768]{2,1,0:T(8,128)(2,1...) custom-call(s32[1]{0:T(128)S(6)} %select_n.40.limit_ref, bf16[1024,768]{1,0:T(8,128)(2,1)} %add_convert_fusion.3.query_ref, ...), custom_call_target="tpu_custom_call" | custom-call | flops 128849018880 | bytes 40000000 | tf_op jit(solution)/shard_map/attend_backward/pallas_call | solution.py:1233
  420.4 3.3 fusion.30
  423.7 1.4 fusion.31
  425.5 2.8 add_convert_fusion.1
  428.2 6.1 %all-to-all-start = ((bf16[8,128,768]{2,1,0:T(8,128)(2,1)}), bf16[8,128,768]{2,1,0:T(8,128)(2,1)S(1)}, u32[]{:S(2)}, u32[]{:S(2)}) async-start(bf16[8,128,768]{2,1,0:T(8,128)(2,1)} %bitcast.140), calls=%async_computation | async-start | bytes 3145728 | tf_op jit(solution)/shard_map/all_to_all | solution.py:1399
  434.4 1.8 convert_reduce_fusion.5
  436.2 1.7 convert_reduce_fusion.4
  438.2 2.5 convolution_convert_fusion.4
  440.8 2.5 convolution_convert_fusion.5
  443.4 1.3 concatenate.7.refs_3_
  444.7 3.9 convolution_convert_fusion.6
  448.5 54.2 %sum_gradients.1 = (bf16[4,48,384]{2,1,0:T(8,128)(2,1)}, bf16[4,48,384]{2,1,0:T(8,128)(2,1)}, bf16[4,48,384]{2,1,0:T(8,128)(2,1)}, f32[16,768]{1,0:T(8,128)}) custom-call(bf16[8,2,48,768]{3,2,1,0:T(8,128)(2,1)} %bitcast.156, bf16[8,2,48,768]{3,2,1,0:T(8,128)(2,1)} %bitcast.155, bf16[8,2,48,768]{3,2,1,0:T(8,128)(2,1)} %bitcast.154, f32[16,768]{1,0:T(8,128)} %concatenate.7.refs_3_), custom_call_target="tpu_custom_call" | custom-call | tf_op jit(solution)/shard_map/sum_gradients/pallas_call | solution.py:847
  502.8 0.8 slice.86
  503.6 0.7 slice.92
  504.3 0.9 convert_bitcast_fusion.4
  505.4 0.7 copy.55
  506.2 0.9 convert_bitcast_fusion.3
  507.3 0.7 copy.56
  509.1 1.1 copy.54
  512.8 1.1 bitcast_convert_fusion
  514.6 2.0 copy.52
  (170 shorter events, 10.2 us)
Async XLA Ops:
  0.7 4.5 copy-start.37
  3.2 2.7 copy-start.38
  3.2 2.7 copy-start.39
  3.2 2.7 copy-start.40
  3.2 2.7 copy-start.41
  3.2 2.7 copy-start.42
  3.3 2.7 copy-start.43
  3.3 2.7 copy-start.44
  3.3 2.7 copy-start.45
  3.3 2.7 copy-start.19
  3.3 2.7 copy-start.20
  83.5 2.7 copy-start.1
  91.3 17.0 %copy-start.13 = (bf16[1,8,96,768]{3,2,1,0:T(8,128)(2,1)}, bf16[1,8,96,768]{3,2,1,0:T(8,128)(2,1)S(1)}, u32[]{:S(2)}) copy-start(bf16[1,8,96,768]{3,2,1,0:T(8,128)(2,1)S(1)} %get-tuple-element.130) | copy-start | bytes 3538948
  91.3 17.0 %copy-start.8 = (bf16[1,8,96,768]{3,2,1,0:T(8,128)(2,1)}, bf16[1,8,96,768]{3,2,1,0:T(8,128)(2,1)S(1)}, u32[]{:S(2)}) copy-start(bf16[1,8,96,768]{3,2,1,0:T(8,128)(2,1)S(1)} %get-tuple-element.129) | copy-start | bytes 3538948
  91.3 24.1 %copy-start.15 = (bf16[1,8,96,768]{3,2,1,0:T(8,128)(2,1)}, bf16[1,8,96,768]{3,2,1,0:T(8,128)(2,1)S(1)}, u32[]{:S(2)}) copy-start(bf16[1,8,96,768]{3,2,1,0:T(8,128)(2,1)S(1)} %get-tuple-element.131) | copy-start | bytes 3538948
  96.3 12.0 %slice-start = ((s8[6291456]{0:T(1024)(128)(4,1)}), s8[4194304]{0:T(1024)(128)(4,1)S(1)}, s32[]{:S(2)}) async-start(s8[6291456]{0:T(1024)(128)(4,1)} %bitcast.135), calls=%async_computation.1 | async-start | bytes 8388608
  98.0 17.4 %copy-start.11 = (bf16[1,8,128,768]{3,2,1,0:T(8,128)(2,1)}, bf16[1,8,128,768]{3,2,1,0:T(8,128)(2,1)S(1)}, u32[]{:S(2)}) copy-start(bf16[1,8,128,768]{3,2,1,0:T(8,128)(2,1)S(1)} %constant_dynamic-slice_fusion.1) | copy-start | bytes 4718596
  98.0 10.3 %slice-start.1 = ((s8[6291456]{0:T(1024)(128)(4,1)}), s8[2097152]{0:T(1024)(128)(4,1)S(1)}, s32[]{:S(2)}) async-start(s8[6291456]{0:T(1024)(128)(4,1)} %bitcast.135), calls=%async_computation.2 | async-start | bytes 4194304
  98.0 10.3 %copy-start.36 = (f32[768]{0:T(1024)S(1)}, f32[768]{0:T(1024)}, u32[]{:S(2)}) copy-start(f32[768]{0:T(1024)} %add.143) | copy-start | bytes 9220
  108.3 7.1 %copy-start.34 = (f32[768]{0:T(1024)S(1)}, f32[768]{0:T(1024)}, u32[]{:S(2)}) copy-start(f32[768]{0:T(1024)} %add.140) | copy-start | bytes 9220
  117.9 80.9 %copy-start.35 = (f32[768]{0:T(1024)S(1)}, f32[768]{0:T(1024)}, u32[]{:S(2)}) copy-start(f32[768]{0:T(1024)} %add.146) | copy-start | bytes 9220
  203.1 13.0 %copy-start.4 = (f32[1024,768]{1,0:T(8,128)}, f32[1024,768]{1,0:T(8,128)S(1)}, u32[]{:S(2)}) copy-start(f32[1024,768]{1,0:T(8,128)S(1)} %get-tuple-element.142) | copy-start | bytes 9437188
  216.1 11.0 %copy-start.50 = (bf16[1024,3072]{1,0:T(8,128)(2,1)}, bf16[1024,3072]{1,0:T(8,128)(2,1)S(1)}, u32[]{:S(2)}) copy-start(bf16[1024,3072]{1,0:T(8,128)(2,1)S(1)} %get-tuple-element.143) | copy-start | bytes 18874372
  227.9 3.6 copy-start.2
  227.9 6.5 %copy-start.51 = (bf16[1024,3072]{1,0:T(8,128)(2,1)S(1)}, bf16[1024,3072]{1,0:T(8,128)(2,1)}, u32[]{:S(2)}) copy-start(bf16[1024,3072]{1,0:T(8,128)(2,1)} %copy-done.50) | copy-start | bytes 18874372
  231.5 10.0 %slice-start.4 = ((s8[4718592]{0:T(1024)(128)(4,1)}), s8[4194304]{0:T(1024)(128)(4,1)S(1)}, s32[]{:S(2)}) async-start(s8[4718592]{0:T(1024)(128)(4,1)} %bitcast.186), calls=%async_computation.5 | async-start | bytes 8388608
  234.4 7.1 %slice-start.5 = ((s8[4718592]{0:T(1024)(128)(4,1)}), s8[524288]{0:T(1024)(128)(4,1)S(1)}, s32[]{:S(2)}) async-start(s8[4718592]{0:T(1024)(128)(4,1)} %bitcast.186), calls=%async_computation.6 | async-start | bytes 1048576
  234.4 19.7 %slice-start.2 = ((s8[4718592]{0:T(1024)(128)(4,1)}), s8[4194304]{0:T(1024)(128)(4,1)S(1)}, s32[]{:S(2)}) async-start(s8[4718592]{0:T(1024)(128)(4,1)} %bitcast.182), calls=%async_computation.3 | async-start | bytes 8388608
  241.5 12.6 %copy-start.5 = (f32[1024,768]{1,0:T(8,128)S(1)}, f32[1024,768]{1,0:T(8,128)}, u32[]{:S(2)}) copy-start(f32[1024,768]{1,0:T(8,128)} %copy-done.4) | copy-start | bytes 9437188
  241.5 12.6 %slice-start.3 = ((s8[4718592]{0:T(1024)(128)(4,1)}), s8[524288]{0:T(1024)(128)(4,1)S(1)}, s32[]{:S(2)}) async-start(s8[4718592]{0:T(1024)(128)(4,1)} %bitcast.182), calls=%async_computation.4 | async-start | bytes 1048576
  420.4 3.3 copy-start.14
  420.4 3.3 copy-start.48
  428.2 9.7 %copy-start.3 = (bf16[1024,1,768]{2,0,1:T(8,128)(2,1)S(1)}, bf16[1024,1,768]{2,0,1:T(8,128)(2,1)}, u32[]{:S(2)}) copy-start(bf16[1024,1,768]{2,0,1:T(8,128)(2,1)} %param.37) | copy-start | bytes 4718596
  428.2 85.7 %all-to-all-start = ((bf16[8,128,768]{2,1,0:T(8,128)(2,1)}), bf16[8,128,768]{2,1,0:T(8,128)(2,1)S(1)}, u32[]{:S(2)}, u32[]{:S(2)}) async-start(bf16[8,128,768]{2,1,0:T(8,128)(2,1)} %bitcast.140), calls=%async_computation | async-start | bytes 3145728 | tf_op jit(solution)/shard_map/all_to_all | solution.py:1399
  434.4 3.8 copy-start.7
  434.4 3.8 copy-start.12
  440.7 2.5 copy-start.25
  440.7 2.6 copy-start.33
  440.7 2.6 copy-start.32
  440.7 2.6 copy-start.31
  440.7 2.6 copy-start.23
  440.7 2.6 copy-start.24
  440.8 3.9 copy-start.10
  502.8 5.2 %copy-start.22 = (bf16[4,48,384]{2,1,0:T(8,128)(2,1)S(1)}, bf16[4,48,384]{2,1,0:T(8,128)(2,1)}, u32[]{:S(2)}) copy-start(bf16[4,48,384]{2,1,0:T(8,128)(2,1)} %get-tuple-element.49) | copy-start | bytes 442372
  502.8 6.2 %copy-start.18 = (bf16[4,96,768]{2,1,0:T(8,128)(2,1)S(1)}, bf16[4,96,768]{2,1,0:T(8,128)(2,1)}, u32[]{:S(2)}) copy-start(bf16[4,96,768]{2,1,0:T(8,128)(2,1)} %get-tuple-element.51) | copy-start | bytes 1769476
  507.3 2.9 copy-start.21
  508.0 3.6 copy-start.46
  508.0 4.8 copy-start.17
  (11 other events, 16.2 us)
